TPU v7x, 128 devices: a whole 4x4x4 slice. The times are simulated.
128 devices in a mesh: tile: 64 (over x, z_hi, y, core), layer: 2 (over z_lo).
Axes of the slice: x: 4, y: 4, z: 4 (z_hi: 2, z_lo: 2; z = z_hi * 2 + z_lo), core: 2. Of those that a mesh axis runs over, the one named last changes fastest.
Arguments:
- viscosity: float32 [8, 4096, 1024], P('layer', 'tile'), may hold values from 0.02 to 0.16
- friction: float32 [4096, 1024], P('tile'), may hold values from 0.05 to 0.5
- base_vel: float32 [2, 4096, 1024], P(None, 'tile'), may hold values from -6 to 6
- surf_vel: float32 [2, 4096, 1024], P(None, 'tile'), may hold values from -6 to 6
- layer_thick: float32 [8], P('layer'), may hold values from 0.5 to 1.5
- ice_mask: int32 [4096, 1024], P('tile'), may hold values 0 or 1
- obs_slots: bfloat16 [4096, 64, 2, 128], P('tile'), may hold values from -6 to 6
- obs_target: int32 [4096, 64], P('tile'), may hold values from 0 to 1023
Outputs:
- adjoint: float32 [2, 8, 4096, 1024], P(None, 'layer', 'tile')
- gradient: float32 [4096, 1024], P('tile')
Inputs may be any that keep to these rules, and one draw needn't show every extreme that they name: `obs_target`: values below 512 name a patch of the owner's strip; values 512 or more mark an empty slot. Several slots may name the same patch.
All inputs are finite; a program needn't handle non-finite values. No bound on the sum of `ice_mask` on one device may be relied on, other than what follows from the above.
Results may differ from a plain program's by a relative error of at most 0.0025.
Values may be sent and summed in bfloat16 or wider, within the bound.
No kernel may reach another device: no remote copies, remote signals or barrier semaphores. Data moves between devices by JAX's collectives and lax.ppermute only.
A program may use at most 64 MiB of HBM per device.

v0:
```python
import jax
import jax.numpy as jnp
from jax import lax
from jax.sharding import PartitionSpec as P

PATCH = 128
SWEEPS = 3


vertical_weight = 8.0
along_weight = 4.0
cross_weight = 1.0
relax_factor = 0.7


def extended_2(x, sides, width):
    edges = {}
    for axis, dim in sides:
        devices, length = (lax.axis_size(axis), x.shape[dim])
        up = [(i, (i + 1) % devices) for i in range(devices - 1)]
        last = lax.slice_in_dim(x, length - width, length, axis=dim)
        leading = lax.slice_in_dim(x, 0, width, axis=dim)
        edges[dim] = (
            lax.ppermute(last, axis, up),
            lax.ppermute(leading, axis, [(b, a) for a, b in up]),
        )
    done = []
    for _, dim in sides:
        low, high = edges[dim]
        around = [(width, width) if d in done else (0, 0) for d in range(x.ndim)]
        x = jnp.concatenate([jnp.pad(low, around), x, jnp.pad(high, around)], axis=dim)
        done.append(dim)
    return x


def copy_for_each(x, axis):
    devices = lax.axis_size(axis)
    return lax.all_to_all(jnp.broadcast_to(x[None], (devices, *x.shape)), axis, 0, 0, tiled=True)


def taken_together(x, axis):
    return copy_for_each(x, axis).sum(axis=0)


def face_terms(visc_ext):
    centre = visc_ext[1:-1, 1:-1, 1:-1]
    below = 0.5 * (centre + visc_ext[:-2, 1:-1, 1:-1])
    above = 0.5 * (centre + visc_ext[2:, 1:-1, 1:-1])
    north = 0.5 * (centre + visc_ext[1:-1, :-2, 1:-1])
    south = 0.5 * (centre + visc_ext[1:-1, 2:, 1:-1])
    west = 0.5 * (centre + visc_ext[1:-1, 1:-1, :-2])
    east = 0.5 * (centre + visc_ext[1:-1, 1:-1, 2:])
    return (below, above, north, south, west, east)


def weights():
    row_weight = jnp.array([along_weight, cross_weight], jnp.float32).reshape(2, 1, 1, 1)
    col_weight = jnp.array([cross_weight, along_weight], jnp.float32).reshape(2, 1, 1, 1)
    return (row_weight, col_weight)


def diagonal(faces, bottom_drag):
    below, above, north, south, west, east = faces
    row_weight, col_weight = weights()
    return (
        vertical_weight * (below + above)
        + row_weight * (north + south)
        + col_weight * (west + east)
        + bottom_drag
    )


def neighbour_sum(extended, faces):
    below, above, north, south, west, east = faces
    row_weight, col_weight = weights()
    vertical = below * extended[:, :-2, 1:-1, 1:-1] + above * extended[:, 2:, 1:-1, 1:-1]
    rowwise = north * extended[:, 1:-1, :-2, 1:-1] + south * extended[:, 1:-1, 2:, 1:-1]
    colwise = west * extended[:, 1:-1, 1:-1, :-2] + east * extended[:, 1:-1, 1:-1, 2:]
    return vertical_weight * vertical + row_weight * rowwise + col_weight * colwise


def accumulate(slots, marks, patch_count):
    flat_slots = slots.reshape(-1, 2 * PATCH)
    patch_ids = jnp.arange(patch_count, dtype=jnp.int32)
    onehot = (marks.reshape(-1)[None, :] == patch_ids[:, None]).astype(jnp.bfloat16)
    summed = jnp.dot(onehot, flat_slots, preferred_element_type=jnp.float32)
    return (summed, jnp.sum(onehot, axis=1, dtype=jnp.float32))


def body(viscosity, friction, base_vel, surf_vel, layer_thick, ice_mask, obs_slots, obs_target):
    layer_count, strip_rows, strip_cols = viscosity.shape
    patch_count = strip_rows * strip_cols // PATCH
    slots, marks = (
        lax.all_to_all(obs_slots, "tile", split_axis=0, concat_axis=0, tiled=True),
        lax.all_to_all(obs_target, "tile", split_axis=0, concat_axis=0, tiled=True),
    )
    summed, counts = accumulate(slots, marks, patch_count)
    obs_sum = (
        summed.reshape(strip_rows, strip_cols // PATCH, 2, PATCH)
        .transpose(2, 0, 1, 3)
        .reshape(2, strip_rows, strip_cols)
    )
    count_map = jnp.repeat(counts.reshape(strip_rows, strip_cols // PATCH), PATCH, axis=1)
    maskf = ice_mask.astype(jnp.float32)
    misfit = maskf * (count_map * surf_vel - obs_sum)
    rhs = layer_thick[None, :, None, None] * misfit[:, None]
    visc_ext = extended_2(viscosity, (("tile", 1), ("layer", 0)), 1)
    faces = face_terms(jnp.pad(visc_ext, ((0, 0), (0, 0), (1, 1))))
    global_layer = lax.axis_index("layer") * layer_count + jnp.arange(layer_count, dtype=jnp.int32)
    bottom_drag = jnp.where(global_layer[:, None, None] == 0, friction[None], jnp.float32(0.0))
    diag = diagonal(faces, bottom_drag)
    adjoint = maskf * (relax_factor * rhs / diag)
    for sweep_index in range(SWEEPS - 1):
        extended = extended_2(adjoint.astype(jnp.bfloat16), (("tile", 2), ("layer", 1)), 1).astype(
            adjoint.dtype
        )
        extended = jnp.pad(extended, ((0, 0), (0, 0), (0, 0), (1, 1)))
        adjoint = maskf * (
            adjoint + relax_factor * (rhs - diag * adjoint + neighbour_sum(extended, faces)) / diag
        )
    partial_depth = jnp.sum(layer_thick[None, :, None, None] * adjoint, axis=1)
    integral = taken_together(partial_depth, "layer")
    gradient = -maskf * friction * (base_vel[0] * integral[0] + base_vel[1] * integral[1])
    return (adjoint, gradient)


def solution(mesh):
    in_specs = (
        P("layer", "tile", None),
        P("tile", None),
        P(None, "tile", None),
        P(None, "tile", None),
        P("layer"),
        P("tile", None),
        P("tile", None, None, None),
        P("tile", None),
    )
    out_specs = (P(None, "layer", "tile", None), P("tile", None))
    return jax.shard_map(body, mesh=mesh, in_specs=in_specs, out_specs=out_specs, check_vma=False)
```

profile of v0, /device:TPU:2, one launch (start us, length us, event | category | flops | bytes accessed | tf_op | source)
XLA Modules:
  0.0 138.3 jit_solution(730446697383781620)
XLA Ops:
  0.6 19.8 %all_to_all.19 = s32[64,1,64]{2,1,0:T(1,128)S(1)} all-to-all(s32[64,1,64]{2,1,0:T(1,128)} %bitcast.37), channel_id=1, replica_groups=mesh['tile'=64,'layer'=2] {'tile'}, dimensions={0} | all-to-all | bytes 32768 | tf_op jit(solution)/shard_map/all_to_all | solution.py:95
  20.5 6.6 %all-to-all-start.1 = ((bf16[64,64,2,128]{3,2,1,0:T(2,128)(2,1)}), bf16[64,64,2,128]{3,2,1,0:T(2,128)(2,1)}, u32[]{:S(2)}, u32[]{:S(2)}) async-start(bf16[64,64,2,128]{3,2,1,0:T(2,128)(2,1)} %param.20), calls=%async_computation.1 | async-start | bytes 4194304 | tf_op jit(solution)/shard_map/all_to_all | solution.py:94
  27.1 2.2 %collective-permute-start.1 = (f32[4,1,1024]{2,1,0:T(1,128)S(1)}, f32[4,1,1024]{2,1,0:T(1,128)S(1)}, u32[]{:S(2)}, u32[]{:S(2)}) collective-permute-start(f32[4,1,1024]{2,1,0:T(1,128)S(1)} %get-tuple-element.29), channel_id=1, source_target_pairs={{0,2},{2,4},{4,6},{6,8},{8,10},{10,12},{12,14},{14,16},{16,18},{18... | collective-permute-start | bytes 49160 | tf_op jit(solution)/shard_map/ppermute | solution.py:24
  29.3 8.0 %collective-permute-start.2 = (f32[4,1,1024]{2,1,0:T(1,128)S(1)}, f32[4,1,1024]{2,1,0:T(1,128)S(1)}, u32[]{:S(2)}, u32[]{:S(2)}) collective-permute-start(f32[4,1,1024]{2,1,0:T(1,128)S(1)} %get-tuple-element.30), channel_id=1, source_target_pairs={{2,0},{4,2},{6,4},{8,6},{10,8},{12,10},{14,12},{16,14},{18,16},{20... | collective-permute-start | bytes 49160 | tf_op jit(solution)/shard_map/ppermute | solution.py:25
  37.4 2.9 %collective-permute-start = (f32[1,64,1024]{2,1,0:T(8,128)S(1)}, f32[1,64,1024]{2,1,0:T(8,128)S(1)}, u32[]{:S(2)}, u32[]{:S(2)}) collective-permute-start(f32[1,64,1024]{2,1,0:T(8,128)S(1)} %get-tuple-element.31), channel_id=1, source_target_pairs={{0,1},{2,3},{4,5},{6,7},{8,9},{10,11},{12,13},{14,15},{16,17},{18,... | collective-permute-start | bytes 786440 | tf_op jit(solution)/shard_map/ppermute | solution.py:24
  40.3 1.3 collective-permute-start.3
  41.6 1.3 broadcast_select_fusion
  44.3 0.9 convert_reduce_fusion
  45.4 0.8 copy.33
  46.2 11.0 %collective-permute-done = f32[1,64,1024]{2,1,0:T(8,128)S(1)} collective-permute-done((f32[1,64,1024]{2,1,0:T(8,128)S(1)}, f32[1,64,1024]{2,1,0:T(8,128)S(1)}, u32[]{:S(2)}, u32[]{:S(2)}) %collective-permute-start) | collective-permute-done | bytes 262176 | tf_op jit(solution)/shard_map/ppermute | solution.py:24
  57.2 1.7 %collective-permute-done.3 = f32[1,64,1024]{2,1,0:T(8,128)S(1)} collective-permute-done((f32[1,64,1024]{2,1,0:T(8,128)S(1)}, f32[1,64,1024]{2,1,0:T(8,128)S(1)}, u32[]{:S(2)}, u32[]{:S(2)}) %collective-permute-start.3) | collective-permute-done | bytes 262176 | tf_op jit(solution)/shard_map/ppermute | solution.py:25
  59.7 3.5 %add_multiply_fusion = (f32[4,64,1024]{2,1,0:T(8,128)S(1)}, f32[4,64,1024]{2,1,0:T(8,128)}, f32[4,64,1024]{2,1,0:T(8,128)}, f32[4,64,1024]{2,1,0:T(8,128)S(1)}, ...) fusion(f32[4,64,1024]{2,1,0:T(8,128)S(1)} %copy-done.8, ...), kind=kLoop, calls=%fused_computation.98 | loop fusion | flops 6291456 | bytes 13156352 | tf_op jit(solution)/shard_map/mul | solution.py:66
  63.2 3.2 %copy.32 = bf16[512,8,2,128]{3,1,2,0:T(8,128)(2,1)} copy(bf16[512,8,2,128]{3,2,1,0:T(2,128)(2,1)} %bitcast.14) | data formatting | bytes 4194304
  66.4 4.1 %copy.22 = bf16[4096,256]{0,1:T(8,128)(2,1)} copy(bf16[4096,256]{1,0:T(8,128)(2,1)} %bitcast.33) | data formatting | bytes 4194304 | tf_op jit(solution)/shard_map/reshape | solution.py:83
  70.5 3.7 %fusion.49 = f32[2,64,8,128]{3,2,0,1:T(8,128)} fusion(bf16[2,128,4096,1]{2,1,0,3:T(8,128)(2,1)} %bitcast.34, s32[64,8]{1,0:T(8,128)S(1)} %multiply_add_fusion, s32[4096]{0:T(1024)S(1)} %eq.40), kind=kOutput, calls=%fused_computation.77 | convolution fusion | flops 1075838976 | bytes 2639872 | tf_op jit(solution)/shard_map/dot_general | solution.py:86
  74.2 2.2 %reshape.77 = f32[2,64,1024]{2,0,1:T(2,128)} reshape(f32[2,64,8,128]{3,2,0,1:T(8,128)} %fusion.49) | data formatting | bytes 1048576 | tf_op jit(solution)/shard_map/reshape | solution.py:101
  76.4 1.6 %fusion.63 = f32[2,64,1024]{2,1,0:T(8,128)S(1)} fusion(f32[2,64,1024]{2,0,1:T(2,128)} %reshape.77, f32[2,64,1024]{2,1,0:T(8,128)} %param.17, f32[64,1024]{1,0:T(8,128)} %bitcast.36, f32[64,1024]{1,0:T(8,128)S(1)} %convert_element_type.34), kind=kLoop, calls=%fused_computation.101 | loop fusion | flops 393216 | bytes 2097152 | tf_op jit(solution)/shard_map/mul | solution.py:105
  78.0 0.8 fusion.62
  78.9 3.2 %collective-permute-start.4 = (bf16[2,1,64,1024]{3,2,1,0:T(8,128)(2,1)S(1)}, bf16[2,1,64,1024]{3,2,1,0:T(8,128)(2,1)S(1)}, u32[]{:S(2)}, u32[]{:S(2)}) collective-permute-start(bf16[2,1,64,1024]{3,2,1,0:T(8,128)(2,1)S(1)} %get-tuple-element.24), channel_id=1, source_target_pairs={{0,1},{2,3},{4,5},{6,7},{8,9},{10,11},{12,13},{14,15},{16,17},{18,... | collective-permute-start | bytes 786440 | tf_op jit(solution)/shard_map/ppermute | solution.py:24
  82.1 1.3 collective-permute-start.7
  83.5 2.1 %collective-permute-start.5 = (bf16[2,4,1,1024]{3,2,1,0:T(2,128)(2,1)S(1)}, bf16[2,4,1,1024]{3,2,1,0:T(2,128)(2,1)S(1)}, u32[]{:S(2)}, u32[]{:S(2)}) collective-permute-start(bf16[2,4,1,1024]{3,2,1,0:T(2,128)(2,1)S(1)} %get-tuple-element.22), channel_id=1, source_target_pairs={{0,2},{2,4},{4,6},{6,8},{8,10},{10,12},{12,14},{14,16},{16,18},{18... | collective-permute-start | bytes 49160 | tf_op jit(solution)/shard_map/ppermute | solution.py:24
  85.6 8.4 %collective-permute-start.6 = (bf16[2,4,1,1024]{3,2,1,0:T(2,128)(2,1)S(1)}, bf16[2,4,1,1024]{3,2,1,0:T(2,128)(2,1)S(1)}, u32[]{:S(2)}, u32[]{:S(2)}) collective-permute-start(bf16[2,4,1,1024]{3,2,1,0:T(2,128)(2,1)S(1)} %get-tuple-element.23), channel_id=1, source_target_pairs={{2,0},{4,2},{6,4},{8,6},{10,8},{12,10},{14,12},{16,14},{18,16},{20... | collective-permute-start | bytes 49160 | tf_op jit(solution)/shard_map/ppermute | solution.py:25
  94.0 1.6 %collective-permute-done.6 = bf16[2,4,1,1024]{3,2,1,0:T(2,128)(2,1)S(1)} collective-permute-done((bf16[2,4,1,1024]{3,2,1,0:T(2,128)(2,1)S(1)}, bf16[2,4,1,1024]{3,2,1,0:T(2,128)(2,1)S(1)}, u32[]{:S(2)}, u32[]{:S(2)}) %collective-permute-start.6) | collective-permute-done | bytes 16416 | tf_op jit(solution)/shard_map/ppermute | solution.py:25
  96.2 4.2 %fusion.68 = (bf16[2,4,64,1024]{3,2,1,0:T(8,128)(2,1)S(1)}, f32[2,4,64,1024]{3,2,1,0:T(8,128)S(1)}) fusion(f32[4,64,1024]{2,1,0:T(8,128)S(1)} %copy-done.5, f32[2,6,66,1024]{3,2,1,0:T(8,128)S(1)} %fusion.45, f32[4,64,1024]{2,1,0:T(8,128)S(1)} %copy-done.6, f32[4,64,1024]{2,1,0:T(8,128)S(1)} %copy-done.3, f32[4,64,1024]{2,1,0:T(8,128)S(1)} %copy-done.4, ...), kind=kLoop, calls=%fused_computation.111 | loop fusion | flops 16252928 | bytes 26347008 | tf_op jit(solution)/shard_map/convert_element_type | solution.py:114
  100.5 4.6 %collective-permute-start.8 = (bf16[2,1,64,1024]{3,2,1,0:T(8,128)(2,1)S(1)}, bf16[2,1,64,1024]{3,2,1,0:T(8,128)(2,1)S(1)}, u32[]{:S(2)}, u32[]{:S(2)}) collective-permute-start(bf16[2,1,64,1024]{3,2,1,0:T(8,128)(2,1)S(1)} %get-tuple-element.20), channel_id=1, source_target_pairs={{0,1},{2,3},{4,5},{6,7},{8,9},{10,11},{12,13},{14,15},{16,17},{18,... | collective-permute-start | bytes 786440 | tf_op jit(solution)/shard_map/ppermute | solution.py:24
  105.1 1.3 collective-permute-start.11
  106.5 1.9 %collective-permute-start.9 = (bf16[2,4,1,1024]{3,2,1,0:T(2,128)(2,1)S(1)}, bf16[2,4,1,1024]{3,2,1,0:T(2,128)(2,1)S(1)}, u32[]{:S(2)}, u32[]{:S(2)}) collective-permute-start(bf16[2,4,1,1024]{3,2,1,0:T(2,128)(2,1)S(1)} %get-tuple-element.18), channel_id=1, source_target_pairs={{0,2},{2,4},{4,6},{6,8},{8,10},{10,12},{12,14},{14,16},{16,18},{18... | collective-permute-start | bytes 49160 | tf_op jit(solution)/shard_map/ppermute | solution.py:24
  108.4 8.7 %collective-permute-start.10 = (bf16[2,4,1,1024]{3,2,1,0:T(2,128)(2,1)S(1)}, bf16[2,4,1,1024]{3,2,1,0:T(2,128)(2,1)S(1)}, u32[]{:S(2)}, u32[]{:S(2)}) collective-permute-start(bf16[2,4,1,1024]{3,2,1,0:T(2,128)(2,1)S(1)} %get-tuple-element.19), channel_id=1, source_target_pairs={{2,0},{4,2},{6,4},{8,6},{10,8},{12,10},{14,12},{16,14},{18,16},{20... | collective-permute-start | bytes 49160 | tf_op jit(solution)/shard_map/ppermute | solution.py:25
  117.1 1.4 %collective-permute-done.10 = bf16[2,4,1,1024]{3,2,1,0:T(2,128)(2,1)S(1)} collective-permute-done((bf16[2,4,1,1024]{3,2,1,0:T(2,128)(2,1)S(1)}, bf16[2,4,1,1024]{3,2,1,0:T(2,128)(2,1)S(1)}, u32[]{:S(2)}, u32[]{:S(2)}) %collective-permute-start.10) | collective-permute-done | bytes 16416 | tf_op jit(solution)/shard_map/ppermute | solution.py:25
  119.0 5.3 %multiply_reduce_fusion = (f32[2,64,1024]{2,1,0:T(8,128)S(1)}, f32[2,4,64,1024]{3,2,1,0:T(8,128)}) fusion(f32[4]{0:T(128)S(1)} %copy-done.14, f32[2,4,64,1024]{3,2,1,0:T(8,128)S(1)} %get-tuple-element.5, f32[4,64,1024]{2,1,0:T(8,128)S(1)} %copy-done.5, f32[2,6,66,1024]{3,2,1,0:T(8,128)S(1)} %fusion.48, f32[4,64,1024]{2,1,0:T(8,128)S(1)} %copy-done.6, ...), kind=kLoop, calls=%fused_computation.64 | loop fusion | flops 15073280 | bytes 27919872 | tf_op jit(solution)/shard_map/reduce_sum | solution.py:121
  124.5 12.9 %all_to_all.20 = f32[2,2,64,1024]{3,2,1,0:T(8,128)S(1)} all-to-all(f32[2,2,64,1024]{3,2,1,0:T(8,128)S(1)} %broadcast_in_dim.28), channel_id=1, replica_groups=mesh['tile'=64,'layer'=2] {'layer'}, dimensions={0} | all-to-all | bytes 2097152 | tf_op jit(solution)/shard_map/all_to_all | solution.py:38
  137.5 0.8 fusion.66
  (64 shorter events, 3.9 us)
Async XLA Ops:
  20.5 6.6 %copy-start.7 = (f32[4,64,1024]{2,1,0:T(8,128)S(1)}, f32[4,64,1024]{2,1,0:T(8,128)}, u32[]{:S(2)}) copy-start(f32[4,64,1024]{2,1,0:T(8,128)} %param.14) | copy-start | bytes 3145732
  20.5 21.2 %copy-start.9 = (f32[64,1024]{1,0:T(8,128)S(1)}, f32[64,1024]{1,0:T(8,128)}, u32[]{:S(2)}) copy-start(f32[64,1024]{1,0:T(8,128)} %param.15) | copy-start | bytes 786436
  20.5 42.7 %all-to-all-start.1 = ((bf16[64,64,2,128]{3,2,1,0:T(2,128)(2,1)}), bf16[64,64,2,128]{3,2,1,0:T(2,128)(2,1)}, u32[]{:S(2)}, u32[]{:S(2)}) async-start(bf16[64,64,2,128]{3,2,1,0:T(2,128)(2,1)} %param.20), calls=%async_computation.1 | async-start | bytes 4194304 | tf_op jit(solution)/shard_map/all_to_all | solution.py:94
  27.1 15.9 %copy-start.11 = (s32[64,1024]{1,0:T(8,128)S(1)}, s32[64,1024]{1,0:T(8,128)}, u32[]{:S(2)}) copy-start(s32[64,1024]{1,0:T(8,128)} %param.19) | copy-start | bytes 786436
  27.1 31.9 %collective-permute-start.1 = (f32[4,1,1024]{2,1,0:T(1,128)S(1)}, f32[4,1,1024]{2,1,0:T(1,128)S(1)}, u32[]{:S(2)}, u32[]{:S(2)}) collective-permute-start(f32[4,1,1024]{2,1,0:T(1,128)S(1)} %get-tuple-element.29), channel_id=1, source_target_pairs={{0,2},{2,4},{4,6},{6,8},{8,10},{10,12},{12,14},{14,16},{16,18},{18... | collective-permute-start | bytes 49160 | tf_op jit(solution)/shard_map/ppermute | solution.py:24
  29.3 29.7 %collective-permute-start.2 = (f32[4,1,1024]{2,1,0:T(1,128)S(1)}, f32[4,1,1024]{2,1,0:T(1,128)S(1)}, u32[]{:S(2)}, u32[]{:S(2)}) collective-permute-start(f32[4,1,1024]{2,1,0:T(1,128)S(1)} %get-tuple-element.30), channel_id=1, source_target_pairs={{2,0},{4,2},{6,4},{8,6},{10,8},{12,10},{14,12},{16,14},{18,16},{20... | collective-permute-start | bytes 49160 | tf_op jit(solution)/shard_map/ppermute | solution.py:25
  37.4 19.8 %collective-permute-start = (f32[1,64,1024]{2,1,0:T(8,128)S(1)}, f32[1,64,1024]{2,1,0:T(8,128)S(1)}, u32[]{:S(2)}, u32[]{:S(2)}) collective-permute-start(f32[1,64,1024]{2,1,0:T(8,128)S(1)} %get-tuple-element.31), channel_id=1, source_target_pairs={{0,1},{2,3},{4,5},{6,7},{8,9},{10,11},{12,13},{14,15},{16,17},{18,... | collective-permute-start | bytes 786440 | tf_op jit(solution)/shard_map/ppermute | solution.py:24
  40.3 18.6 %collective-permute-start.3 = (f32[1,64,1024]{2,1,0:T(8,128)S(1)}, f32[1,64,1024]{2,1,0:T(8,128)S(1)}, u32[]{:S(2)}, u32[]{:S(2)}) collective-permute-start(f32[1,64,1024]{2,1,0:T(8,128)S(1)} %get-tuple-element.32), channel_id=1, source_target_pairs={{1,0},{3,2},{5,4},{7,6},{9,8},{11,10},{13,12},{15,14},{17,16},{19,... | collective-permute-start | bytes 786440 | tf_op jit(solution)/shard_map/ppermute | solution.py:25
  57.2 2.5 %copy-start.8 = (f32[4,64,1024]{2,1,0:T(8,128)S(1)}, f32[4,64,1024]{2,1,0:T(8,128)}, u32[]{:S(2)}) copy-start(f32[4,64,1024]{2,1,0:T(8,128)} %param.14) | copy-start | bytes 3145732
  74.2 3.8 %copy-start.14 = (f32[4]{0:T(128)S(1)}, f32[4]{0:T(128)}, u32[]{:S(2)}) copy-start(f32[4]{0:T(128)} %param.18) | copy-start | bytes 52
  74.2 3.8 %copy-start.15 = (f32[2]{0:T(128)S(1)}, f32[2]{0:T(128)}, u32[]{:S(2)}) copy-start(f32[2]{0:T(128)} %constant.28.clone) | copy-start | bytes 28
  74.2 3.8 %copy-start.16 = (f32[2]{0:T(128)S(1)}, f32[2]{0:T(128)}, u32[]{:S(2)}) copy-start(f32[2]{0:T(128)} %constant.27.clone) | copy-start | bytes 28
  76.4 1.6 %copy-start = (f32[4,64,1024]{2,1,0:T(8,128)S(1)}, f32[4,64,1024]{2,1,0:T(8,128)}, u32[]{:S(2)}) copy-start(f32[4,64,1024]{2,1,0:T(8,128)} %broadcast_select_fusion) | copy-start | bytes 3145732
  78.8 17.3 %copy-start.6 = (f32[4,64,1024]{2,1,0:T(8,128)S(1)}, f32[4,64,1024]{2,1,0:T(8,128)}, u32[]{:S(2)}) copy-start(f32[4,64,1024]{2,1,0:T(8,128)} %get-tuple-element.28) | copy-start | bytes 3145732
  78.9 16.7 %collective-permute-start.4 = (bf16[2,1,64,1024]{3,2,1,0:T(8,128)(2,1)S(1)}, bf16[2,1,64,1024]{3,2,1,0:T(8,128)(2,1)S(1)}, u32[]{:S(2)}, u32[]{:S(2)}) collective-permute-start(bf16[2,1,64,1024]{3,2,1,0:T(8,128)(2,1)S(1)} %get-tuple-element.24), channel_id=1, source_target_pairs={{0,1},{2,3},{4,5},{6,7},{8,9},{10,11},{12,13},{14,15},{16,17},{18,... | collective-permute-start | bytes 786440 | tf_op jit(solution)/shard_map/ppermute | solution.py:24
  82.1 13.5 %collective-permute-start.7 = (bf16[2,1,64,1024]{3,2,1,0:T(8,128)(2,1)S(1)}, bf16[2,1,64,1024]{3,2,1,0:T(8,128)(2,1)S(1)}, u32[]{:S(2)}, u32[]{:S(2)}) collective-permute-start(bf16[2,1,64,1024]{3,2,1,0:T(8,128)(2,1)S(1)} %get-tuple-element.25), channel_id=1, source_target_pairs={{1,0},{3,2},{5,4},{7,6},{9,8},{11,10},{13,12},{15,14},{17,16},{19,... | collective-permute-start | bytes 786440 | tf_op jit(solution)/shard_map/ppermute | solution.py:25
  83.4 12.8 %copy-start.5 = (f32[4,64,1024]{2,1,0:T(8,128)S(1)}, f32[4,64,1024]{2,1,0:T(8,128)}, u32[]{:S(2)}) copy-start(f32[4,64,1024]{2,1,0:T(8,128)} %get-tuple-element.27) | copy-start | bytes 3145732
  83.5 10.5 %collective-permute-start.5 = (bf16[2,4,1,1024]{3,2,1,0:T(2,128)(2,1)S(1)}, bf16[2,4,1,1024]{3,2,1,0:T(2,128)(2,1)S(1)}, u32[]{:S(2)}, u32[]{:S(2)}) collective-permute-start(bf16[2,4,1,1024]{3,2,1,0:T(2,128)(2,1)S(1)} %get-tuple-element.22), channel_id=1, source_target_pairs={{0,2},{2,4},{4,6},{6,8},{8,10},{10,12},{12,14},{14,16},{16,18},{18... | collective-permute-start | bytes 49160 | tf_op jit(solution)/shard_map/ppermute | solution.py:24
  85.5 10.6 %copy-start.1 = (f32[4,64,1024]{2,1,0:T(8,128)S(1)}, f32[4,64,1024]{2,1,0:T(8,128)}, u32[]{:S(2)}) copy-start(f32[4,64,1024]{2,1,0:T(8,128)} %get-tuple-element.7) | copy-start | bytes 3145732
  85.5 10.6 %copy-start.2 = (f32[4,64,1024]{2,1,0:T(8,128)S(1)}, f32[4,64,1024]{2,1,0:T(8,128)}, u32[]{:S(2)}) copy-start(f32[4,64,1024]{2,1,0:T(8,128)} %get-tuple-element.8) | copy-start | bytes 3145732
  85.6 10.6 %copy-start.3 = (f32[4,64,1024]{2,1,0:T(8,128)S(1)}, f32[4,64,1024]{2,1,0:T(8,128)}, u32[]{:S(2)}) copy-start(f32[4,64,1024]{2,1,0:T(8,128)} %get-tuple-element.16) | copy-start | bytes 3145732
  85.6 10.6 %copy-start.4 = (f32[4,64,1024]{2,1,0:T(8,128)S(1)}, f32[4,64,1024]{2,1,0:T(8,128)}, u32[]{:S(2)}) copy-start(f32[4,64,1024]{2,1,0:T(8,128)} %get-tuple-element.17) | copy-start | bytes 3145732
  85.6 10.0 %collective-permute-start.6 = (bf16[2,4,1,1024]{3,2,1,0:T(2,128)(2,1)S(1)}, bf16[2,4,1,1024]{3,2,1,0:T(2,128)(2,1)S(1)}, u32[]{:S(2)}, u32[]{:S(2)}) collective-permute-start(bf16[2,4,1,1024]{3,2,1,0:T(2,128)(2,1)S(1)} %get-tuple-element.23), channel_id=1, source_target_pairs={{2,0},{4,2},{6,4},{8,6},{10,8},{12,10},{14,12},{16,14},{18,16},{20... | collective-permute-start | bytes 49160 | tf_op jit(solution)/shard_map/ppermute | solution.py:25
  100.5 17.9 %collective-permute-start.8 = (bf16[2,1,64,1024]{3,2,1,0:T(8,128)(2,1)S(1)}, bf16[2,1,64,1024]{3,2,1,0:T(8,128)(2,1)S(1)}, u32[]{:S(2)}, u32[]{:S(2)}) collective-permute-start(bf16[2,1,64,1024]{3,2,1,0:T(8,128)(2,1)S(1)} %get-tuple-element.20), channel_id=1, source_target_pairs={{0,1},{2,3},{4,5},{6,7},{8,9},{10,11},{12,13},{14,15},{16,17},{18,... | collective-permute-start | bytes 786440 | tf_op jit(solution)/shard_map/ppermute | solution.py:24
  105.1 13.4 %collective-permute-start.11 = (bf16[2,1,64,1024]{3,2,1,0:T(8,128)(2,1)S(1)}, bf16[2,1,64,1024]{3,2,1,0:T(8,128)(2,1)S(1)}, u32[]{:S(2)}, u32[]{:S(2)}) collective-permute-start(bf16[2,1,64,1024]{3,2,1,0:T(8,128)(2,1)S(1)} %get-tuple-element.21), channel_id=1, source_target_pairs={{1,0},{3,2},{5,4},{7,6},{9,8},{11,10},{13,12},{15,14},{17,16},{19,... | collective-permute-start | bytes 786440 | tf_op jit(solution)/shard_map/ppermute | solution.py:25
  106.5 10.6 %collective-permute-start.9 = (bf16[2,4,1,1024]{3,2,1,0:T(2,128)(2,1)S(1)}, bf16[2,4,1,1024]{3,2,1,0:T(2,128)(2,1)S(1)}, u32[]{:S(2)}, u32[]{:S(2)}) collective-permute-start(bf16[2,4,1,1024]{3,2,1,0:T(2,128)(2,1)S(1)} %get-tuple-element.18), channel_id=1, source_target_pairs={{0,2},{2,4},{4,6},{6,8},{8,10},{10,12},{12,14},{14,16},{16,18},{18... | collective-permute-start | bytes 49160 | tf_op jit(solution)/shard_map/ppermute | solution.py:24
  108.4 10.1 %collective-permute-start.10 = (bf16[2,4,1,1024]{3,2,1,0:T(2,128)(2,1)S(1)}, bf16[2,4,1,1024]{3,2,1,0:T(2,128)(2,1)S(1)}, u32[]{:S(2)}, u32[]{:S(2)}) collective-permute-start(bf16[2,4,1,1024]{3,2,1,0:T(2,128)(2,1)S(1)} %get-tuple-element.19), channel_id=1, source_target_pairs={{2,0},{4,2},{6,4},{8,6},{10,8},{12,10},{14,12},{16,14},{18,16},{20... | collective-permute-start | bytes 49160 | tf_op jit(solution)/shard_map/ppermute | solution.py:25
  124.4 13.1 %copy-start.10 = (f32[64,1024]{1,0:T(8,128)S(1)}, f32[64,1024]{1,0:T(8,128)}, u32[]{:S(2)}) copy-start(f32[64,1024]{1,0:T(8,128)} %param.15) | copy-start | bytes 786436
  124.5 13.1 %copy-start.12 = (s32[64,1024]{1,0:T(8,128)S(1)}, s32[64,1024]{1,0:T(8,128)}, u32[]{:S(2)}) copy-start(s32[64,1024]{1,0:T(8,128)} %param.19) | copy-start | bytes 786436
  124.5 13.1 %copy-start.13 = (f32[2,64,1024]{2,1,0:T(8,128)S(1)}, f32[2,64,1024]{2,1,0:T(8,128)}, u32[]{:S(2)}) copy-start(f32[2,64,1024]{2,1,0:T(8,128)} %param.16) | copy-start | bytes 1572868
where the time goes:
time: 139 us; the launch traced here: 138 us
  starting transfers between devices  52.4 us (38%)
  blocking collectives  32.8 us (24%)
  other arithmetic  21 us (15%)
  waiting for transfers between devices  15.7 us (11%)
  local copies, waits for them, and re-layouts  11.5 us (8%)
  matrix products  3.73 us (3%)
    ppermute x6, starting transfers between devices, extended_2(): lax.ppermute(leading, axis, [(b, a) for a, b in up])  29 us
    all_to_all x1, blocking collectives, body(): lax.all_to_all(obs_target, 'tile', split_axis=0, concat_axis=0, tiled=True)  19.8 us
    ppermute x6, starting transfers between devices, extended_2(): lax.ppermute(last, axis, up)  16.9 us
    all_to_all x1, blocking collectives, copy_for_each(): lax.all_to_all(jnp.broadcast_to(x[None], (devices, *x.shape)), axis, 0, 0...  12.9 us
    ppermute x6, waiting for transfers between devices, extended_2(): lax.ppermute(last, axis, up)  11 us
    all_to_all x1, starting transfers between devices, body(): lax.all_to_all(obs_slots, 'tile', split_axis=0, concat_axis=0, tiled=True)  6.55 us
    reduce_sum x1, other arithmetic, body(): partial_depth = jnp.sum(layer_thick[None, :, None, None] * adjoint, axis=1)  5.29 us
    convert_element_type x2, other arithmetic, body(): adjoint.astype(jnp.bfloat16)  5.04 us
  transfers between devices with their start and end apart: 13, of which 4 were waited for; matrix products, arithmetic and copies ran while one was open for 6% of the time, Pallas kernels for 0%

commit v1 on v0

v1 whole, which is shorter than its diff:
```python
import jax
import jax.numpy as jnp
from jax import lax
from jax.experimental import pallas as pl
from jax.experimental.pallas import tpu as pltpu
from jax.sharding import PartitionSpec as P

F32 = jnp.float32
BF16 = jnp.bfloat16
ROWS = 64
EXT = 68
VROWS = 70
PAIR = ("tile", "layer")


def full(*shape):
    return pl.BlockSpec(memory_space=pltpu.VMEM)


def smem():
    return pl.BlockSpec(memory_space=pltpu.SMEM)


def out(shape, dtype=F32):
    return jax.ShapeDtypeStruct(shape, dtype)


def row(r):
    return pl.ds(pl.multiple_of(r * 8, 8), 8)


def east(x, last):
    r = pltpu.roll(x, 127, 1)
    return jnp.where(last, pltpu.roll(r, 7, 0), r)


def west(x, first):
    r = pltpu.roll(x, 1, 1)
    return jnp.where(first, pltpu.roll(r, 1, 0), r)


def lanes():
    lane = lax.broadcasted_iota(jnp.int32, (8, 128), 1)
    sub = lax.broadcasted_iota(jnp.int32, (8, 128), 0)
    return lane, sub


def code_of(t):
    return jnp.where(t < 512, (128 + (t & 127)) << (t >> 7), 0)


def pack_kernel(sc, slots, target, o, f, codes):
    own = sc[0]
    c = code_of(target[...]).astype(F32)
    codes[...] = jnp.concatenate([c, c], axis=1)
    for d in range(slots.shape[0]):
        f[d] = slots[d].astype(F32)
        o[d, pl.ds(0, 64), :] = f[d, pl.ds(own, 64, stride=2), :].astype(BF16)
        o[d, pl.ds(64, 8), :] = jnp.broadcast_to(codes[pl.ds(d, 1), :], (8, 128)).astype(BF16)


def pack(sc, slots, target):
    n = slots.shape[0]
    step = 16
    return pl.pallas_call(
        pack_kernel,
        grid=(n // step,),
        in_specs=[
            smem(),
            pl.BlockSpec((step, 128, 128), lambda i: (i, 0, 0)),
            pl.BlockSpec((step, 64), lambda i: (i, 0)),
        ],
        out_specs=pl.BlockSpec((step, 72, 128), lambda i: (i, 0, 0)),
        out_shape=out((n, 72, 128), BF16),
        scratch_shapes=[pltpu.VMEM((step, 128, 128), F32), pltpu.VMEM((step, 128), F32)],
    )(sc, slots, target)


def spread(dst, at, x):
    n = x.shape[0]
    for k in range(8):
        dst[pl.ds(at + k, n, stride=8), :] = x[:, k * 128 : (k + 1) * 128]


def coef_kernel(sc, visc, other, edges, fric, mask, bvel, svel, fz, fr, fc, inv, wgt, svm, msk, v, g, mk, fk, bv):
    own, odd = sc[0], sc[1]
    for i in range(4):
        for src, at in ((visc, own * 4 + i), (other, (1 - own) * 4 + i)):
            for h in range(0, ROWS, 16):
                spread(v.at[at], (3 + h) * 8, src[i, h : h + 16, :].astype(F32))
    for h in range(0, ROWS, 16):
        spread(mk, (2 + h) * 8, mask[h : h + 16, :].astype(F32))
        spread(fk, (2 + h) * 8, fric[h : h + 16, :])
        spread(svm, h * 8, svel[own, h : h + 16, :])
        for c in range(2):
            spread(bv.at[c], h * 8, bvel[c, h : h + 16, :])
    for kind in range(2):
        above = (odd + kind) % 2 == 1
        for who in range(2):
            spread(g.at[who], 0, edges[who, kind].astype(F32))
        vat = jnp.where(above, 0, 3 + ROWS)
        cat = jnp.where(above, 0, 2 + ROWS)
        for who in range(2):
            base = jnp.where(who == 0, own, 1 - own) * 4
            for i in range(4):
                for r in range(3):
                    v[base + i, row(vat + r), :] = g[who, pl.ds((i * 3 + r) * 8, 8), :]
        for r in range(2):
            mk[row(cat + r), :] = g[0, pl.ds((12 + r) * 8, 8), :]
            fk[row(cat + r), :] = g[0, pl.ds((14 + r) * 8, 8), :]
    lane, sub = lanes()
    last, first = lane == 127, lane == 0
    end = last & (sub == 7)
    start = first & (sub == 0)

    def step(r, carry):
        up, here, down = row(r), row(r + 1), row(r + 2)
        m = mk[here_of(r), :] > 0.5
        drag = fk[here_of(r), :]
        prev = None
        for l in range(8):
            c = v[l, here, :]
            fe = 0.5 * (c + jnp.where(end, 0.0, east(c, last)))
            fw = 0.5 * (c + jnp.where(start, 0.0, west(c, first)))
            south = 0.5 * (c + v[l, down, :])
            north = 0.5 * (c + v[l, up, :])
            below = 4.0 * c if l == 0 else prev
            above = 4.0 * (c + v[l + 1, here, :]) if l < 7 else 4.0 * c
            fz[l, here_of(r), :] = above
            fr[l, here_of(r), :] = south
            fc[l, here_of(r), :] = jnp.where(end, 0.0, fe)
            rows_, cols_, both = north + south, fe + fw, below + above
            if l == 0:
                both = both + drag
            for k, (rw, cw) in enumerate(((4.0, 1.0), (1.0, 4.0))):
                diag = both + rw * rows_ + cw * cols_
                inv[k, l, here_of(r), :] = jnp.where(m, 0.7 / diag, 0.0)
            prev = above
        return carry

    def here_of(r):
        return row(r)

    lax.fori_loop(0, EXT, step, 0)

    def weigh(r, carry):
        m = mk[row(r + 2), :]
        msk[row(r), :] = m
        svm[row(r), :] = svm[row(r), :] * m
        w = -m * fk[row(r + 2), :]
        for c in range(2):
            wgt[c, row(r), :] = w * bv[c, row(r), :]
        return carry

    lax.fori_loop(0, ROWS, weigh, 0)


def coefficients(sc, visc, other, edges, fric, mask, bvel, svel):
    field = (8, EXT * 8, 128)
    strip = (ROWS * 8, 128)
    return pl.pallas_call(
        coef_kernel,
        in_specs=[smem()] + [full()] * 7,
        out_specs=[full()] * 7,
        out_shape=[out(field), out(field), out(field), out((2, *field)), out((2, *strip)), out(strip), out(strip)],
        scratch_shapes=[
            pltpu.VMEM((8, VROWS * 8, 128), F32),
            pltpu.VMEM((2, 128, 128), F32),
            pltpu.VMEM((EXT * 8, 128), F32),
            pltpu.VMEM((EXT * 8, 128), F32),
            pltpu.VMEM((2, *strip), F32),
        ],
    )(sc, visc, other, edges, fric, mask, bvel, svel)


def misfit_kernel(sc, got, svm, msk, m_out, e_out, hot, rhs, pc):
    odd = sc[1]
    p = lax.broadcasted_iota(jnp.int32, (512, 128), 0)
    pc[...] = code_of(p).astype(F32)
    lane = lax.broadcasted_iota(jnp.int32, (8, 128), 1)
    for b in range(32):
        for h in range(2):
            rhs[pl.ds(b * 128 + h * 64, 64), pl.ds(0, 128)] = got[2 * b + h, pl.ds(0, 64), :]
        c = jnp.where(
            lane < 64, got[2 * b, pl.ds(64, 8), :].astype(F32), got[2 * b + 1, pl.ds(64, 8), :].astype(F32)
        )
        same = pc[...].reshape(64, 8, 128) == c[None]
        hot[:, pl.ds(b * 128, 128)] = jnp.where(same, 1.0, 0.0).reshape(512, 128).astype(BF16)
    rhs[:, pl.ds(128, 128)] = jnp.ones((4096, 128), BF16)
    sums = jnp.dot(hot[...], rhs[...], preferred_element_type=F32)
    m_out[...] = sums[:, 128:] * svm[...] - msk[...] * sums[:, :128]
    for kind in range(2):
        at = jnp.where((odd + kind) % 2 == 0, ROWS - 2, 0)
        for r in range(2):
            e_out[kind, pl.ds(r * 8, 8), :] = m_out[row(at + r), :]


def misfit(sc, got, svm, msk):
    return pl.pallas_call(
        misfit_kernel,
        in_specs=[smem()] + [full()] * 3,
        out_specs=[full()] * 2,
        out_shape=[out((ROWS * 8, 128)), out((2, 16, 128))],
        scratch_shapes=[
            pltpu.VMEM((512, 4096), BF16),
            pltpu.VMEM((4096, 256), BF16),
            pltpu.VMEM((512, 128), F32),
        ],
    )(sc, got, svm, msk)


def sweep_kernel(sc, thick, m_own, m_oth, e_own, e_oth, fz, fr, fc, inv, wgt, adj, grad, m, a1, a2, a3, acc):
    own, odd = sc[0], sc[1]
    lane, _ = lanes()
    last, first = lane == 127, lane == 0

    def relaxed(a, l, r, c, rw, cw):
        here = row(r)
        x = a[l, here, :]
        n = None
        if l < 7:
            n = fz[l, here, :] * a[l + 1, here, :]
        if l > 0:
            t = fz[l - 1, here, :] * a[l - 1, here, :]
            n = t if n is None else n + t
        rows_ = fr[l, here, :] * a[l, row(r + 1), :] + fr[l, row(r - 1), :] * a[l, row(r - 1), :]
        f = fc[l, here, :]
        cols_ = f * east(x, last) + west(f * x, first)
        n = n + rw * rows_ + cw * cols_
        return 0.3 * x + inv[c, l, here, :] * (thick[l] * m[here, :] + n)

    for q in range(2):
        c = own if q == 0 else 1 - own
        mine, edge = (m_own, e_own) if q == 0 else (m_oth, e_oth)
        m[pl.ds(16, ROWS * 8), :] = mine[...]
        for kind in range(2):
            above = (odd + kind) % 2 == 1
            at = jnp.where(above, 0, ROWS + 2)
            for r in range(2):
                m[row(at + r), :] = edge[kind, pl.ds(r * 8, 8), :]
        rw = jnp.where(c == 0, 4.0, 1.0)
        cw = jnp.where(c == 0, 1.0, 4.0)

        def first_sweep(r):
            for l in range(8):
                a1[l, row(r), :] = inv[c, l, row(r), :] * (thick[l] * m[row(r), :])

        def second_sweep(r):
            for l in range(8):
                a2[l, row(r), :] = relaxed(a1, l, r, c, rw, cw)

        def third_sweep(r):
            total = None
            for l in range(8):
                y = relaxed(a2, l, r, c, rw, cw)
                a3[l, row(r - 2), :] = y
                total = thick[l] * y if l == 0 else total + thick[l] * y
            w = wgt[c, row(r - 2), :] * total
            acc[row(r - 2), :] = w if q == 0 else acc[row(r - 2), :] + w

        for r in range(4):
            first_sweep(r)
        for r in range(1, 3):
            second_sweep(r)

        def step(r, carry):
            first_sweep(r)
            second_sweep(r - 1)
            third_sweep(r - 2)
            return carry

        lax.fori_loop(4, EXT, step, 0)
        for i in range(4):
            for h in range(0, ROWS, 8):
                for k in range(8):
                    adj[c, i, pl.ds(h, 8), pl.ds(k * 128, 128)] = a3[own * 4 + i, pl.ds(h * 8 + k, 8, stride=8), :]
    for h in range(0, ROWS, 8):
        for k in range(8):
            grad[pl.ds(h, 8), pl.ds(k * 128, 128)] = acc[pl.ds(h * 8 + k, 8, stride=8), :]


def sweeps(sc, thick, m_own, m_oth, e_own, e_oth, fz, fr, fc, inv, wgt):
    return pl.pallas_call(
        sweep_kernel,
        in_specs=[smem(), smem()] + [full()] * 9,
        out_specs=[full()] * 2,
        out_shape=[out((2, 4, ROWS, 1024)), out((ROWS, 1024))],
        scratch_shapes=[
            pltpu.VMEM((EXT * 8, 128), F32),
            pltpu.VMEM((8, EXT * 8, 128), F32),
            pltpu.VMEM((8, EXT * 8, 128), F32),
            pltpu.VMEM((8, ROWS * 8, 128), F32),
            pltpu.VMEM((ROWS * 8, 128), F32),
        ],
    )(sc, thick, m_own, m_oth, e_own, e_oth, fz, fr, fc, inv, wgt)


def swaps(tiles, offset, across):
    perm = []
    for t in range(offset, tiles - 1, 2):
        for layer in range(2):
            a, b = t * 2 + layer, (t + 1) * 2 + (1 - layer if across else layer)
            perm += [(a, b), (b, a)]
    return perm


def swap_layers(x):
    return lax.ppermute(x, "layer", [(0, 1), (1, 0)])


def body(viscosity, friction, base_vel, surf_vel, layer_thick, ice_mask, obs_slots, obs_target):
    tiles = lax.axis_size("tile")
    own = lax.axis_index("layer")
    odd = lax.axis_index("tile") % 2
    sc = jnp.stack([own, odd]).astype(jnp.int32)

    other = swap_layers(viscosity.astype(BF16))
    payload = pack(sc, obs_slots.reshape(tiles, 128, 128), obs_target)
    got = lax.all_to_all(payload, "tile", split_axis=0, concat_axis=0, tiled=True)

    def edge(at):
        return jnp.concatenate(
            [
                lax.slice_in_dim(viscosity, (ROWS - 3) if at else 0, ROWS if at else 3, axis=1).reshape(12, 1024),
                lax.slice_in_dim(ice_mask, (ROWS - 2) if at else 0, ROWS if at else 2, axis=0).astype(F32),
                lax.slice_in_dim(friction, (ROWS - 2) if at else 0, ROWS if at else 2, axis=0),
            ]
        ).astype(BF16)

    top, bottom = edge(0), edge(1)
    to_a = jnp.where(odd == 0, bottom, top)
    to_b = jnp.where(odd == 0, top, bottom)
    edges = jnp.stack(
        [
            jnp.stack([lax.ppermute(to_a, PAIR, swaps(tiles, 0, False)), lax.ppermute(to_b, PAIR, swaps(tiles, 1, False))]),
            jnp.stack([lax.ppermute(to_a, PAIR, swaps(tiles, 0, True)), lax.ppermute(to_b, PAIR, swaps(tiles, 1, True))]),
        ]
    )
    thick_other = swap_layers(layer_thick)
    thick = jnp.where(
        own == 0, jnp.concatenate([layer_thick, thick_other]), jnp.concatenate([thick_other, layer_thick])
    )
    fz, fr, fc, inv, wgt, svm, msk = coefficients(
        sc, viscosity, other, edges, friction, ice_mask, base_vel, surf_vel
    )
    m_own, e_send = misfit(sc, got, svm, msk)
    m_oth = swap_layers(m_own)
    e_own = jnp.stack(
        [
            lax.ppermute(e_send[0], PAIR, swaps(tiles, 0, False)),
            lax.ppermute(e_send[1], PAIR, swaps(tiles, 1, False)),
        ]
    )
    e_oth = swap_layers(e_own)
    adjoint, gradient = sweeps(sc, thick, m_own, m_oth, e_own, e_oth, fz, fr, fc, inv, wgt)
    return adjoint, gradient


def solution(mesh):
    in_specs = (
        P("layer", "tile", None),
        P("tile", None),
        P(None, "tile", None),
        P(None, "tile", None),
        P("layer"),
        P("tile", None),
        P("tile", None, None, None),
        P("tile", None),
    )
    out_specs = (P(None, "layer", "tile", None), P("tile", None))
    return jax.shard_map(body, mesh=mesh, in_specs=in_specs, out_specs=out_specs, check_vma=False)
```

time: 139 us -> 107 us (0.77)
  Pallas kernels: 0 us -> 54.3 us
  blocking collectives: 32.8 us -> 0 us
  starting transfers between devices: 52.4 us -> 30.9 us
  other arithmetic: 21 us -> 4.02 us
  local copies, waits for them, and re-layouts: 11.5 us -> 3.34 us
  matrix products: 3.73 us -> 0 us
  waiting for transfers between devices: 15.7 us -> 13.1 us
    pallas_call x0 -> x4, Pallas kernels: none -> 54.3 us  [the longest x1 32.3 us: sweeps(): pl.pallas_call(sweep_kernel, in_specs=[smem(), smem()] + [full()] * 9, ou...]
    all_to_all x2 -> x0, blocking collectives: 32.8 us -> none  [the longest x1 19.8 us: body(): lax.all_to_all(obs_target, 'tile', split_axis=0, concat_axis=0, tiled=True)]
    ppermute x12 -> x10, starting transfers between devices: 45.9 us -> 19.8 us  [the longest x1 7.24 us: body(): lax.ppermute(to_b, PAIR, swaps(tiles, 1, True))]
    reduce_sum x3 -> x0, other arithmetic: 6.31 us -> none  [the longest x1 5.29 us: body(): partial_depth = jnp.sum(layer_thick[None, :, None, None] * adjoint, axis=1)]
    reshape x3 -> x2, local copies, waits for them, and re-layouts: 6.36 us -> 0.06 us  [edge(): lax.slice_in_dim(viscosity, ROWS - 3 if at else 0, ROWS if at else 3, axi...]
    mul x3 -> x0, other arithmetic: 5.89 us -> none  [the longest x1 3.49 us: diagonal(): vertical_weight * (below + above) + row_weight * (north + south)]
    convert_element_type x5 -> x1, other arithmetic: 6.18 us -> 1.29 us  [body(): other = swap_layers(viscosity.astype(BF16))]
    all_to_all x1, starting transfers between devices: 6.55 us -> 11 us  [body(): lax.all_to_all(payload, 'tile', split_axis=0, concat_axis=0, tiled=True)]
  transfers between devices with their start and end apart: 13 -> 11, of which waited for: 4 -> 4; matrix products, arithmetic and copies ran while one was open for 6% -> 3% of each run, Pallas kernels for 0% -> 17%
where the time goes in v1:
time: 107 us; the launch traced here: 106 us
  Pallas kernels  54.3 us (51%)
  starting transfers between devices  30.9 us (29%)
  waiting for transfers between devices  13.1 us (12%)
  other arithmetic  4.02 us (4%)
  local copies, waits for them, and re-layouts  3.34 us (3%)
    pallas_call x1, Pallas kernels, sweeps(): pl.pallas_call(sweep_kernel, in_specs=[smem(), smem()] + [full()] * 9, ou...  32.3 us
    pallas_call x1, Pallas kernels, coefficients(): pl.pallas_call(coef_kernel, in_specs=[smem()] + [full()] * 7, out_specs=[...  14.4 us
    all_to_all x1, starting transfers between devices, body(): lax.all_to_all(payload, 'tile', split_axis=0, concat_axis=0, tiled=True)  11 us
    ppermute x1, starting transfers between devices, body(): lax.ppermute(to_b, PAIR, swaps(tiles, 1, True))  7.24 us
    ppermute x1, waiting for transfers between devices, body(): lax.ppermute(to_b, PAIR, swaps(tiles, 1, True))  5.47 us
    ppermute x4, starting transfers between devices, swap_layers(): return lax.ppermute(x, 'layer', [(0, 1), (1, 0)])  4.88 us
    ppermute x1, waiting for transfers between devices, body(): lax.ppermute(e_send[1], PAIR, swaps(tiles, 1, False))  4.81 us
    pallas_call x1, Pallas kernels, pack(): pl.pallas_call(pack_kernel, grid=(n // step,), in_specs=[smem(), pl.Block...  3.93 us
  transfers between devices with their start and end apart: 11, of which 4 were waited for; matrix products, arithmetic and copies ran while one was open for 3% of the time, Pallas kernels for 17%

profile of v1, /device:TPU:2, one launch (start us, length us, event | category | flops | bytes accessed | tf_op | source)
XLA Modules:
  0.0 106.5 jit_solution(6199824100670472023)
XLA Ops:
  0.6 1.3 %convert_element_type.11 = bf16[4,64,1024]{2,1,0:T(8,128)(2,1)S(1)} convert(f32[4,64,1024]{2,1,0:T(8,128)} %visc.1) | non-fusion elementwise | flops 262144 | bytes 1572864 | tf_op jit(solution)/shard_map/convert_element_type | solution.py:317
  1.9 2.0 %collective-permute-start.1 = (bf16[4,64,1024]{2,1,0:T(8,128)(2,1)S(1)}, bf16[4,64,1024]{2,1,0:T(8,128)(2,1)S(1)}, u32[]{:S(2)}, u32[]{:S(2)}) collective-permute-start(bf16[4,64,1024]{2,1,0:T(8,128)(2,1)S(1)} %convert_element_type.11), channel_id=1, source_target_pairs={{0,1},{1,0},{2,3},{3,2},{4,5},{5,4},{6,7},{7,6},{8,9},{9,8},{10,11... | collective-permute-start | bytes 1572872 | tf_op jit(solution)/shard_map/ppermute | solution.py:308
  3.9 0.6 pad_add_fusion.sc
  4.5 3.9 %shard_map.95 = bf16[64,72,128]{2,1,0:T(8,128)(2,1)} custom-call(s32[2]{0:T(128)} %pad_add_fusion.sc, bf16[64,128,128]{2,1,0:T(8,128)(2,1)} %bitcast.17, s32[64,64]{1,0:T(8,128)} %target.1), custom_call_target="tpu_custom_call" | custom-call | tf_op jit(solution)/shard_map/pallas_call | solution.py:65
  8.4 11.0 %all-to-all-start = ((bf16[64,72,128]{2,1,0:T(8,128)(2,1)}), bf16[64,72,128]{2,1,0:T(8,128)(2,1)S(1)}, u32[]{:S(2)}, u32[]{:S(2)}) async-start(bf16[64,72,128]{2,1,0:T(8,128)(2,1)} %shard_map.95), calls=%async_computation | async-start | bytes 2359296 | tf_op jit(solution)/shard_map/all_to_all | solution.py:319
  19.5 0.8 convert_convert_fusion.1
  20.5 0.1 collective-permute-start.4
  20.6 7.2 %collective-permute-start.5 = (bf16[16,1024]{1,0:T(8,128)(2,1)S(1)}, bf16[16,1024]{1,0:T(8,128)(2,1)S(1)}, u32[]{:S(2)}, u32[]{:S(2)}) collective-permute-start(bf16[16,1024]{1,0:T(8,128)(2,1)S(1)} %get-tuple-element.27), channel_id=1, source_target_pairs={{2,5},{5,2},{3,4},{4,3},{6,9},{9,6},{7,8},{8,7},{10,13},{13,10},{1... | collective-permute-start | bytes 98312 | tf_op jit(solution)/shard_map/ppermute | solution.py:336
  27.8 0.1 collective-permute-start.2
  27.9 3.8 %collective-permute-start.3 = (bf16[16,1024]{1,0:T(8,128)(2,1)S(1)}, bf16[16,1024]{1,0:T(8,128)(2,1)S(1)}, u32[]{:S(2)}, u32[]{:S(2)}) collective-permute-start(bf16[16,1024]{1,0:T(8,128)(2,1)S(1)} %get-tuple-element.27), channel_id=1, source_target_pairs={{2,4},{4,2},{3,5},{5,3},{6,8},{8,6},{7,9},{9,7},{10,12},{12,10},{1... | collective-permute-start | bytes 98312 | tf_op jit(solution)/shard_map/ppermute | solution.py:335
  31.7 0.0 collective-permute-done.4
  31.7 5.5 %collective-permute-done.5 = bf16[16,1024]{1,0:T(8,128)(2,1)S(1)} collective-permute-done((bf16[16,1024]{1,0:T(8,128)(2,1)S(1)}, bf16[16,1024]{1,0:T(8,128)(2,1)S(1)}, u32[]{:S(2)}, u32[]{:S(2)}) %collective-permute-start.5) | collective-permute-done | bytes 32800 | tf_op jit(solution)/shard_map/ppermute | solution.py:336
  37.2 0.0 collective-permute-done.2
  37.2 1.7 %collective-permute-done.3 = bf16[16,1024]{1,0:T(8,128)(2,1)S(1)} collective-permute-done((bf16[16,1024]{1,0:T(8,128)(2,1)S(1)}, bf16[16,1024]{1,0:T(8,128)(2,1)S(1)}, u32[]{:S(2)}, u32[]{:S(2)}) %collective-permute-start.3) | collective-permute-done | bytes 32800 | tf_op jit(solution)/shard_map/ppermute | solution.py:335
  38.9 0.7 pad_maximum_fusion.edges
  39.6 0.0 collective-permute-done.1.other
  39.6 0.8 copy-done.2
  40.4 14.4 %shard_map.96 = (f32[8,544,128]{2,1,0:T(8,128)}, f32[8,544,128]{2,1,0:T(8,128)}, f32[8,544,128]{2,1,0:T(8,128)}, f32[2,8,544,128]{3,2,1,0:T(8,128)}, f32[2,512,1...) custom-call(s32[2]{0:T(128)} %pad_add_fusion.sc, f32[4,64,1024]{2,1,0:T(8,128)} %visc.1, ...), custom_call_target="tpu_custom_call" | custom-call | tf_op jit(solution)/shard_map/pallas_call | solution.py:161
  54.8 0.0 all-to-all-done.got
  54.8 1.0 copy-done
  55.8 3.8 %shard_map.97 = (f32[512,128]{1,0:T(8,128)}, f32[2,16,128]{2,1,0:T(8,128)}) custom-call(s32[2]{0:T(128)} %pad_add_fusion.sc, bf16[64,72,128]{2,1,0:T(8,128)(2,1)} %copy-done, f32[512,128]{1,0:T(8,128)} %get-tuple-element.11.svm, f32[512,128]{1,0:T(8,128)} %get-tuple-element.12.msk), custom_call_target="tpu_custom_call" | custom-call | tf_op jit(solution)/shard_map/pallas_call | solution.py:199
  59.5 0.0 collective-permute-start.6
  59.5 0.7 slice_bitcast_fusion.1
  60.3 3.8 %collective-permute-start.8 = (f32[16,128]{1,0:T(8,128)S(1)}, f32[16,128]{1,0:T(8,128)S(1)}, u32[]{:S(2)}, u32[]{:S(2)}) collective-permute-start(f32[16,128]{1,0:T(8,128)S(1)} %get-tuple-element.29), channel_id=1, source_target_pairs={{2,4},{4,2},{3,5},{5,3},{6,8},{8,6},{7,9},{9,7},{10,12},{12,10},{1... | collective-permute-start | bytes 24584 | tf_op jit(solution)/shard_map/ppermute | solution.py:351
  64.0 0.9 collective-permute-start
  64.9 4.8 %collective-permute-done.8 = f32[16,128]{1,0:T(8,128)S(1)} collective-permute-done((f32[16,128]{1,0:T(8,128)S(1)}, f32[16,128]{1,0:T(8,128)S(1)}, u32[]{:S(2)}, u32[]{:S(2)}) %collective-permute-start.8) | collective-permute-done | bytes 8224 | tf_op jit(solution)/shard_map/ppermute | solution.py:351
  69.7 2.0 %collective-permute-start.9 = (f32[2,16,128]{2,1,0:T(8,128)S(1)}, f32[2,16,128]{2,1,0:T(8,128)S(1)}, u32[]{:S(2)}, u32[]{:S(2)}) collective-permute-start(f32[2,16,128]{2,1,0:T(8,128)S(1)} %pad_maximum_fusion.3.e_own), channel_id=1, source_target_pairs={{0,1},{1,0},{2,3},{3,2},{4,5},{5,4},{6,7},{7,6},{8,9},{9,8},{10,11... | collective-permute-start | bytes 49160 | tf_op jit(solution)/shard_map/ppermute | solution.py:308
  71.8 0.6 broadcast_select_fusion.2.thick
  72.4 1.1 %collective-permute-done.9.e_oth = f32[2,16,128]{2,1,0:T(8,128)S(1)} collective-permute-done((f32[2,16,128]{2,1,0:T(8,128)S(1)}, f32[2,16,128]{2,1,0:T(8,128)S(1)}, u32[]{:S(2)}, u32[]{:S(2)}) %collective-permute-start.9) | collective-permute-done | bytes 16416 | tf_op jit(solution)/shard_map/ppermute | solution.py:308
  73.5 0.6 copy-done.5
  74.1 0.1 copy-done.3
  74.2 32.3 %shard_map.98 = (f32[2,4,64,1024]{3,2,1,0:T(8,128)}, f32[64,1024]{1,0:T(8,128)}) custom-call(s32[2]{0:T(128)} %pad_add_fusion.sc, f32[8]{0:T(128)} %broadcast_select_fusion.2.thick, f32[512,128]{1,0:T(8,128)} %get-tuple-element.13.m_own, f32[512,128]{1,0:T(8,128)} %copy-done.3, f32[2,16,128]{2,1,0:T(8,128)} %copy-done.4, f32[2,16,128]{2,1,0:T(8,128)} %copy-done.5, ...), custom_call_target="tpu_custom_call" | custom-call | tf_op jit(solution)/shard_map/pallas_call | solution.py:283
  (23 shorter events, 0.2 us)
Async XLA Ops:
  1.9 37.7 %collective-permute-start.1 = (bf16[4,64,1024]{2,1,0:T(8,128)(2,1)S(1)}, bf16[4,64,1024]{2,1,0:T(8,128)(2,1)S(1)}, u32[]{:S(2)}, u32[]{:S(2)}) collective-permute-start(bf16[4,64,1024]{2,1,0:T(8,128)(2,1)S(1)} %convert_element_type.11), channel_id=1, source_target_pairs={{0,1},{1,0},{2,3},{3,2},{4,5},{5,4},{6,7},{7,6},{8,9},{9,8},{10,11... | collective-permute-start | bytes 1572872 | tf_op jit(solution)/shard_map/ppermute | solution.py:308
  4.5 15.0 %copy-start.1 = (f32[64,1024]{1,0:T(8,128)S(1)}, f32[64,1024]{1,0:T(8,128)}, u32[]{:S(2)}) copy-start(f32[64,1024]{1,0:T(8,128)} %fric.1) | copy-start | bytes 786436
  8.4 46.3 %all-to-all-start = ((bf16[64,72,128]{2,1,0:T(8,128)(2,1)}), bf16[64,72,128]{2,1,0:T(8,128)(2,1)S(1)}, u32[]{:S(2)}, u32[]{:S(2)}) async-start(bf16[64,72,128]{2,1,0:T(8,128)(2,1)} %shard_map.95), calls=%async_computation | async-start | bytes 2359296 | tf_op jit(solution)/shard_map/all_to_all | solution.py:319
  20.5 11.2 %collective-permute-start.4 = (bf16[16,1024]{1,0:T(8,128)(2,1)S(1)}, bf16[16,1024]{1,0:T(8,128)(2,1)S(1)}, u32[]{:S(2)}, u32[]{:S(2)}) collective-permute-start(bf16[16,1024]{1,0:T(8,128)(2,1)S(1)} %get-tuple-element.26), channel_id=1, source_target_pairs={{0,3},{3,0},{1,2},{2,1},{4,7},{7,4},{5,6},{6,5},{8,11},{11,8},{9,1... | collective-permute-start | bytes 98312 | tf_op jit(solution)/shard_map/ppermute | solution.py:336
  20.6 16.6 %collective-permute-start.5 = (bf16[16,1024]{1,0:T(8,128)(2,1)S(1)}, bf16[16,1024]{1,0:T(8,128)(2,1)S(1)}, u32[]{:S(2)}, u32[]{:S(2)}) collective-permute-start(bf16[16,1024]{1,0:T(8,128)(2,1)S(1)} %get-tuple-element.27), channel_id=1, source_target_pairs={{2,5},{5,2},{3,4},{4,3},{6,9},{9,6},{7,8},{8,7},{10,13},{13,10},{1... | collective-permute-start | bytes 98312 | tf_op jit(solution)/shard_map/ppermute | solution.py:336
  27.8 9.3 %collective-permute-start.2 = (bf16[16,1024]{1,0:T(8,128)(2,1)S(1)}, bf16[16,1024]{1,0:T(8,128)(2,1)S(1)}, u32[]{:S(2)}, u32[]{:S(2)}) collective-permute-start(bf16[16,1024]{1,0:T(8,128)(2,1)S(1)} %get-tuple-element.26), channel_id=1, source_target_pairs={{0,2},{2,0},{1,3},{3,1},{4,6},{6,4},{5,7},{7,5},{8,10},{10,8},{9,1... | collective-permute-start | bytes 98312 | tf_op jit(solution)/shard_map/ppermute | solution.py:335
  27.9 11.0 %collective-permute-start.3 = (bf16[16,1024]{1,0:T(8,128)(2,1)S(1)}, bf16[16,1024]{1,0:T(8,128)(2,1)S(1)}, u32[]{:S(2)}, u32[]{:S(2)}) collective-permute-start(bf16[16,1024]{1,0:T(8,128)(2,1)S(1)} %get-tuple-element.27), channel_id=1, source_target_pairs={{2,4},{4,2},{3,5},{5,3},{6,8},{8,6},{7,9},{9,7},{10,12},{12,10},{1... | collective-permute-start | bytes 98312 | tf_op jit(solution)/shard_map/ppermute | solution.py:335
  39.6 24.5 %copy-start.6 = (f32[4]{0:T(128)S(1)}, f32[4]{0:T(128)}, u32[]{:S(2)}) copy-start(f32[4]{0:T(128)} %param.12) | copy-start | bytes 52
  39.6 0.8 copy-start.2
  54.8 1.0 copy-start
  59.5 13.9 %collective-permute-start.6 = (f32[512,128]{1,0:T(8,128)}, f32[512,128]{1,0:T(8,128)S(1)}, u32[]{:S(2)}, u32[]{:S(2)}) collective-permute-start(f32[512,128]{1,0:T(8,128)} %get-tuple-element.13.m_own), channel_id=1, source_target_pairs={{0,1},{1,0},{2,3},{3,2},{4,5},{5,4},{6,7},{7,6},{8,9},{9,8},{10,11... | collective-permute-start | bytes 786440 | tf_op jit(solution)/shard_map/ppermute | solution.py:308
  60.3 4.7 %collective-permute-start.7 = (f32[16,128]{1,0:T(8,128)S(1)}, f32[16,128]{1,0:T(8,128)S(1)}, u32[]{:S(2)}, u32[]{:S(2)}) collective-permute-start(f32[16,128]{1,0:T(8,128)S(1)} %get-tuple-element.28), channel_id=1, source_target_pairs={{0,2},{2,0},{1,3},{3,1},{4,6},{6,4},{5,7},{7,5},{8,10},{10,8},{9,1... | collective-permute-start | bytes 24584 | tf_op jit(solution)/shard_map/ppermute | solution.py:350
  60.3 9.5 %collective-permute-start.8 = (f32[16,128]{1,0:T(8,128)S(1)}, f32[16,128]{1,0:T(8,128)S(1)}, u32[]{:S(2)}, u32[]{:S(2)}) collective-permute-start(f32[16,128]{1,0:T(8,128)S(1)} %get-tuple-element.29), channel_id=1, source_target_pairs={{2,4},{4,2},{3,5},{5,3},{6,8},{8,6},{7,9},{9,7},{10,12},{12,10},{1... | collective-permute-start | bytes 24584 | tf_op jit(solution)/shard_map/ppermute | solution.py:351
  64.0 7.7 %collective-permute-start = (f32[4]{0:T(128)S(1)}, f32[4]{0:T(128)S(1)}, u32[]{:S(2)}, u32[]{:S(2)}) collective-permute-start(f32[4]{0:T(128)S(1)} %copy-done.6), channel_id=1, source_target_pairs={{0,1},{1,0},{2,3},{3,2},{4,5},{5,4},{6,7},{7,6},{8,9},{9,8},{10,11... | collective-permute-start | bytes 56 | tf_op jit(solution)/shard_map/ppermute | solution.py:308
  69.7 3.8 %copy-start.4 = (f32[2,16,128]{2,1,0:T(8,128)}, f32[2,16,128]{2,1,0:T(8,128)S(1)}, u32[]{:S(2)}) copy-start(f32[2,16,128]{2,1,0:T(8,128)S(1)} %pad_maximum_fusion.3.e_own) | copy-start | bytes 49156
  69.7 3.7 %collective-permute-start.9 = (f32[2,16,128]{2,1,0:T(8,128)S(1)}, f32[2,16,128]{2,1,0:T(8,128)S(1)}, u32[]{:S(2)}, u32[]{:S(2)}) collective-permute-start(f32[2,16,128]{2,1,0:T(8,128)S(1)} %pad_maximum_fusion.3.e_own), channel_id=1, source_target_pairs={{0,1},{1,0},{2,3},{3,2},{4,5},{5,4},{6,7},{7,6},{8,9},{9,8},{10,11... | collective-permute-start | bytes 49160 | tf_op jit(solution)/shard_map/ppermute | solution.py:308
  73.5 0.6 copy-start.5
  73.5 0.7 copy-start.3

commit v2 on v1

v2 whole, which is shorter than its diff:
```python
import jax
import jax.numpy as jnp
from jax import lax
from jax.experimental import pallas as pl
from jax.experimental.pallas import tpu as pltpu
from jax.sharding import PartitionSpec as P

F32 = jnp.float32
BF16 = jnp.bfloat16
ROWS = 64
EXT = 68
PAIR = ("tile", "layer")
FIELD = (8, EXT * 8, 128)
STRIP = (ROWS * 8, 128)
MIB = 1 << 20


def vm():
    return pl.BlockSpec(memory_space=pltpu.VMEM)


def sm():
    return pl.BlockSpec(memory_space=pltpu.SMEM)


def hbm():
    return pl.BlockSpec(memory_space=pl.ANY)


def kept(*shape, dtype=F32):
    return pltpu.VMEM(shape, dtype)


def near(x):
    return pltpu.with_memory_space_constraint(x, pltpu.VMEM)


def row(r):
    return pl.ds(pl.multiple_of(r * 8, 8), 8)


def place(sc):
    return sc[0] & 1, sc[0] >> 1


def lanes():
    lane = lax.broadcasted_iota(jnp.int32, (8, 128), 1)
    sub = lax.broadcasted_iota(jnp.int32, (8, 128), 0)
    return lane, sub


def east(x, last):
    r = pltpu.roll(x, 127, 1)
    return jnp.where(last, pltpu.roll(r, 7, 0), r)


def west(x, first):
    r = pltpu.roll(x, 1, 1)
    return jnp.where(first, pltpu.roll(r, 1, 0), r)


def code_of(t):
    return jnp.where(t < 512, (128 + (t & 127)) << (t >> 7), 0)


def pack_kernel(sc, slots, target, o, f, codes):
    own, _ = place(sc)
    c = code_of(target[...]).astype(F32)
    codes[...] = jnp.concatenate([c, c], axis=1)
    for d in range(slots.shape[0]):
        f[d] = slots[d].astype(F32)
        o[d, pl.ds(0, 64), :] = f[d, pl.ds(own, 64, stride=2), :].astype(BF16)
        o[d, pl.ds(64, 8), :] = jnp.broadcast_to(codes[pl.ds(d, 1), :], (8, 128)).astype(BF16)


def pack(sc, slots, target):
    n = slots.shape[0]
    step = 8
    return pl.pallas_call(
        pack_kernel,
        grid=(n // step,),
        in_specs=[
            sm(),
            pl.BlockSpec((step, 128, 128), lambda i: (i, 0, 0)),
            pl.BlockSpec((step, 64), lambda i: (i, 0)),
        ],
        out_specs=pl.BlockSpec((step, 72, 128), lambda i: (i, 0, 0)),
        out_shape=jax.ShapeDtypeStruct((n, 72, 128), BF16),
        scratch_shapes=[pltpu.VMEM((step, 128, 128), F32), pltpu.VMEM((step, 128), F32)],
        compiler_params=pltpu.CompilerParams(vmem_limit_bytes=8 * MIB),
    )(sc, slots, target)


def spread(dst, at, x):
    n = x.shape[0]
    for k in range(8):
        dst[pl.ds(at + k, n, stride=8), :] = x[:, k * 128 : (k + 1) * 128]


def coefficient_row(view, m, drag, r, fz, fr, fc, inv):
    lane, sub = lanes()
    last, first = lane == 127, lane == 0
    end = last & (sub == 7)
    start = first & (sub == 0)
    prev = None
    for l in range(8):
        c = view(l, 0)
        fe = 0.5 * (c + jnp.where(end, 0.0, east(c, last)))
        fw = 0.5 * (c + jnp.where(start, 0.0, west(c, first)))
        south = 0.5 * (c + view(l, 1))
        north = 0.5 * (c + view(l, -1))
        below = 4.0 * c if l == 0 else prev
        above = 4.0 * (c + view(l + 1, 0)) if l < 7 else 4.0 * c
        fz[l, row(r), :] = above
        fr[l, row(r), :] = south
        fc[l, row(r), :] = jnp.where(end, 0.0, fe)
        rows_, cols_, both = north + south, fe + fw, below + above
        if l == 0:
            both = both + drag
        for k, (rw, cw) in enumerate(((4.0, 1.0), (1.0, 4.0))):
            diag = both + rw * rows_ + cw * cols_
            inv[k, l, row(r), :] = jnp.where(m, 0.7 / diag, 0.0)
        prev = above


def coef_kernel(sc, t1, t2, visc, other, fric, mask, bvel, svel, fz, fr, fc, inv, wgt, svm, msk, drg, v, bv):
    own, _ = place(sc)
    for i in range(4):
        for src, at in ((visc, own * 4 + i), (other, (1 - own) * 4 + i)):
            for h in range(0, ROWS, 16):
                spread(v.at[at], h * 8, src[i, h : h + 16, :].astype(F32))
    for h in range(0, ROWS, 16):
        spread(msk, h * 8, mask[h : h + 16, :].astype(F32))
        spread(drg, h * 8, fric[h : h + 16, :])
        spread(svm, h * 8, svel[own, h : h + 16, :])
        for c in range(2):
            spread(bv.at[c], h * 8, bvel[c, h : h + 16, :])

    def step(r, carry):
        m, d = msk[row(r), :], drg[row(r), :]
        coefficient_row(lambda l, j: v[l, row(r + j), :], m > 0.5, d, r + 2, fz, fr, fc, inv)
        svm[row(r), :] = svm[row(r), :] * m
        for c in range(2):
            wgt[c, row(r), :] = (-m * d) * bv[c, row(r), :]
        return carry

    lax.fori_loop(1, ROWS - 1, step, 0)
    for r in (0, ROWS - 1):
        m, d = msk[row(r), :], drg[row(r), :]
        svm[row(r), :] = svm[row(r), :] * m
        for c in range(2):
            wgt[c, row(r), :] = (-m * d) * bv[c, row(r), :]


def coefficients(sc, t1, t2, visc, other, fric, mask, bvel, svel):
    return pl.pallas_call(
        coef_kernel,
        in_specs=[sm()] * 3 + [vm()] * 6,
        out_specs=[vm()] * 9,
        out_shape=[
            kept(*FIELD),
            kept(*FIELD),
            kept(*FIELD),
            kept(2, *FIELD),
            kept(2, *STRIP),
            kept(*STRIP),
            kept(*STRIP),
            kept(*STRIP),
            kept(8, *STRIP),
        ],
        scratch_shapes=[pltpu.VMEM((2, *STRIP), F32)],
        compiler_params=pltpu.CompilerParams(vmem_limit_bytes=24 * MIB),
    )(sc, t1, t2, visc, near(other), fric, mask, bvel, svel)


def ghost_kernel(sc, ea, eb, ea2, eb2, msk, drg, v, fz0, fr0, fc0, inv0, fz, fr, fc, inv, g, u):
    own, odd = place(sc)
    for kind, pair in enumerate(((ea, ea2), (eb, eb2))):
        side = jnp.where((odd + kind) % 2 == 1, 0, 1)
        for who, e in enumerate(pair):
            spread(g.at[side, who], 0, e[...].astype(F32))
    for side in range(2):
        at = 0 if side == 0 else 2
        for who in range(2):
            base = (own if who == 0 else 1 - own) * 4
            for i in range(4):
                for r in range(3):
                    u[side, base + i, row(at + r), :] = g[side, who, pl.ds((i * 3 + r) * 8, 8), :]
        for l in range(8):
            for r in range(2):
                strip_row = r if side == 0 else ROWS - 2 + r
                u[side, l, row(3 * (1 - side) + r), :] = v[l, row(strip_row), :]
        for j in range(3):
            if side == 0:
                r, ghost, inside = j, j, 0
            else:
                r, ghost, inside = ROWS + 1 + j, j - 1, ROWS - 1
            if (side == 0 and j == 2) or (side == 1 and j == 0):
                m, d = msk[row(inside), :], drg[row(inside), :]
            else:
                m, d = g[side, 0, pl.ds((12 + ghost) * 8, 8), :], g[side, 0, pl.ds((14 + ghost) * 8, 8), :]
            coefficient_row(lambda l, s: u[side, l, row(j + 1 + s), :], m > 0.5, d, r, fz, fr, fc, inv)


def ghosts(sc, ea, eb, ea2, eb2, msk, drg, v, fz, fr, fc, inv):
    return pl.pallas_call(
        ghost_kernel,
        in_specs=[sm()] + [vm()] * 11,
        out_specs=[vm()] * 4,
        out_shape=[kept(*FIELD), kept(*FIELD), kept(*FIELD), kept(2, *FIELD)],
        scratch_shapes=[pltpu.VMEM((2, 2, 128, 128), F32), pltpu.VMEM((2, 8, 40, 128), F32)],
        input_output_aliases={8: 0, 9: 1, 10: 2, 11: 3},
        compiler_params=pltpu.CompilerParams(vmem_limit_bytes=24 * MIB),
    )(sc, *(near(x) for x in (ea, eb, ea2, eb2, msk, drg, v, fz, fr, fc, inv)))


def misfit_kernel(sc, got, svm, msk, m_out, ea, eb, hot, rhs, pc):
    _, odd = place(sc)
    p = lax.broadcasted_iota(jnp.int32, (512, 128), 0)
    pc[...] = code_of(p).astype(F32)
    lane = lax.broadcasted_iota(jnp.int32, (8, 128), 1)
    for b in range(32):
        for h in range(2):
            rhs[pl.ds(b * 128 + h * 64, 64), pl.ds(0, 128)] = got[2 * b + h, pl.ds(0, 64), :]
        c = jnp.where(
            lane < 64, got[2 * b, pl.ds(64, 8), :].astype(F32), got[2 * b + 1, pl.ds(64, 8), :].astype(F32)
        )
        same = pc[...].reshape(64, 8, 128) == c[None]
        hot[:, pl.ds(b * 128, 128)] = jnp.where(same, 1.0, 0.0).reshape(512, 128).astype(BF16)
    rhs[:, pl.ds(128, 128)] = jnp.ones((4096, 128), BF16)
    sums = jnp.dot(hot[...], rhs[...], preferred_element_type=F32)
    m_out[...] = sums[:, 128:] * svm[...] - msk[...] * sums[:, :128]
    for kind, e in enumerate((ea, eb)):
        at = jnp.where((odd + kind) % 2 == 0, ROWS - 2, 0)
        for r in range(2):
            e[pl.ds(r * 8, 8), :] = m_out[row(at + r), :]


def misfit(sc, got, svm, msk):
    return pl.pallas_call(
        misfit_kernel,
        in_specs=[sm()] + [vm()] * 3,
        out_specs=[vm()] * 3,
        out_shape=[kept(*STRIP), kept(16, 128), kept(16, 128)],
        scratch_shapes=[
            pltpu.VMEM((512, 4096), BF16),
            pltpu.VMEM((4096, 256), BF16),
            pltpu.VMEM((512, 128), F32),
        ],
        compiler_params=pltpu.CompilerParams(vmem_limit_bytes=24 * MIB),
    )(sc, near(got), near(svm), near(msk))


class Sweeps:
    def __init__(self, sc, t1, t2, c, coefs, a1, a2, a3, acc):
        self.own, self.odd = place(sc)
        self.c = c
        self.fz, self.fr, self.fc, self.inv, self.wgt = coefs
        self.a1, self.a2, self.a3, self.acc = a1, a2, a3, acc
        mine = [jnp.where(self.own == l // 4, t1[l % 4], t2[l % 4]) for l in range(8)]
        self.thick = mine
        self.rw = jnp.where(c == 0, 4.0, 1.0)
        self.cw = jnp.where(c == 0, 1.0, 4.0)
        lane, _ = lanes()
        self.last, self.first_lane = lane == 127, lane == 0

    def neighbours(self, a, l, r, x):
        here = row(r)
        n = None
        if l < 7:
            n = self.fz[l, here, :] * a[l + 1, here, :]
        if l > 0:
            t = self.fz[l - 1, here, :] * a[l - 1, here, :]
            n = t if n is None else n + t
        rows_ = self.fr[l, here, :] * a[l, row(r + 1), :] + self.fr[l, row(r - 1), :] * a[l, row(r - 1), :]
        f = self.fc[l, here, :]
        cols_ = f * east(x, self.last) + west(f * x, self.first_lane)
        return self.inv[self.c, l, here, :] * (n + self.rw * rows_ + self.cw * cols_)

    def first(self, r, m):
        for l in range(8):
            self.a1[l, row(r), :] = self.inv[self.c, l, row(r), :] * (self.thick[l] * m)

    def second(self, r):
        for l in range(8):
            x = self.a1[l, row(r), :]
            self.a2[l, row(r), :] = 1.3 * x + self.neighbours(self.a1, l, r, x)

    def third(self, r):
        total = None
        for l in range(8):
            x = self.a2[l, row(r), :]
            y = 0.3 * x + (self.a1[l, row(r), :] + self.neighbours(self.a2, l, r, x))
            self.a3[l, row(r - 2), :] = y
            total = self.thick[l] * y if l == 0 else total + self.thick[l] * y
        self.acc[row(r - 2), :] = self.wgt[self.c, row(r - 2), :] * total

    def interior(self, m):
        def load(r):
            return m[row(r - 2), :]

        for r in (2, 3, 4):
            self.first(r, load(r))
        for r in (3, 4, 5):
            self.second(r)
            self.first(r + 2, load(r + 2))

        def step(r, carry):
            self.third(r - 2)
            self.second(r)
            self.first(r + 2, load(r + 2))
            return carry

        lax.fori_loop(6, 64, step, 0)
        self.third(62)
        self.second(64)
        self.third(63)

    def edges(self, ga, gb):
        up = jnp.where(self.odd == 1, ga[...], gb[...])
        down = jnp.where(self.odd == 1, gb[...], ga[...])
        for ghost, firsts, seconds, thirds in (
            (up, (0, 1), (1, 2), (2, 3)),
            (down, (66, 67), (65, 66), (64, 65)),
        ):
            for i, r in enumerate(firsts):
                self.first(r, ghost[i * 8 : i * 8 + 8, :])
            for r in seconds:
                self.second(r)
            for r in thirds:
                self.third(r)


def gather_rows(dst, src):
    for h in range(0, ROWS, 8):
        for k in range(8):
            dst[pl.ds(h, 8), pl.ds(k * 128, 128)] = src[pl.ds(h * 8 + k, 8, stride=8), :]


def own_kernel(sc, t1, t2, m, fz, fr, fc, inv, wgt, a1, a2, a3, acc):
    own, _ = place(sc)
    Sweeps(sc, t1, t2, own, (fz, fr, fc, inv, wgt), a1, a2, a3, acc).interior(m)


STATE = (FIELD, FIELD, (8, *STRIP), STRIP)


def own_sweeps(sc, t1, t2, m, coefs):
    return pl.pallas_call(
        own_kernel,
        in_specs=[sm()] * 3 + [vm()] * 6,
        out_specs=[vm()] * 4,
        out_shape=[kept(*s) for s in STATE],
        compiler_params=pltpu.CompilerParams(vmem_limit_bytes=24 * MIB),
    )(sc, t1, t2, near(m), *(near(x) for x in coefs))


def both_kernel(sc, t1, t2, ga, gb, m, fz, fr, fc, inv, wgt, *refs):
    (_, _, _, _), (b1, b2, b3, bacc, a1, a2, a3, acc, adj), (stage, sem) = refs[:4], refs[4:13], refs[13:]
    own, _ = place(sc)
    coefs = (fz, fr, fc, inv, wgt)
    Sweeps(sc, t1, t2, own, coefs, b1, b2, b3, bacc).edges(ga, gb)
    for i in range(4):
        gather_rows(stage.at[i], b3.at[own * 4 + i])
    copy = pltpu.make_async_copy(stage, adj.at[own], sem)
    copy.start()
    Sweeps(sc, t1, t2, 1 - own, coefs, a1, a2, a3, acc).interior(m)
    copy.wait()


def both_sweeps(sc, t1, t2, ga, gb, m, coefs, state):
    return pl.pallas_call(
        both_kernel,
        in_specs=[sm()] * 3 + [vm()] * 12,
        out_specs=[vm()] * 8 + [hbm()],
        out_shape=[kept(*s) for s in STATE] * 2 + [jax.ShapeDtypeStruct((2, 4, ROWS, 1024), F32)],
        scratch_shapes=[pltpu.VMEM((4, ROWS, 1024), F32), pltpu.SemaphoreType.DMA],
        input_output_aliases={11: 0, 12: 1, 13: 2, 14: 3},
        compiler_params=pltpu.CompilerParams(vmem_limit_bytes=24 * MIB),
    )(sc, t1, t2, near(ga), near(gb), near(m), *(near(x) for x in coefs), *(near(x) for x in state))


def last_kernel(sc, t1, t2, g, racc, fz, fr, fc, inv, wgt, *refs):
    (_, _, _, _, _), (a1, a2, a3, acc, adj, grad), (stage, sem) = refs[:5], refs[5:11], refs[11:]
    own, _ = place(sc)
    Sweeps(sc, t1, t2, 1 - own, (fz, fr, fc, inv, wgt), a1, a2, a3, acc).edges(
        g.at[pl.ds(0, 16), :], g.at[pl.ds(16, 16), :]
    )
    for i in range(4):
        gather_rows(stage.at[i], a3.at[own * 4 + i])
    copy = pltpu.make_async_copy(stage, adj.at[1 - own], sem)
    copy.start()
    acc[...] = acc[...] + racc[...]
    gather_rows(grad, acc)
    copy.wait()


def last_sweeps(sc, t1, t2, g, racc, coefs, state, adj):
    return pl.pallas_call(
        last_kernel,
        in_specs=[sm()] * 3 + [vm()] * 11 + [hbm()],
        out_specs=[vm()] * 4 + [hbm(), vm()],
        out_shape=[kept(*s) for s in STATE]
        + [jax.ShapeDtypeStruct((2, 4, ROWS, 1024), F32), jax.ShapeDtypeStruct((ROWS, 1024), F32)],
        scratch_shapes=[pltpu.VMEM((4, ROWS, 1024), F32), pltpu.SemaphoreType.DMA],
        input_output_aliases={10: 0, 11: 1, 12: 2, 13: 3, 14: 4},
        compiler_params=pltpu.CompilerParams(vmem_limit_bytes=24 * MIB),
    )(sc, t1, t2, near(g), near(racc), *(near(x) for x in coefs), *(near(x) for x in state), adj)[4:]


def swaps(tiles, offset, across):
    perm = []
    for t in range(offset, tiles - 1, 2):
        for layer in range(2):
            a, b = t * 2 + layer, (t + 1) * 2 + (1 - layer if across else layer)
            perm += [(a, b), (b, a)]
    return perm


def swap_layers(x):
    return lax.ppermute(x, "layer", [(0, 1), (1, 0)])


def body(viscosity, friction, base_vel, surf_vel, layer_thick, ice_mask, obs_slots, obs_target):
    tiles = lax.axis_size("tile")
    own = lax.axis_index("layer")
    odd = lax.axis_index("tile") % 2
    sc = (own + 2 * odd).astype(jnp.int32).reshape(1)

    def swap(x, kind, across=False):
        return lax.ppermute(x, PAIR, swaps(tiles, kind, across))

    other = swap_layers(viscosity.astype(BF16))
    payload = pack(sc, obs_slots.reshape(tiles, 128, 128), obs_target)
    got = lax.all_to_all(payload, "tile", split_axis=0, concat_axis=0, tiled=True)
    thick_other = swap_layers(layer_thick)

    def edge(at):
        return jnp.concatenate(
            [
                lax.slice_in_dim(viscosity, (ROWS - 3) if at else 0, ROWS if at else 3, axis=1).reshape(12, 1024),
                lax.slice_in_dim(ice_mask, (ROWS - 2) if at else 0, ROWS if at else 2, axis=0).astype(F32),
                lax.slice_in_dim(friction, (ROWS - 2) if at else 0, ROWS if at else 2, axis=0),
            ]
        ).astype(BF16)

    top, bottom = edge(0), edge(1)
    to_a = jnp.where(odd == 0, bottom, top)
    to_b = jnp.where(odd == 0, top, bottom)
    near_rows = (swap(to_a, 0), swap(to_b, 1), swap(to_a, 0, True), swap(to_b, 1, True))
    fz, fr, fc, inv, wgt, svm, msk, drg, v = coefficients(
        sc, layer_thick, thick_other, viscosity, other, friction, ice_mask, base_vel, surf_vel
    )
    fz, fr, fc, inv = ghosts(sc, *near_rows, msk, drg, v, fz, fr, fc, inv)
    coefs = (fz, fr, fc, inv, wgt)

    m_own, ea, eb = misfit(sc, got, svm, msk)
    ga, gb = swap(ea, 0), swap(eb, 1)
    m_oth = swap_layers(m_own)
    state = own_sweeps(sc, layer_thick, thick_other, m_own, coefs)
    g_oth = swap_layers(jnp.concatenate([ga, gb]))
    *both, adj = both_sweeps(sc, layer_thick, thick_other, ga, gb, m_oth, coefs, state)
    adjoint, gradient = last_sweeps(sc, layer_thick, thick_other, g_oth, both[3], coefs, both[4:], adj)
    return adjoint, gradient


def solution(mesh):
    in_specs = (
        P("layer", "tile", None),
        P("tile", None),
        P(None, "tile", None),
        P(None, "tile", None),
        P("layer"),
        P("tile", None),
        P("tile", None, None, None),
        P("tile", None),
    )
    out_specs = (P(None, "layer", "tile", None), P("tile", None))
    return jax.shard_map(body, mesh=mesh, in_specs=in_specs, out_specs=out_specs, check_vma=False)
```

time: 107 us -> 129 us (1.21)
  local copies, waits for them, and re-layouts: 3.34 us -> 33.8 us
  Pallas kernels: 54.3 us -> 33.4 us
  waiting for transfers between devices: 13.1 us -> 25.1 us
  starting transfers between devices: 30.9 us -> 32.9 us
  other arithmetic: 4.02 us -> 2.17 us
    unnamed x14 -> x56, local copies, waits for them, and re-layouts: 2.52 us -> 29.1 us
    pallas_call x4 -> x7, Pallas kernels: 54.3 us -> 33.4 us  [the longest x1 8.12 us: both_sweeps(): pl.pallas_call(both_kernel, in_specs=[sm()] * 3 + [vm()] * 12, out_specs=...]
    ppermute x4, waiting for transfers between devices: 1.1 us -> 21.9 us  [swap_layers(): return lax.ppermute(x, 'layer', [(0, 1), (1, 0)])]
    ppermute x6, waiting for transfers between devices: 12 us -> 3.14 us  [swap(): return lax.ppermute(x, PAIR, swaps(tiles, kind, across))]
    ppermute x6, starting transfers between devices: 14.9 us -> 18 us  [swap(): return lax.ppermute(x, PAIR, swaps(tiles, kind, across))]
    reshape x2, local copies, waits for them, and re-layouts: 0.06 us -> 2.78 us  [edge(): lax.slice_in_dim(viscosity, ROWS - 3 if at else 0, ROWS if at else 3, axi...]
    ppermute x4, starting transfers between devices: 4.88 us -> 3.21 us  [swap_layers(): return lax.ppermute(x, 'layer', [(0, 1), (1, 0)])]
    slice x1, local copies, waits for them, and re-layouts: 0.01 us -> 1.34 us  [edge(): lax.slice_in_dim(friction, ROWS - 2 if at else 0, ROWS if at else 2, axis=0)]
  transfers between devices with their start and end apart: 11 -> 11, of which waited for: 4 -> 2; matrix products, arithmetic and copies ran while one was open for 3% -> 5% of each run, Pallas kernels for 17% -> 19%
where the time goes in v2:
time: 129 us; the launch traced here: 128 us
  local copies, waits for them, and re-layouts  33.8 us (26%)
  Pallas kernels  33.4 us (26%)
  starting transfers between devices  32.9 us (26%)
  waiting for transfers between devices  25.1 us (19%)
  other arithmetic  2.17 us (2%)
    unnamed x56, local copies, waits for them, and re-layouts  29.1 us
    ppermute x4, waiting for transfers between devices, swap_layers(): return lax.ppermute(x, 'layer', [(0, 1), (1, 0)])  21.9 us
    ppermute x6, starting transfers between devices, swap(): return lax.ppermute(x, PAIR, swaps(tiles, kind, across))  18 us
    all_to_all x1, starting transfers between devices, body(): lax.all_to_all(payload, 'tile', split_axis=0, concat_axis=0, tiled=True)  11.6 us
    pallas_call x1, Pallas kernels, both_sweeps(): pl.pallas_call(both_kernel, in_specs=[sm()] * 3 + [vm()] * 12, out_specs=...  8.12 us
    pallas_call x1, Pallas kernels, own_sweeps(): pl.pallas_call(own_kernel, in_specs=[sm()] * 3 + [vm()] * 6, out_specs=[v...  8.04 us
    pallas_call x1, Pallas kernels, coefficients(): pl.pallas_call(coef_kernel, in_specs=[sm()] * 3 + [vm()] * 6, out_specs=[...  7.36 us
    pallas_call x1, Pallas kernels, misfit(): pl.pallas_call(misfit_kernel, in_specs=[sm()] + [vm()] * 3, out_specs=[vm...  3.63 us
  transfers between devices with their start and end apart: 11, of which 2 were waited for; matrix products, arithmetic and copies ran while one was open for 5% of the time, Pallas kernels for 19%

profile of v2, /device:TPU:2, one launch (start us, length us, event | category | flops | bytes accessed | tf_op | source)
XLA Modules:
  0.0 128.3 jit_solution(15831511064143296791)
XLA Ops:
  0.7 1.6 %copy-done.14 = bf16[64,64,2,128]{3,2,1,0:T(2,128)(2,1)S(1)} copy-done((bf16[64,64,2,128]{3,2,1,0:T(2,128)(2,1)S(1)}, bf16[64,64,2,128]{3,2,1,0:T(2,128)(2,1)}, u32[]{:S(2)}) %copy-start.14) | copy-done | bytes 2097176
  3.0 3.3 %shard_map.95 = bf16[64,72,128]{2,1,0:T(8,128)(2,1)} custom-call(s32[1]{0:T(128)} %bitcast.sc, bf16[64,128,128]{2,1,0:T(8,128)(2,1)S(1)} %bitcast.2, s32[64,64]{1,0:T(8,128)S(1)} %copy-done.25), custom_call_target="tpu_custom_call" | custom-call | tf_op jit(solution)/shard_map/pallas_call | solution.py:79
  6.3 11.6 %all-to-all-start = ((bf16[64,72,128]{2,1,0:T(8,128)(2,1)}), bf16[64,72,128]{2,1,0:T(8,128)(2,1)}, u32[]{:S(2)}, u32[]{:S(2)}) async-start(bf16[64,72,128]{2,1,0:T(8,128)(2,1)} %shard_map.95), calls=%async_computation | async-start | bytes 2359296 | tf_op jit(solution)/shard_map/all_to_all | solution.py:435
  18.0 1.1 collective-permute-start.1
  22.1 21.9 %collective-permute-done.t2 = f32[4]{0:T(128)S(1)} collective-permute-done((f32[4]{0:T(128)S(1)}, f32[4]{0:T(128)S(1)}, u32[]{:S(2)}, u32[]{:S(2)}) %collective-permute-start) | collective-permute-done | bytes 48 | tf_op jit(solution)/shard_map/ppermute | solution.py:421
  44.0 7.4 %shard_map.96 = (f32[8,544,128]{2,1,0:T(8,128)S(1)}, f32[8,544,128]{2,1,0:T(8,128)S(1)}, f32[8,544,128]{2,1,0:T(8,128)S(1)}, f32[2,8,544,128]{3,2,1,0:T(8,128)S(...) custom-call(s32[1]{0:T(128)} %bitcast.sc, ...), custom_call_target="tpu_custom_call" | custom-call | tf_op jit(solution)/shard_map/pallas_call | solution.py:156
  51.4 2.1 %copy-done = f32[2,8,544,128]{3,2,1,0:T(8,128)} copy-done((f32[2,8,544,128]{3,2,1,0:T(8,128)}, f32[2,8,544,128]{3,2,1,0:T(8,128)S(1)}, u32[]{:S(2)}) %copy-start) | copy-done | bytes 4456472
  53.5 1.4 %copy-done.4 = f32[8,544,128]{2,1,0:T(8,128)} copy-done((f32[8,544,128]{2,1,0:T(8,128)}, f32[8,544,128]{2,1,0:T(8,128)S(1)}, u32[]{:S(2)}) %copy-start.4) | copy-done | bytes 2228248
  54.8 1.4 %copy-done.8 = f32[8,544,128]{2,1,0:T(8,128)} copy-done((f32[8,544,128]{2,1,0:T(8,128)}, f32[8,544,128]{2,1,0:T(8,128)S(1)}, u32[]{:S(2)}) %copy-start.8) | copy-done | bytes 2228248
  56.3 1.3 %copy-done.15 = f32[8,512,128]{2,1,0:T(8,128)} copy-done((f32[8,512,128]{2,1,0:T(8,128)}, f32[8,512,128]{2,1,0:T(8,128)S(1)}, u32[]{:S(2)}) %copy-start.15) | copy-done | bytes 2097176
  60.0 3.6 %shard_map.97 = (f32[512,128]{1,0:T(8,128)}, f32[16,128]{1,0:T(8,128)S(1)}, f32[16,128]{1,0:T(8,128)S(1)}) custom-call(s32[1]{0:T(128)} %bitcast.sc, bf16[64,72,128]{2,1,0:T(8,128)(2,1)} %all-to-all-done.got, f32[512,128]{1,0:T(8,128)S(1)} %copy-done.24, f32[512,128]{1,0:T(8,128)S(1)} %get-tuple-element.31.msk), custom_call_target="tpu_custom_call" | custom-call | tf_op jit(solution)/shard_map/pallas_call | solution.py:240
  65.2 1.3 %fusion.1 = (bf16[2,1024]{1,0:T(2,128)(2,1)}, bf16[2,1024]{1,0:T(2,128)(2,1)}) fusion(bf16[64,1024]{1,0:T(8,128)(2,1)} %convert.19), kind=kLoop, calls=%fused_computation.8 | loop fusion | bytes 16384 | tf_op jit(solution)/shard_map/slice | solution.py:443
  66.6 1.4 %reshape.20 = bf16[12,1024]{1,0:T(8,128)(2,1)} reshape(bf16[4,3,1024]{2,1,0:T(4,128)(2,1)} %get-tuple-element.58) | data formatting | bytes 49152 | tf_op jit(solution)/shard_map/reshape | solution.py:441
  68.0 1.4 %reshape.21 = bf16[12,1024]{1,0:T(8,128)(2,1)} reshape(bf16[4,3,1024]{2,1,0:T(4,128)(2,1)} %get-tuple-element.59) | data formatting | bytes 49152 | tf_op jit(solution)/shard_map/reshape | solution.py:441
  69.3 6.6 %collective-permute-start.3 = (f32[16,128]{1,0:T(8,128)S(1)}, f32[16,128]{1,0:T(8,128)S(1)}, u32[]{:S(2)}, u32[]{:S(2)}) collective-permute-start(f32[16,128]{1,0:T(8,128)S(1)} %get-tuple-element.33), channel_id=1, source_target_pairs={{2,4},{4,2},{3,5},{5,3},{6,8},{8,6},{7,9},{9,7},{10,12},{12,10},{1... | collective-permute-start | bytes 24584 | tf_op jit(solution)/shard_map/ppermute | solution.py:431
  76.9 1.1 collective-permute-start.8
  78.0 4.0 %collective-permute-start.7 = (bf16[16,1024]{1,0:T(8,128)(2,1)S(1)}, bf16[16,1024]{1,0:T(8,128)(2,1)S(1)}, u32[]{:S(2)}, u32[]{:S(2)}) collective-permute-start(bf16[16,1024]{1,0:T(8,128)(2,1)S(1)} %get-tuple-element.64), channel_id=1, source_target_pairs={{2,4},{4,2},{3,5},{5,3},{6,8},{8,6},{7,9},{9,7},{10,12},{12,10},{1... | collective-permute-start | bytes 98312 | tf_op jit(solution)/shard_map/ppermute | solution.py:431
  82.1 6.2 %collective-permute-start.9 = (bf16[16,1024]{1,0:T(8,128)(2,1)S(1)}, bf16[16,1024]{1,0:T(8,128)(2,1)S(1)}, u32[]{:S(2)}, u32[]{:S(2)}) collective-permute-start(bf16[16,1024]{1,0:T(8,128)(2,1)S(1)} %get-tuple-element.64), channel_id=1, source_target_pairs={{2,5},{5,2},{3,4},{4,3},{6,9},{9,6},{7,8},{8,7},{10,13},{13,10},{1... | collective-permute-start | bytes 98312 | tf_op jit(solution)/shard_map/ppermute | solution.py:431
  88.4 3.1 %collective-permute-done.9.eb2 = bf16[16,1024]{1,0:T(8,128)(2,1)S(1)} collective-permute-done((bf16[16,1024]{1,0:T(8,128)(2,1)S(1)}, bf16[16,1024]{1,0:T(8,128)(2,1)S(1)}, u32[]{:S(2)}, u32[]{:S(2)}) %collective-permute-start.9) | collective-permute-done | bytes 32800 | tf_op jit(solution)/shard_map/ppermute | solution.py:431
  91.5 2.3 %copy-done.1 = f32[2,8,544,128]{3,2,1,0:T(8,128)S(1)} copy-done((f32[2,8,544,128]{3,2,1,0:T(8,128)S(1)}, f32[2,8,544,128]{3,2,1,0:T(8,128)}, u32[]{:S(2)}) %copy-start.1) | copy-done | bytes 4456472
  93.8 1.6 %copy-done.5 = f32[8,544,128]{2,1,0:T(8,128)S(1)} copy-done((f32[8,544,128]{2,1,0:T(8,128)S(1)}, f32[8,544,128]{2,1,0:T(8,128)}, u32[]{:S(2)}) %copy-start.5) | copy-done | bytes 2228248
  95.4 1.6 %copy-done.9 = f32[8,544,128]{2,1,0:T(8,128)S(1)} copy-done((f32[8,544,128]{2,1,0:T(8,128)S(1)}, f32[8,544,128]{2,1,0:T(8,128)}, u32[]{:S(2)}) %copy-start.9) | copy-done | bytes 2228248
  97.0 1.6 %copy-done.16 = f32[8,512,128]{2,1,0:T(8,128)S(1)} copy-done((f32[8,512,128]{2,1,0:T(8,128)S(1)}, f32[8,512,128]{2,1,0:T(8,128)}, u32[]{:S(2)}) %copy-start.16) | copy-done | bytes 2097176
  99.0 2.1 %copy-done.2 = f32[2,8,544,128]{3,2,1,0:T(8,128)} copy-done((f32[2,8,544,128]{3,2,1,0:T(8,128)}, f32[2,8,544,128]{3,2,1,0:T(8,128)S(1)}, u32[]{:S(2)}) %copy-start.2) | copy-done | bytes 4456472
  101.0 1.4 %copy-done.6 = f32[8,544,128]{2,1,0:T(8,128)} copy-done((f32[8,544,128]{2,1,0:T(8,128)}, f32[8,544,128]{2,1,0:T(8,128)S(1)}, u32[]{:S(2)}) %copy-start.6) | copy-done | bytes 2228248
  102.4 1.4 %copy-done.10 = f32[8,544,128]{2,1,0:T(8,128)} copy-done((f32[8,544,128]{2,1,0:T(8,128)}, f32[8,544,128]{2,1,0:T(8,128)S(1)}, u32[]{:S(2)}) %copy-start.10) | copy-done | bytes 2228248
  103.8 2.3 %copy-done.3 = f32[2,8,544,128]{3,2,1,0:T(8,128)S(1)} copy-done((f32[2,8,544,128]{3,2,1,0:T(8,128)S(1)}, f32[2,8,544,128]{3,2,1,0:T(8,128)}, u32[]{:S(2)}) %copy-start.3) | copy-done | bytes 4456472
  106.1 1.6 %copy-done.7 = f32[8,544,128]{2,1,0:T(8,128)S(1)} copy-done((f32[8,544,128]{2,1,0:T(8,128)S(1)}, f32[8,544,128]{2,1,0:T(8,128)}, u32[]{:S(2)}) %copy-start.7) | copy-done | bytes 2228248
  107.7 1.6 %copy-done.11 = f32[8,544,128]{2,1,0:T(8,128)S(1)} copy-done((f32[8,544,128]{2,1,0:T(8,128)S(1)}, f32[8,544,128]{2,1,0:T(8,128)}, u32[]{:S(2)}) %copy-start.11) | copy-done | bytes 2228248
  109.3 8.0 %shard_map.99 = (f32[8,544,128]{2,1,0:T(8,128)S(1)}, f32[8,544,128]{2,1,0:T(8,128)S(1)}, f32[8,512,128]{2,1,0:T(8,128)S(1)}, f32[512,128]{1,0:T(8,128)S(1)}) custom-call(s32[1]{0:T(128)} %bitcast.sc, f32[4]{0:T(128)S(1)} %copy-done.26, f32[4]{0:T(128)S(1)} %collective-permute-done.t2, f32[512,128]{1,0:T(8,128)} %get-tuple-element.34.m, ...), custom_call_target="tpu_custom_call" | custom-call | tf_op jit(solution)/shard_map/pallas_call | solution.py:349
  117.4 8.1 %shard_map.100 = (f32[8,544,128]{2,1,0:T(8,128)S(1)}, f32[8,544,128]{2,1,0:T(8,128)S(1)}, f32[8,512,128]{2,1,0:T(8,128)S(1)}, f32[512,128]{1,0:T(8,128)S(1)}, f3...) custom-call(s32[1]{0:T(128)} %bitcast.sc, ...), custom_call_target="tpu_custom_call", output_to_operand_aliasing={{0}: (11, {}), {1}: (12, {}), {2}: (13, {}), {3}: (14, {})} | custom-call | tf_op jit(solution)/shard_map/pallas_call | solution.py:372
  125.5 2.7 %shard_map.101 = (f32[8,544,128]{2,1,0:T(8,128)S(1)}, f32[8,544,128]{2,1,0:T(8,128)S(1)}, f32[8,512,128]{2,1,0:T(8,128)S(1)}, f32[512,128]{1,0:T(8,128)S(1)}, f3...) custom-call(s32[1]{0:T(128)} %bitcast.sc, ...), custom_call_target="tpu_custom_call", output_to_operand_aliasing={{0}: (10, {}), {1}: (11, {}), {2}: (12, {}), {3}: (13, {}),... | custom-call | tf_op jit(solution)/shard_map/pallas_call | solution.py:399
  (62 shorter events, 9.2 us)
Async XLA Ops:
  0.6 1.6 %copy-start.14 = (bf16[64,64,2,128]{3,2,1,0:T(2,128)(2,1)S(1)}, bf16[64,64,2,128]{3,2,1,0:T(2,128)(2,1)}, u32[]{:S(2)}) copy-start(bf16[64,64,2,128]{3,2,1,0:T(2,128)(2,1)} %param.14) | copy-start | bytes 6291460
  3.0 14.9 %copy-start.12 = (f32[4,64,1024]{2,1,0:T(8,128)S(1)}, f32[4,64,1024]{2,1,0:T(8,128)}, u32[]{:S(2)}) copy-start(f32[4,64,1024]{2,1,0:T(8,128)} %visc.1) | copy-start | bytes 3145732
  6.2 12.9 %copy-start.26 = (f32[4]{0:T(128)S(1)}, f32[4]{0:T(128)}, u32[]{:S(2)}) copy-start(f32[4]{0:T(128)} %t1.7) | copy-start | bytes 52
  6.3 13.9 %copy-start.17 = (f32[64,1024]{1,0:T(8,128)S(1)}, f32[64,1024]{1,0:T(8,128)}, u32[]{:S(2)}) copy-start(f32[64,1024]{1,0:T(8,128)} %fric.1) | copy-start | bytes 786436
  6.3 14.5 %copy-start.20 = (s32[64,1024]{1,0:T(8,128)S(1)}, s32[64,1024]{1,0:T(8,128)}, u32[]{:S(2)}) copy-start(s32[64,1024]{1,0:T(8,128)} %mask.1) | copy-start | bytes 786436
  6.3 52.7 %all-to-all-start = ((bf16[64,72,128]{2,1,0:T(8,128)(2,1)}), bf16[64,72,128]{2,1,0:T(8,128)(2,1)}, u32[]{:S(2)}, u32[]{:S(2)}) async-start(bf16[64,72,128]{2,1,0:T(8,128)(2,1)} %shard_map.95), calls=%async_computation | async-start | bytes 2359296 | tf_op jit(solution)/shard_map/all_to_all | solution.py:435
  17.9 26.1 %copy-start.13 = (f32[4,64,1024]{2,1,0:T(8,128)S(1)}, f32[4,64,1024]{2,1,0:T(8,128)}, u32[]{:S(2)}) copy-start(f32[4,64,1024]{2,1,0:T(8,128)} %visc.1) | copy-start | bytes 3145732
  17.9 26.1 %copy-start.18 = (f32[2,64,1024]{2,1,0:T(8,128)S(1)}, f32[2,64,1024]{2,1,0:T(8,128)}, u32[]{:S(2)}) copy-start(f32[2,64,1024]{2,1,0:T(8,128)} %bvel.1) | copy-start | bytes 1572868
  17.9 26.1 %copy-start.19 = (f32[2,64,1024]{2,1,0:T(8,128)S(1)}, f32[2,64,1024]{2,1,0:T(8,128)}, u32[]{:S(2)}) copy-start(f32[2,64,1024]{2,1,0:T(8,128)} %svel.1) | copy-start | bytes 1572868
  18.0 26.0 %collective-permute-start.1 = (bf16[4,64,1024]{2,1,0:T(8,128)(2,1)S(1)}, bf16[4,64,1024]{2,1,0:T(8,128)(2,1)S(1)}, u32[]{:S(2)}, u32[]{:S(2)}) collective-permute-start(bf16[4,64,1024]{2,1,0:T(8,128)(2,1)S(1)} %convert_element_type.11), channel_id=1, source_target_pairs={{0,1},{1,0},{2,3},{3,2},{4,5},{5,4},{6,7},{7,6},{8,9},{9,8},{10,11... | collective-permute-start | bytes 1572872 | tf_op jit(solution)/shard_map/ppermute | solution.py:421
  19.1 24.9 %collective-permute-start = (f32[4]{0:T(128)S(1)}, f32[4]{0:T(128)S(1)}, u32[]{:S(2)}, u32[]{:S(2)}) collective-permute-start(f32[4]{0:T(128)S(1)} %copy-done.26), channel_id=1, source_target_pairs={{0,1},{1,0},{2,3},{3,2},{4,5},{5,4},{6,7},{7,6},{8,9},{9,8},{10,11... | collective-permute-start | bytes 56 | tf_op jit(solution)/shard_map/ppermute | solution.py:421
  51.4 2.1 %copy-start = (f32[2,8,544,128]{3,2,1,0:T(8,128)}, f32[2,8,544,128]{3,2,1,0:T(8,128)S(1)}, u32[]{:S(2)}) copy-start(f32[2,8,544,128]{3,2,1,0:T(8,128)S(1)} %get-tuple-element.40.inv0) | copy-start | bytes 13369348
  53.4 1.4 %copy-start.4 = (f32[8,544,128]{2,1,0:T(8,128)}, f32[8,544,128]{2,1,0:T(8,128)S(1)}, u32[]{:S(2)}) copy-start(f32[8,544,128]{2,1,0:T(8,128)S(1)} %get-tuple-element.38.fr0) | copy-start | bytes 6684676
  54.8 1.4 %copy-start.8 = (f32[8,544,128]{2,1,0:T(8,128)}, f32[8,544,128]{2,1,0:T(8,128)S(1)}, u32[]{:S(2)}) copy-start(f32[8,544,128]{2,1,0:T(8,128)S(1)} %get-tuple-element.39.fc0) | copy-start | bytes 6684676
  59.0 32.5 %copy-start.22 = (f32[512,128]{1,0:T(8,128)S(1)}, f32[512,128]{1,0:T(8,128)}, u32[]{:S(2)}) copy-start(f32[512,128]{1,0:T(8,128)} %copy-done.21) | copy-start | bytes 786436
  64.2 53.2 %collective-permute-start.5 = (f32[512,128]{1,0:T(8,128)}, f32[512,128]{1,0:T(8,128)S(1)}, u32[]{:S(2)}, u32[]{:S(2)}) collective-permute-start(f32[512,128]{1,0:T(8,128)} %get-tuple-element.34.m), channel_id=1, source_target_pairs={{0,1},{1,0},{2,3},{3,2},{4,5},{5,4},{6,7},{7,6},{8,9},{9,8},{10,11... | collective-permute-start | bytes 786440 | tf_op jit(solution)/shard_map/ppermute | solution.py:421
  69.3 8.7 %collective-permute-start.2 = (f32[16,128]{1,0:T(8,128)}, f32[16,128]{1,0:T(8,128)S(1)}, u32[]{:S(2)}, u32[]{:S(2)}) collective-permute-start(f32[16,128]{1,0:T(8,128)} %copy-done.27), channel_id=1, source_target_pairs={{0,2},{2,0},{1,3},{3,1},{4,6},{6,4},{5,7},{7,5},{8,10},{10,8},{9,1... | collective-permute-start | bytes 24584 | tf_op jit(solution)/shard_map/ppermute | solution.py:431
  69.3 12.7 %collective-permute-start.3 = (f32[16,128]{1,0:T(8,128)S(1)}, f32[16,128]{1,0:T(8,128)S(1)}, u32[]{:S(2)}, u32[]{:S(2)}) collective-permute-start(f32[16,128]{1,0:T(8,128)S(1)} %get-tuple-element.33), channel_id=1, source_target_pairs={{2,4},{4,2},{3,5},{5,3},{6,8},{8,6},{7,9},{9,7},{10,12},{12,10},{1... | collective-permute-start | bytes 24584 | tf_op jit(solution)/shard_map/ppermute | solution.py:431
  76.8 11.5 %collective-permute-start.6 = (bf16[16,1024]{1,0:T(8,128)(2,1)S(1)}, bf16[16,1024]{1,0:T(8,128)(2,1)S(1)}, u32[]{:S(2)}, u32[]{:S(2)}) collective-permute-start(bf16[16,1024]{1,0:T(8,128)(2,1)S(1)} %get-tuple-element.65), channel_id=1, source_target_pairs={{0,2},{2,0},{1,3},{3,1},{4,6},{6,4},{5,7},{7,5},{8,10},{10,8},{9,1... | collective-permute-start | bytes 98312 | tf_op jit(solution)/shard_map/ppermute | solution.py:431
  76.9 11.5 %collective-permute-start.8 = (bf16[16,1024]{1,0:T(8,128)(2,1)S(1)}, bf16[16,1024]{1,0:T(8,128)(2,1)S(1)}, u32[]{:S(2)}, u32[]{:S(2)}) collective-permute-start(bf16[16,1024]{1,0:T(8,128)(2,1)S(1)} %get-tuple-element.65), channel_id=1, source_target_pairs={{0,3},{3,0},{1,2},{2,1},{4,7},{7,4},{5,6},{6,5},{8,11},{11,8},{9,1... | collective-permute-start | bytes 98312 | tf_op jit(solution)/shard_map/ppermute | solution.py:431
  78.0 10.4 %collective-permute-start.7 = (bf16[16,1024]{1,0:T(8,128)(2,1)S(1)}, bf16[16,1024]{1,0:T(8,128)(2,1)S(1)}, u32[]{:S(2)}, u32[]{:S(2)}) collective-permute-start(bf16[16,1024]{1,0:T(8,128)(2,1)S(1)} %get-tuple-element.64), channel_id=1, source_target_pairs={{2,4},{4,2},{3,5},{5,3},{6,8},{8,6},{7,9},{9,7},{10,12},{12,10},{1... | collective-permute-start | bytes 98312 | tf_op jit(solution)/shard_map/ppermute | solution.py:431
  82.1 9.5 %collective-permute-start.9 = (bf16[16,1024]{1,0:T(8,128)(2,1)S(1)}, bf16[16,1024]{1,0:T(8,128)(2,1)S(1)}, u32[]{:S(2)}, u32[]{:S(2)}) collective-permute-start(bf16[16,1024]{1,0:T(8,128)(2,1)S(1)} %get-tuple-element.64), channel_id=1, source_target_pairs={{2,5},{5,2},{3,4},{4,3},{6,9},{9,6},{7,8},{8,7},{10,13},{13,10},{1... | collective-permute-start | bytes 98312 | tf_op jit(solution)/shard_map/ppermute | solution.py:431
  88.3 37.2 %collective-permute-start.4 = (f32[32,128]{1,0:T(8,128)S(1)}, f32[32,128]{1,0:T(8,128)S(1)}, u32[]{:S(2)}, u32[]{:S(2)}) collective-permute-start(f32[32,128]{1,0:T(8,128)S(1)} %pad_maximum_fusion.2), channel_id=1, source_target_pairs={{0,1},{1,0},{2,3},{3,2},{4,5},{5,4},{6,7},{7,6},{8,9},{9,8},{10,11... | collective-permute-start | bytes 49160 | tf_op jit(solution)/shard_map/ppermute | solution.py:421
  91.5 2.3 %copy-start.1 = (f32[2,8,544,128]{3,2,1,0:T(8,128)S(1)}, f32[2,8,544,128]{3,2,1,0:T(8,128)}, u32[]{:S(2)}) copy-start(f32[2,8,544,128]{3,2,1,0:T(8,128)} %copy-done) | copy-start | bytes 13369348
  93.8 1.6 %copy-start.5 = (f32[8,544,128]{2,1,0:T(8,128)S(1)}, f32[8,544,128]{2,1,0:T(8,128)}, u32[]{:S(2)}) copy-start(f32[8,544,128]{2,1,0:T(8,128)} %copy-done.4) | copy-start | bytes 6684676
  95.4 1.6 %copy-start.9 = (f32[8,544,128]{2,1,0:T(8,128)S(1)}, f32[8,544,128]{2,1,0:T(8,128)}, u32[]{:S(2)}) copy-start(f32[8,544,128]{2,1,0:T(8,128)} %copy-done.8) | copy-start | bytes 6684676
  97.0 1.6 %copy-start.16 = (f32[8,512,128]{2,1,0:T(8,128)S(1)}, f32[8,512,128]{2,1,0:T(8,128)}, u32[]{:S(2)}) copy-start(f32[8,512,128]{2,1,0:T(8,128)} %copy-done.15) | copy-start | bytes 6291460
  98.9 2.1 %copy-start.2 = (f32[2,8,544,128]{3,2,1,0:T(8,128)}, f32[2,8,544,128]{3,2,1,0:T(8,128)S(1)}, u32[]{:S(2)}) copy-start(f32[2,8,544,128]{3,2,1,0:T(8,128)S(1)} %get-tuple-element.44.inv) | copy-start | bytes 13369348
  102.4 1.4 %copy-start.10 = (f32[8,544,128]{2,1,0:T(8,128)}, f32[8,544,128]{2,1,0:T(8,128)S(1)}, u32[]{:S(2)}) copy-start(f32[8,544,128]{2,1,0:T(8,128)S(1)} %get-tuple-element.43.fc) | copy-start | bytes 6684676
  103.8 2.3 %copy-start.3 = (f32[2,8,544,128]{3,2,1,0:T(8,128)S(1)}, f32[2,8,544,128]{3,2,1,0:T(8,128)}, u32[]{:S(2)}) copy-start(f32[2,8,544,128]{3,2,1,0:T(8,128)} %copy-done.2) | copy-start | bytes 13369348
  106.1 1.6 %copy-start.7 = (f32[8,544,128]{2,1,0:T(8,128)S(1)}, f32[8,544,128]{2,1,0:T(8,128)}, u32[]{:S(2)}) copy-start(f32[8,544,128]{2,1,0:T(8,128)} %copy-done.6) | copy-start | bytes 6684676
  107.7 1.6 %copy-start.11 = (f32[8,544,128]{2,1,0:T(8,128)S(1)}, f32[8,544,128]{2,1,0:T(8,128)}, u32[]{:S(2)}) copy-start(f32[8,544,128]{2,1,0:T(8,128)} %copy-done.10) | copy-start | bytes 6684676
  (7 other events, 6.4 us)

commit v3 on v2

--- a/solution.py
+++ b/solution.py
@@ -4,6 +4,7 @@
 from jax.experimental import pallas as pl
 from jax.experimental.pallas import tpu as pltpu
 from jax.sharding import PartitionSpec as P
+
 
 F32 = jnp.float32
 BF16 = jnp.bfloat16
@@ -24,7 +25,11 @@
 
 
 def hbm():
-    return pl.BlockSpec(memory_space=pl.ANY)
+    return pl.BlockSpec(memory_space=pltpu.HBM)
+
+
+def far(x):
+    return pltpu.with_memory_space_constraint(x, pltpu.HBM)
 
 
 def kept(*shape, dtype=F32):
@@ -63,32 +68,100 @@
     return jnp.where(t < 512, (128 + (t & 127)) << (t >> 7), 0)
 
 
-def pack_kernel(sc, slots, target, o, f, codes):
+def pack_kernel(sc, slots, target, o, x, y, t, f, codes, sin, sout, st):
     own, _ = place(sc)
-    c = code_of(target[...]).astype(F32)
+    n = slots.shape[0]
+    step = n // CHUNKS
+    tin = pltpu.make_async_copy(target, t, st)
+    tin.start()
+    ins = [
+        pltpu.make_async_copy(slots.at[pl.ds(i * step, step)], x.at[pl.ds(i * step, step)], sin.at[i])
+        for i in range(CHUNKS)
+    ]
+    outs = [
+        pltpu.make_async_copy(y.at[pl.ds(i * step, step)], o.at[pl.ds(i * step, step)], sout.at[i])
+        for i in range(CHUNKS)
+    ]
+    for i in ins:
+        i.start()
+    tin.wait()
+    c = code_of(t[...]).astype(F32)
     codes[...] = jnp.concatenate([c, c], axis=1)
-    for d in range(slots.shape[0]):
-        f[d] = slots[d].astype(F32)
-        o[d, pl.ds(0, 64), :] = f[d, pl.ds(own, 64, stride=2), :].astype(BF16)
-        o[d, pl.ds(64, 8), :] = jnp.broadcast_to(codes[pl.ds(d, 1), :], (8, 128)).astype(BF16)
+    for i in range(CHUNKS):
+        ins[i].wait()
+
+        def one(d, carry):
+            f[d] = x[d].astype(F32)
+            y[d, pl.ds(0, 64), :] = f[d, pl.ds(own, 64, stride=2), :].astype(BF16)
+            y[d, pl.ds(64, 8), :] = jnp.broadcast_to(codes[pl.ds(d, 1), :], (8, 128)).astype(BF16)
+            return carry
+
+        lax.fori_loop(i * step, (i + 1) * step, one, 0, unroll=8)
+        outs[i].start()
+    for i in outs:
+        i.wait()
+
+
+CHUNKS = 4
 
 
 def pack(sc, slots, target):
     n = slots.shape[0]
-    step = 8
     return pl.pallas_call(
         pack_kernel,
-        grid=(n // step,),
-        in_specs=[
-            sm(),
-            pl.BlockSpec((step, 128, 128), lambda i: (i, 0, 0)),
-            pl.BlockSpec((step, 64), lambda i: (i, 0)),
+        in_specs=[sm(), hbm(), hbm()],
+        out_specs=hbm(),
+        out_shape=pltpu.HBM((n, 72, 128), BF16),
+        scratch_shapes=[
+            pltpu.VMEM((n, 128, 128), BF16),
+            pltpu.VMEM((n, 72, 128), BF16),
+            pltpu.VMEM((n, 64), jnp.int32),
+            pltpu.VMEM((n, 128, 128), F32),
+            pltpu.VMEM((n, 128), F32),
+            pltpu.SemaphoreType.DMA((CHUNKS,)),
+            pltpu.SemaphoreType.DMA((CHUNKS,)),
+            pltpu.SemaphoreType.DMA,
         ],
-        out_specs=pl.BlockSpec((step, 72, 128), lambda i: (i, 0, 0)),
-        out_shape=jax.ShapeDtypeStruct((n, 72, 128), BF16),
-        scratch_shapes=[pltpu.VMEM((step, 128, 128), F32), pltpu.VMEM((step, 128), F32)],
+        compiler_params=pltpu.CompilerParams(vmem_limit_bytes=16 * MIB),
+    )(sc, far(slots), far(target))
+
+
+def edge_kernel(sc, visc, mask, fric, to_a, to_b, v, m, d, s, sem):
+    _, odd = place(sc)
+    copies = []
+    for side in range(2):
+        at = pl.ds(side * (ROWS - 8), 8)
+        copies.append(pltpu.make_async_copy(visc.at[:, at, :], v.at[side], sem.at[side * 3]))
+        copies.append(pltpu.make_async_copy(mask.at[at, :], m.at[side], sem.at[side * 3 + 1]))
+        copies.append(pltpu.make_async_copy(fric.at[at, :], d.at[side], sem.at[side * 3 + 2]))
+    for c in copies:
+        c.start()
+    for c in copies:
+        c.wait()
+    for side in range(2):
+        for i in range(4):
+            s[side, pl.ds(3 * i, 3), :] = v[side, i, pl.ds(5 * side, 3), :]
+        s[side, pl.ds(12, 2), :] = m[side, pl.ds(6 * side, 2), :].astype(F32)
+        s[side, pl.ds(14, 2), :] = d[side, pl.ds(6 * side, 2), :]
+    to_a[...] = s[1 - odd].astype(BF16)
+    to_b[...] = s[odd].astype(BF16)
+
+
+def edge_rows(sc, visc, mask, fric):
+    return pl.pallas_call(
+        edge_kernel,
+        in_specs=[sm(), hbm(), hbm(), hbm()],
+        out_specs=[vm()] * 2,
+        out_shape=[kept(16, 1024, dtype=BF16)] * 2,
+        scratch_shapes=[
+            pltpu.VMEM((2, 4, 8, 1024), F32),
+            pltpu.VMEM((2, 8, 1024), jnp.int32),
+            pltpu.VMEM((2, 8, 1024), F32),
+            pltpu.VMEM((2, 16, 1024), F32),
+            pltpu.SemaphoreType.DMA((6,)),
+        ],
         compiler_params=pltpu.CompilerParams(vmem_limit_bytes=8 * MIB),
-    )(sc, slots, target)
+    )(sc, far(visc), far(mask), far(fric))
 
 
 def spread(dst, at, x):
@@ -123,7 +196,11 @@
         prev = above
 
 
-def coef_kernel(sc, t1, t2, visc, other, fric, mask, bvel, svel, fz, fr, fc, inv, wgt, svm, msk, drg, v, bv):
+GROUPS = ((2, 16), (16, 32), (32, 48), (48, 66))
+
+
+def coef_kernel(sc, visc, other, fric, mask, bvel, svel, *refs):
+    outs, (fz, fr, fc, inv, wgt, svm, msk, drg, v, bv, sem, sem2) = refs[:9], refs[9:]
     own, _ = place(sc)
     for i in range(4):
         for src, at in ((visc, own * 4 + i), (other, (1 - own) * 4 + i)):
@@ -136,41 +213,55 @@
         for c in range(2):
             spread(bv.at[c], h * 8, bvel[c, h : h + 16, :])
 
-    def step(r, carry):
-        m, d = msk[row(r), :], drg[row(r), :]
-        coefficient_row(lambda l, j: v[l, row(r + j), :], m > 0.5, d, r + 2, fz, fr, fc, inv)
-        svm[row(r), :] = svm[row(r), :] * m
-        for c in range(2):
-            wgt[c, row(r), :] = (-m * d) * bv[c, row(r), :]
-        return carry
-
-    lax.fori_loop(1, ROWS - 1, step, 0)
-    for r in (0, ROWS - 1):
+    def strips(r):
         m, d = msk[row(r), :], drg[row(r), :]
         svm[row(r), :] = svm[row(r), :] * m
         for c in range(2):
             wgt[c, row(r), :] = (-m * d) * bv[c, row(r), :]
-
-
-def coefficients(sc, t1, t2, visc, other, fric, mask, bvel, svel):
+        return m, d
+
+    def step(r, carry):
+        m, d = strips(r)
+        coefficient_row(lambda l, j: v[l, row(r + j), :], m > 0.5, d, r + 2, fz, fr, fc, inv)
+        return carry
+
+    strips(0)
+    strips(ROWS - 1)
+    copies = []
+    for i, (src, dst) in enumerate(zip((msk, drg, v), (outs[6], outs[7], outs[8]))):
+        copies.append(pltpu.make_async_copy(src, dst, sem2.at[i]))
+    for c in copies:
+        c.start()
+    for k, (a, b) in enumerate(GROUPS):
+        lax.fori_loop(max(a - 2, 1), min(b - 2, ROWS - 1), step, 0)
+        part = pl.ds(a * 8, (b - a) * 8)
+        for i, src in enumerate((fz, fr, fc)):
+            copies.append(pltpu.make_async_copy(src.at[:, part, :], outs[i].at[:, part, :], sem.at[k, i]))
+            copies[-1].start()
+        copies.append(pltpu.make_async_copy(inv.at[:, :, part, :], outs[3].at[:, :, part, :], sem.at[k, 3]))
+        copies[-1].start()
+    for i, (src, dst) in enumerate(zip((wgt, svm), (outs[4], outs[5]))):
+        copies.append(pltpu.make_async_copy(src, dst, sem2.at[3 + i]))
+        copies[-1].start()
+    for c in copies:
+        c.wait()
+
+
+def coefficients(sc, visc, other, fric, mask, bvel, svel):
+    shapes = (FIELD, FIELD, FIELD, (2, *FIELD), (2, *STRIP), STRIP, STRIP, STRIP, (8, *STRIP))
     return pl.pallas_call(
         coef_kernel,
-        in_specs=[sm()] * 3 + [vm()] * 6,
-        out_specs=[vm()] * 9,
-        out_shape=[
-            kept(*FIELD),
-            kept(*FIELD),
-            kept(*FIELD),
-            kept(2, *FIELD),
-            kept(2, *STRIP),
-            kept(*STRIP),
-            kept(*STRIP),
-            kept(*STRIP),
-            kept(8, *STRIP),
+        in_specs=[sm()] + [vm()] * 6,
+        out_specs=[hbm()] * 9,
+        out_shape=[pltpu.HBM(x, F32) for x in shapes],
+        scratch_shapes=[pltpu.VMEM(x, F32) for x in shapes]
+        + [
+            pltpu.VMEM((2, *STRIP), F32),
+            pltpu.SemaphoreType.DMA((len(GROUPS), 4)),
+            pltpu.SemaphoreType.DMA((5,)),
         ],
-        scratch_shapes=[pltpu.VMEM((2, *STRIP), F32)],
-        compiler_params=pltpu.CompilerParams(vmem_limit_bytes=24 * MIB),
-    )(sc, t1, t2, visc, near(other), fric, mask, bvel, svel)
+        compiler_params=pltpu.CompilerParams(vmem_limit_bytes=32 * MIB),
+    )(sc, visc, other, fric, mask, bvel, svel)
 
 
 def ghost_kernel(sc, ea, eb, ea2, eb2, msk, drg, v, fz0, fr0, fc0, inv0, fz, fr, fc, inv, g, u):
@@ -214,12 +305,29 @@
     )(sc, *(near(x) for x in (ea, eb, ea2, eb2, msk, drg, v, fz, fr, fc, inv)))
 
 
-def misfit_kernel(sc, got, svm, msk, m_out, ea, eb, hot, rhs, pc):
+PARTS = 4
+
+
+def misfit_kernel(sc, got_h, svm_h, *refs):
+    here, m_out, ea, eb = refs[:8], *refs[8:11]
+    kept_, (got, svm, hot, rhs, pc, sem, sem2) = refs[11:19], refs[19:]
     _, odd = place(sc)
+    n = got.shape[0] // PARTS
+    parts = [
+        pltpu.make_async_copy(got_h.at[pl.ds(i * n, n)], got.at[pl.ds(i * n, n)], sem.at[i]) for i in range(PARTS)
+    ]
+    strips = pltpu.make_async_copy(svm_h, svm, sem.at[PARTS])
+    rest = [pltpu.make_async_copy(x, y, sem2.at[i]) for i, (x, y) in enumerate(zip(here, kept_))]
+    for c in (*parts, strips, *rest):
+        c.start()
+    msk = kept_[0]
     p = lax.broadcasted_iota(jnp.int32, (512, 128), 0)
     pc[...] = code_of(p).astype(F32)
+    rhs[:, pl.ds(128, 128)] = jnp.ones((4096, 128), BF16)
     lane = lax.broadcasted_iota(jnp.int32, (8, 128), 1)
     for b in range(32):
+        if b % (32 // PARTS) == 0:
+            parts[b // (32 // PARTS)].wait()
         for h in range(2):
             rhs[pl.ds(b * 128 + h * 64, 64), pl.ds(0, 128)] = got[2 * b + h, pl.ds(0, 64), :]
         c = jnp.where(
@@ -227,28 +335,35 @@
         )
         same = pc[...].reshape(64, 8, 128) == c[None]
         hot[:, pl.ds(b * 128, 128)] = jnp.where(same, 1.0, 0.0).reshape(512, 128).astype(BF16)
-    rhs[:, pl.ds(128, 128)] = jnp.ones((4096, 128), BF16)
     sums = jnp.dot(hot[...], rhs[...], preferred_element_type=F32)
+    strips.wait()
+    rest[0].wait()
     m_out[...] = sums[:, 128:] * svm[...] - msk[...] * sums[:, :128]
     for kind, e in enumerate((ea, eb)):
         at = jnp.where((odd + kind) % 2 == 0, ROWS - 2, 0)
         for r in range(2):
             e[pl.ds(r * 8, 8), :] = m_out[row(at + r), :]
-
-
-def misfit(sc, got, svm, msk):
+    for c in rest[1:]:
+        c.wait()
+
+
+def misfit(sc, got, svm, *rest):
     return pl.pallas_call(
         misfit_kernel,
-        in_specs=[sm()] + [vm()] * 3,
-        out_specs=[vm()] * 3,
-        out_shape=[kept(*STRIP), kept(16, 128), kept(16, 128)],
+        in_specs=[sm()] + [hbm()] * 10,
+        out_specs=[vm()] * 11,
+        out_shape=[kept(*STRIP), kept(16, 128), kept(16, 128)] + [kept(*x.shape) for x in rest],
         scratch_shapes=[
+            pltpu.VMEM(got.shape, BF16),
+            pltpu.VMEM(STRIP, F32),
             pltpu.VMEM((512, 4096), BF16),
             pltpu.VMEM((4096, 256), BF16),
             pltpu.VMEM((512, 128), F32),
+            pltpu.SemaphoreType.DMA((PARTS + 1,)),
+            pltpu.SemaphoreType.DMA((8,)),
         ],
         compiler_params=pltpu.CompilerParams(vmem_limit_bytes=24 * MIB),
-    )(sc, near(got), near(svm), near(msk))
+    )(sc, *(far(x) for x in (got, svm, *rest)))
 
 
 class Sweeps:
@@ -373,7 +488,7 @@
         both_kernel,
         in_specs=[sm()] * 3 + [vm()] * 12,
         out_specs=[vm()] * 8 + [hbm()],
-        out_shape=[kept(*s) for s in STATE] * 2 + [jax.ShapeDtypeStruct((2, 4, ROWS, 1024), F32)],
+        out_shape=[kept(*s) for s in STATE] * 2 + [pltpu.HBM((2, 4, ROWS, 1024), F32)],
         scratch_shapes=[pltpu.VMEM((4, ROWS, 1024), F32), pltpu.SemaphoreType.DMA],
         input_output_aliases={11: 0, 12: 1, 13: 2, 14: 3},
         compiler_params=pltpu.CompilerParams(vmem_limit_bytes=24 * MIB),
@@ -401,11 +516,11 @@
         in_specs=[sm()] * 3 + [vm()] * 11 + [hbm()],
         out_specs=[vm()] * 4 + [hbm(), vm()],
         out_shape=[kept(*s) for s in STATE]
-        + [jax.ShapeDtypeStruct((2, 4, ROWS, 1024), F32), jax.ShapeDtypeStruct((ROWS, 1024), F32)],
+        + [pltpu.HBM((2, 4, ROWS, 1024), F32), jax.ShapeDtypeStruct((ROWS, 1024), F32)],
         scratch_shapes=[pltpu.VMEM((4, ROWS, 1024), F32), pltpu.SemaphoreType.DMA],
         input_output_aliases={10: 0, 11: 1, 12: 2, 13: 3, 14: 4},
         compiler_params=pltpu.CompilerParams(vmem_limit_bytes=24 * MIB),
-    )(sc, t1, t2, near(g), near(racc), *(near(x) for x in coefs), *(near(x) for x in state), adj)[4:]
+    )(sc, t1, t2, near(g), near(racc), *(near(x) for x in coefs), *(near(x) for x in state), far(adj))[4:]
 
 
 def swaps(tiles, offset, across):
@@ -435,26 +550,16 @@
     got = lax.all_to_all(payload, "tile", split_axis=0, concat_axis=0, tiled=True)
     thick_other = swap_layers(layer_thick)
 
-    def edge(at):
-        return jnp.concatenate(
-            [
-                lax.slice_in_dim(viscosity, (ROWS - 3) if at else 0, ROWS if at else 3, axis=1).reshape(12, 1024),
-                lax.slice_in_dim(ice_mask, (ROWS - 2) if at else 0, ROWS if at else 2, axis=0).astype(F32),
-                lax.slice_in_dim(friction, (ROWS - 2) if at else 0, ROWS if at else 2, axis=0),
-            ]
-        ).astype(BF16)
-
-    top, bottom = edge(0), edge(1)
-    to_a = jnp.where(odd == 0, bottom, top)
-    to_b = jnp.where(odd == 0, top, bottom)
+    to_a, to_b = edge_rows(sc, viscosity, ice_mask, friction)
     near_rows = (swap(to_a, 0), swap(to_b, 1), swap(to_a, 0, True), swap(to_b, 1, True))
-    fz, fr, fc, inv, wgt, svm, msk, drg, v = coefficients(
-        sc, layer_thick, thick_other, viscosity, other, friction, ice_mask, base_vel, surf_vel
+    fz, fr, fc, inv, wgt, svm, msk, drg, v = coefficients(sc, viscosity, other, friction, ice_mask, base_vel, surf_vel)
+    got, near_rows, thick_other = lax.optimization_barrier((got, near_rows, thick_other))
+    m_own, ea, eb, msk, drg, v, fz, fr, fc, inv, wgt = misfit(
+        sc, got, svm, msk, drg, v, fz, fr, fc, inv, wgt
     )
     fz, fr, fc, inv = ghosts(sc, *near_rows, msk, drg, v, fz, fr, fc, inv)
     coefs = (fz, fr, fc, inv, wgt)
 
-    m_own, ea, eb = misfit(sc, got, svm, msk)
     ga, gb = swap(ea, 0), swap(eb, 1)
     m_oth = swap_layers(m_own)
     state = own_sweeps(sc, layer_thick, thick_other, m_own, coefs)
@@ -476,4 +581,5 @@
         P("tile", None),
     )
     out_specs = (P(None, "layer", "tile", None), P("tile", None))
+
     return jax.shard_map(body, mesh=mesh, in_specs=in_specs, out_specs=out_specs, check_vma=False)

time: 129 us -> 88.6 us (0.69)
  local copies, waits for them, and re-layouts: 33.8 us -> 0.04 us
  waiting for transfers between devices: 25.1 us -> 16.1 us
  Pallas kernels: 33.4 us -> 37.1 us
  other arithmetic: 2.17 us -> 0.07 us
    unnamed x56 -> x14, local copies, waits for them, and re-layouts: 29.1 us -> 0.04 us
    ppermute x4, waiting for transfers between devices: 21.9 us -> 13.8 us  [swap_layers(): return lax.ppermute(x, 'layer', [(0, 1), (1, 0)])]
    pallas_call x3 -> x4, Pallas kernels: 14.2 us -> 18.3 us  [the longest x1 8.76 us: coefficients(): pl.pallas_call(coef_kernel, in_specs=[sm()] + [vm()] * 6, out_specs=[hbm(...]
    reshape x2 -> x0, local copies, waits for them, and re-layouts: 2.78 us -> none  [edge(): lax.slice_in_dim(viscosity, ROWS - 3 if at else 0, ROWS if at else 3, axi...]
    slice x2 -> x0, local copies, waits for them, and re-layouts: 2 us -> none  [the longest x1 1.34 us: edge(): lax.slice_in_dim(friction, ROWS - 2 if at else 0, ROWS if at else 2, axis=0)]
  transfers between devices with their start and end apart: 11 -> 11, of which waited for: 2 -> 2; matrix products, arithmetic and copies ran while one was open for 5% -> 0% of each run, Pallas kernels for 19% -> 29%
where the time goes in v3:
time: 88.6 us; the launch traced here: 88.1 us
  Pallas kernels  37.1 us (42%)
  starting transfers between devices  34 us (38%)
  waiting for transfers between devices  16.1 us (18%)
  between operations  0.9 us (1%)
    ppermute x6, starting transfers between devices, swap(): return lax.ppermute(x, PAIR, swaps(tiles, kind, across))  18.1 us
    ppermute x4, waiting for transfers between devices, swap_layers(): return lax.ppermute(x, 'layer', [(0, 1), (1, 0)])  13.8 us
    all_to_all x1, starting transfers between devices, body(): lax.all_to_all(payload, 'tile', split_axis=0, concat_axis=0, tiled=True)  11.7 us
    pallas_call x1, Pallas kernels, coefficients(): pl.pallas_call(coef_kernel, in_specs=[sm()] + [vm()] * 6, out_specs=[hbm(...  8.76 us
    pallas_call x1, Pallas kernels, both_sweeps(): pl.pallas_call(both_kernel, in_specs=[sm()] * 3 + [vm()] * 12, out_specs=...  8.12 us
    pallas_call x1, Pallas kernels, own_sweeps(): pl.pallas_call(own_kernel, in_specs=[sm()] * 3 + [vm()] * 6, out_specs=[v...  7.67 us
    pallas_call x1, Pallas kernels, misfit(): pl.pallas_call(misfit_kernel, in_specs=[sm()] + [hbm()] * 10, out_specs=[...  5.58 us
    ppermute x4, starting transfers between devices, swap_layers(): return lax.ppermute(x, 'layer', [(0, 1), (1, 0)])  4.22 us
  transfers between devices with their start and end apart: 11, of which 2 were waited for; matrix products, arithmetic and copies ran while one was open for 0% of the time, Pallas kernels for 29%

profile of v3, /device:TPU:2, one launch (start us, length us, event | category | flops | bytes accessed | tf_op | source)
XLA Modules:
  0.0 88.1 jit_solution(6464500698502580474)
XLA Ops:
  0.6 0.0 copy-start
  0.7 2.8 %shard_map.95 = bf16[64,72,128]{2,1,0:T(8,128)(2,1)} custom-call(s32[1]{0:T(128)} %bitcast.sc, bf16[64,128,128]{2,1,0:T(8,128)(2,1)} %bitcast.2, s32[64,64]{1,0:T(8,128)} %target.1), custom_call_target="tpu_custom_call" | custom-call | tf_op jit(solution)/shard_map/pallas_call | solution.py:110
  3.5 0.0 copy-start.6
  3.5 0.0 copy-start.1
  3.5 0.0 copy-start.2
  3.5 0.0 copy-start.3
  3.6 0.0 copy-start.4
  3.6 11.7 %all-to-all-start = ((bf16[64,72,128]{2,1,0:T(8,128)(2,1)}), bf16[64,72,128]{2,1,0:T(8,128)(2,1)}, u32[]{:S(2)}, u32[]{:S(2)}) async-start(bf16[64,72,128]{2,1,0:T(8,128)(2,1)} %shard_map.95), calls=%async_computation | async-start | bytes 2359296 | tf_op jit(solution)/shard_map/all_to_all | solution.py:550
  15.2 0.0 copy-start.5
  15.2 0.1 convert_element_type.3
  15.3 1.1 %collective-permute-start.5 = (bf16[4,64,1024]{2,1,0:T(8,128)(2,1)S(1)}, bf16[4,64,1024]{2,1,0:T(8,128)(2,1)S(1)}, u32[]{:S(2)}, u32[]{:S(2)}) collective-permute-start(bf16[4,64,1024]{2,1,0:T(8,128)(2,1)S(1)} %convert_element_type.3), channel_id=1, source_target_pairs={{0,1},{1,0},{2,3},{3,2},{4,5},{5,4},{6,7},{7,6},{8,9},{9,8},{10,11... | collective-permute-start | bytes 1572872 | tf_op jit(solution)/shard_map/ppermute | solution.py:536
  16.4 1.1 %shard_map.96 = (bf16[16,1024]{1,0:T(8,128)(2,1)S(1)}, bf16[16,1024]{1,0:T(8,128)(2,1)S(1)}) custom-call(s32[1]{0:T(128)} %bitcast.sc, f32[4,64,1024]{2,1,0:T(8,128)} %visc.3, s32[64,1024]{1,0:T(8,128)} %mask.3, f32[64,1024]{1,0:T(8,128)} %fric.3), custom_call_target="tpu_custom_call" | custom-call | tf_op jit(solution)/shard_map/pallas_call | solution.py:151
  17.5 0.1 collective-permute-start
  17.6 7.7 %collective-permute-start.1 = (bf16[16,1024]{1,0:T(8,128)(2,1)S(1)}, bf16[16,1024]{1,0:T(8,128)(2,1)S(1)}, u32[]{:S(2)}, u32[]{:S(2)}) collective-permute-start(bf16[16,1024]{1,0:T(8,128)(2,1)S(1)} %get-tuple-element.47), channel_id=1, source_target_pairs={{2,4},{4,2},{3,5},{5,3},{6,8},{8,6},{7,9},{9,7},{10,12},{12,10},{1... | collective-permute-start | bytes 98312 | tf_op jit(solution)/shard_map/ppermute | solution.py:546
  25.3 0.1 collective-permute-start.2
  25.4 3.0 %collective-permute-start.3 = (bf16[16,1024]{1,0:T(8,128)(2,1)S(1)}, bf16[16,1024]{1,0:T(8,128)(2,1)S(1)}, u32[]{:S(2)}, u32[]{:S(2)}) collective-permute-start(bf16[16,1024]{1,0:T(8,128)(2,1)S(1)} %get-tuple-element.47), channel_id=1, source_target_pairs={{2,5},{5,2},{3,4},{4,3},{6,9},{9,6},{7,8},{8,7},{10,13},{13,10},{1... | collective-permute-start | bytes 98312 | tf_op jit(solution)/shard_map/ppermute | solution.py:546
  28.4 13.8 %collective-permute-done.5.other = bf16[4,64,1024]{2,1,0:T(8,128)(2,1)S(1)} collective-permute-done((bf16[4,64,1024]{2,1,0:T(8,128)(2,1)S(1)}, bf16[4,64,1024]{2,1,0:T(8,128)(2,1)S(1)}, u32[]{:S(2)}, u32[]{:S(2)}) %collective-permute-start.5) | collective-permute-done | bytes 524320 | tf_op jit(solution)/shard_map/ppermute | solution.py:536
  42.3 1.0 %collective-permute-start.4 = (f32[4]{0:T(128)S(1)}, f32[4]{0:T(128)S(1)}, u32[]{:S(2)}, u32[]{:S(2)}) collective-permute-start(f32[4]{0:T(128)S(1)} %copy-done.6), channel_id=1, source_target_pairs={{0,1},{1,0},{2,3},{3,2},{4,5},{5,4},{6,7},{7,6},{8,9},{9,8},{10,11... | collective-permute-start | bytes 56 | tf_op jit(solution)/shard_map/ppermute | solution.py:536
  43.3 8.8 %shard_map.97 = (f32[8,544,128]{2,1,0:T(8,128)}, f32[8,544,128]{2,1,0:T(8,128)}, f32[8,544,128]{2,1,0:T(8,128)}, f32[2,8,544,128]{3,2,1,0:T(8,128)}, f32[2,512,1...) custom-call(s32[1]{0:T(128)} %bitcast.sc, ...), custom_call_target="tpu_custom_call" | custom-call | tf_op jit(solution)/shard_map/pallas_call | solution.py:252
  52.1 0.0 collective-permute-done.4.t2
  52.1 0.0 collective-permute-done.1.eb
  52.1 0.0 collective-permute-done.2.ea2
  52.1 0.0 all-to-all-done.got_h
  52.1 5.6 %shard_map.98 = (f32[512,128]{1,0:T(8,128)S(1)}, f32[16,128]{1,0:T(8,128)S(1)}, f32[16,128]{1,0:T(8,128)S(1)}, f32[512,128]{1,0:T(8,128)S(1)}, f32[512,128]{1,0:...) custom-call(s32[1]{0:T(128)} %bitcast.sc, ...), custom_call_target="tpu_custom_call" | custom-call | tf_op jit(solution)/shard_map/pallas_call | solution.py:351
  57.7 1.1 %collective-permute-start.9 = (f32[512,128]{1,0:T(8,128)S(1)}, f32[512,128]{1,0:T(8,128)S(1)}, u32[]{:S(2)}, u32[]{:S(2)}) collective-permute-start(f32[512,128]{1,0:T(8,128)S(1)} %get-tuple-element.61.m), channel_id=1, source_target_pairs={{0,1},{1,0},{2,3},{3,2},{4,5},{5,4},{6,7},{7,6},{8,9},{9,8},{10,11... | collective-permute-start | bytes 786440 | tf_op jit(solution)/shard_map/ppermute | solution.py:536
  58.8 7.2 %collective-permute-start.7 = (f32[16,128]{1,0:T(8,128)S(1)}, f32[16,128]{1,0:T(8,128)S(1)}, u32[]{:S(2)}, u32[]{:S(2)}) collective-permute-start(f32[16,128]{1,0:T(8,128)S(1)} %get-tuple-element.60), channel_id=1, source_target_pairs={{2,4},{4,2},{3,5},{5,3},{6,8},{8,6},{7,9},{9,7},{10,12},{12,10},{1... | collective-permute-start | bytes 24584 | tf_op jit(solution)/shard_map/ppermute | solution.py:546
  66.0 2.2 %collective-permute-done.7.gb = f32[16,128]{1,0:T(8,128)S(1)} collective-permute-done((f32[16,128]{1,0:T(8,128)S(1)}, f32[16,128]{1,0:T(8,128)S(1)}, u32[]{:S(2)}, u32[]{:S(2)}) %collective-permute-start.7) | collective-permute-done | bytes 8224 | tf_op jit(solution)/shard_map/ppermute | solution.py:546
  68.3 1.0 %collective-permute-start.8 = (f32[32,128]{1,0:T(8,128)S(1)}, f32[32,128]{1,0:T(8,128)S(1)}, u32[]{:S(2)}, u32[]{:S(2)}) collective-permute-start(f32[32,128]{1,0:T(8,128)S(1)} %pad_maximum_fusion), channel_id=1, source_target_pairs={{0,1},{1,0},{2,3},{3,2},{4,5},{5,4},{6,7},{7,6},{8,9},{9,8},{10,11... | collective-permute-start | bytes 49160 | tf_op jit(solution)/shard_map/ppermute | solution.py:536
  69.3 0.3 shard_map.99
  69.6 7.7 %shard_map.100 = (f32[8,544,128]{2,1,0:T(8,128)S(1)}, f32[8,544,128]{2,1,0:T(8,128)S(1)}, f32[8,512,128]{2,1,0:T(8,128)S(1)}, f32[512,128]{1,0:T(8,128)S(1)}) custom-call(s32[1]{0:T(128)} %bitcast.sc, f32[4]{0:T(128)S(1)} %copy-done.6, f32[4]{0:T(128)S(1)} %collective-permute-done.4.t2, f32[512,128]{1,0:T(8,128)S(1)} %get-tuple-element.61.m, ...), custom_call_target="tpu_custom_call" | custom-call | tf_op jit(solution)/shard_map/pallas_call | solution.py:464
  77.3 8.1 %shard_map.101 = (f32[8,544,128]{2,1,0:T(8,128)S(1)}, f32[8,544,128]{2,1,0:T(8,128)S(1)}, f32[8,512,128]{2,1,0:T(8,128)S(1)}, f32[512,128]{1,0:T(8,128)S(1)}, f3...) custom-call(s32[1]{0:T(128)} %bitcast.sc, ...), custom_call_target="tpu_custom_call", output_to_operand_aliasing={{0}: (11, {}), {1}: (12, {}), {2}: (13, {}), {3}: (14, {})} | custom-call | tf_op jit(solution)/shard_map/pallas_call | solution.py:487
  85.4 2.7 %shard_map.102 = (f32[8,544,128]{2,1,0:T(8,128)S(1)}, f32[8,544,128]{2,1,0:T(8,128)S(1)}, f32[8,512,128]{2,1,0:T(8,128)S(1)}, f32[512,128]{1,0:T(8,128)S(1)}, f3...) custom-call(s32[1]{0:T(128)} %bitcast.sc, ...), custom_call_target="tpu_custom_call", output_to_operand_aliasing={{0}: (10, {}), {1}: (11, {}), {2}: (12, {}), {3}: (13, {}),... | custom-call | tf_op jit(solution)/shard_map/pallas_call | solution.py:514
  (14 shorter events, 0.0 us)
Async XLA Ops:
  0.6 14.6 %copy-start = (f32[4,64,1024]{2,1,0:T(8,128)S(1)}, f32[4,64,1024]{2,1,0:T(8,128)}, u32[]{:S(2)}) copy-start(f32[4,64,1024]{2,1,0:T(8,128)} %visc.3) | copy-start | bytes 3145732
  3.5 38.7 %copy-start.6 = (f32[4]{0:T(128)S(1)}, f32[4]{0:T(128)}, u32[]{:S(2)}) copy-start(f32[4]{0:T(128)} %t1.5) | copy-start | bytes 52
  3.5 39.8 %copy-start.1 = (f32[4,64,1024]{2,1,0:T(8,128)S(1)}, f32[4,64,1024]{2,1,0:T(8,128)}, u32[]{:S(2)}) copy-start(f32[4,64,1024]{2,1,0:T(8,128)} %visc.3) | copy-start | bytes 3145732
  3.5 39.7 %copy-start.2 = (f32[64,1024]{1,0:T(8,128)S(1)}, f32[64,1024]{1,0:T(8,128)}, u32[]{:S(2)}) copy-start(f32[64,1024]{1,0:T(8,128)} %fric.3) | copy-start | bytes 786436
  3.5 39.7 %copy-start.3 = (s32[64,1024]{1,0:T(8,128)S(1)}, s32[64,1024]{1,0:T(8,128)}, u32[]{:S(2)}) copy-start(s32[64,1024]{1,0:T(8,128)} %mask.3) | copy-start | bytes 786436
  3.6 39.7 %copy-start.4 = (f32[2,64,1024]{2,1,0:T(8,128)S(1)}, f32[2,64,1024]{2,1,0:T(8,128)}, u32[]{:S(2)}) copy-start(f32[2,64,1024]{2,1,0:T(8,128)} %bvel.1) | copy-start | bytes 1572868
  3.6 48.6 %all-to-all-start = ((bf16[64,72,128]{2,1,0:T(8,128)(2,1)}), bf16[64,72,128]{2,1,0:T(8,128)(2,1)}, u32[]{:S(2)}, u32[]{:S(2)}) async-start(bf16[64,72,128]{2,1,0:T(8,128)(2,1)} %shard_map.95), calls=%async_computation | async-start | bytes 2359296 | tf_op jit(solution)/shard_map/all_to_all | solution.py:550
  15.2 28.1 %copy-start.5 = (f32[2,64,1024]{2,1,0:T(8,128)S(1)}, f32[2,64,1024]{2,1,0:T(8,128)}, u32[]{:S(2)}) copy-start(f32[2,64,1024]{2,1,0:T(8,128)} %svel.1) | copy-start | bytes 1572868
  15.3 26.9 %collective-permute-start.5 = (bf16[4,64,1024]{2,1,0:T(8,128)(2,1)S(1)}, bf16[4,64,1024]{2,1,0:T(8,128)(2,1)S(1)}, u32[]{:S(2)}, u32[]{:S(2)}) collective-permute-start(bf16[4,64,1024]{2,1,0:T(8,128)(2,1)S(1)} %convert_element_type.3), channel_id=1, source_target_pairs={{0,1},{1,0},{2,3},{3,2},{4,5},{5,4},{6,7},{7,6},{8,9},{9,8},{10,11... | collective-permute-start | bytes 1572872 | tf_op jit(solution)/shard_map/ppermute | solution.py:536
  17.5 34.5 %collective-permute-start = (bf16[16,1024]{1,0:T(8,128)(2,1)S(1)}, bf16[16,1024]{1,0:T(8,128)(2,1)S(1)}, u32[]{:S(2)}, u32[]{:S(2)}) collective-permute-start(bf16[16,1024]{1,0:T(8,128)(2,1)S(1)} %get-tuple-element.46), channel_id=1, source_target_pairs={{0,2},{2,0},{1,3},{3,1},{4,6},{6,4},{5,7},{7,5},{8,10},{10,8},{9,1... | collective-permute-start | bytes 98312 | tf_op jit(solution)/shard_map/ppermute | solution.py:546
  17.6 34.4 %collective-permute-start.1 = (bf16[16,1024]{1,0:T(8,128)(2,1)S(1)}, bf16[16,1024]{1,0:T(8,128)(2,1)S(1)}, u32[]{:S(2)}, u32[]{:S(2)}) collective-permute-start(bf16[16,1024]{1,0:T(8,128)(2,1)S(1)} %get-tuple-element.47), channel_id=1, source_target_pairs={{2,4},{4,2},{3,5},{5,3},{6,8},{8,6},{7,9},{9,7},{10,12},{12,10},{1... | collective-permute-start | bytes 98312 | tf_op jit(solution)/shard_map/ppermute | solution.py:546
  25.3 26.8 %collective-permute-start.2 = (bf16[16,1024]{1,0:T(8,128)(2,1)S(1)}, bf16[16,1024]{1,0:T(8,128)(2,1)S(1)}, u32[]{:S(2)}, u32[]{:S(2)}) collective-permute-start(bf16[16,1024]{1,0:T(8,128)(2,1)S(1)} %get-tuple-element.46), channel_id=1, source_target_pairs={{0,3},{3,0},{1,2},{2,1},{4,7},{7,4},{5,6},{6,5},{8,11},{11,8},{9,1... | collective-permute-start | bytes 98312 | tf_op jit(solution)/shard_map/ppermute | solution.py:546
  25.4 26.7 %collective-permute-start.3 = (bf16[16,1024]{1,0:T(8,128)(2,1)S(1)}, bf16[16,1024]{1,0:T(8,128)(2,1)S(1)}, u32[]{:S(2)}, u32[]{:S(2)}) collective-permute-start(bf16[16,1024]{1,0:T(8,128)(2,1)S(1)} %get-tuple-element.47), channel_id=1, source_target_pairs={{2,5},{5,2},{3,4},{4,3},{6,9},{9,6},{7,8},{8,7},{10,13},{13,10},{1... | collective-permute-start | bytes 98312 | tf_op jit(solution)/shard_map/ppermute | solution.py:546
  42.3 9.8 %collective-permute-start.4 = (f32[4]{0:T(128)S(1)}, f32[4]{0:T(128)S(1)}, u32[]{:S(2)}, u32[]{:S(2)}) collective-permute-start(f32[4]{0:T(128)S(1)} %copy-done.6), channel_id=1, source_target_pairs={{0,1},{1,0},{2,3},{3,2},{4,5},{5,4},{6,7},{7,6},{8,9},{9,8},{10,11... | collective-permute-start | bytes 56 | tf_op jit(solution)/shard_map/ppermute | solution.py:536
  57.7 19.6 %collective-permute-start.9 = (f32[512,128]{1,0:T(8,128)S(1)}, f32[512,128]{1,0:T(8,128)S(1)}, u32[]{:S(2)}, u32[]{:S(2)}) collective-permute-start(f32[512,128]{1,0:T(8,128)S(1)} %get-tuple-element.61.m), channel_id=1, source_target_pairs={{0,1},{1,0},{2,3},{3,2},{4,5},{5,4},{6,7},{7,6},{8,9},{9,8},{10,11... | collective-permute-start | bytes 786440 | tf_op jit(solution)/shard_map/ppermute | solution.py:536
  58.8 7.2 %collective-permute-start.6 = (f32[16,128]{1,0:T(8,128)S(1)}, f32[16,128]{1,0:T(8,128)S(1)}, u32[]{:S(2)}, u32[]{:S(2)}) collective-permute-start(f32[16,128]{1,0:T(8,128)S(1)} %get-tuple-element.59), channel_id=1, source_target_pairs={{0,2},{2,0},{1,3},{3,1},{4,6},{6,4},{5,7},{7,5},{8,10},{10,8},{9,1... | collective-permute-start | bytes 24584 | tf_op jit(solution)/shard_map/ppermute | solution.py:546
  58.8 9.5 %collective-permute-start.7 = (f32[16,128]{1,0:T(8,128)S(1)}, f32[16,128]{1,0:T(8,128)S(1)}, u32[]{:S(2)}, u32[]{:S(2)}) collective-permute-start(f32[16,128]{1,0:T(8,128)S(1)} %get-tuple-element.60), channel_id=1, source_target_pairs={{2,4},{4,2},{3,5},{5,3},{6,8},{8,6},{7,9},{9,7},{10,12},{12,10},{1... | collective-permute-start | bytes 24584 | tf_op jit(solution)/shard_map/ppermute | solution.py:546
  68.3 17.1 %collective-permute-start.8 = (f32[32,128]{1,0:T(8,128)S(1)}, f32[32,128]{1,0:T(8,128)S(1)}, u32[]{:S(2)}, u32[]{:S(2)}) collective-permute-start(f32[32,128]{1,0:T(8,128)S(1)} %pad_maximum_fusion), channel_id=1, source_target_pairs={{0,1},{1,0},{2,3},{3,2},{4,5},{5,4},{6,7},{7,6},{8,9},{9,8},{10,11... | collective-permute-start | bytes 49160 | tf_op jit(solution)/shard_map/ppermute | solution.py:536

commit v4 on v3

v4 whole, which is shorter than its diff:
```python
import jax
import jax.numpy as jnp
from jax import lax
from jax.experimental import pallas as pl
from jax.experimental.pallas import tpu as pltpu
from jax.sharding import PartitionSpec as P


F32 = jnp.float32
BF16 = jnp.bfloat16
ROWS = 64
EXT = 68
PAIR = ("tile", "layer")
FIELD = (EXT, 64, 128)
STRIP = (ROWS * 8, 128)
MIB = 1 << 20


def vm():
    return pl.BlockSpec(memory_space=pltpu.VMEM)


def sm():
    return pl.BlockSpec(memory_space=pltpu.SMEM)


def hbm():
    return pl.BlockSpec(memory_space=pltpu.HBM)


def far(x):
    return pltpu.with_memory_space_constraint(x, pltpu.HBM)


def kept(*shape, dtype=F32):
    return pltpu.VMEM(shape, dtype)


def near(x):
    return pltpu.with_memory_space_constraint(x, pltpu.VMEM)


def row(r):
    return pl.ds(pl.multiple_of(r * 8, 8), 8)


def at(l):
    return pl.ds(l * 8, 8)


def place(sc):
    return sc[0] & 1, sc[0] >> 1


def lanes():
    lane = lax.broadcasted_iota(jnp.int32, (8, 128), 1)
    sub = lax.broadcasted_iota(jnp.int32, (8, 128), 0)
    return lane, sub


def east(x, last):
    r = pltpu.roll(x, 127, 1)
    return jnp.where(last, pltpu.roll(r, 7, 0), r)


def west(x, first):
    r = pltpu.roll(x, 1, 1)
    return jnp.where(first, pltpu.roll(r, 1, 0), r)


def code_of(t):
    return jnp.where(t < 512, (128 + (t & 127)) << (t >> 7), 0)


def pack_kernel(sc, slots, target, o, x, y, t, f, codes, sin, sout, st):
    own, _ = place(sc)
    n = slots.shape[0]
    step = n // CHUNKS
    tin = pltpu.make_async_copy(target, t, st)
    tin.start()
    ins = [
        pltpu.make_async_copy(slots.at[pl.ds(i * step, step)], x.at[pl.ds(i * step, step)], sin.at[i])
        for i in range(CHUNKS)
    ]
    outs = [
        pltpu.make_async_copy(y.at[pl.ds(i * step, step)], o.at[pl.ds(i * step, step)], sout.at[i])
        for i in range(CHUNKS)
    ]
    for i in ins:
        i.start()
    tin.wait()
    c = code_of(t[...]).astype(F32)
    codes[...] = jnp.concatenate([c, c], axis=1)
    for i in range(CHUNKS):
        ins[i].wait()

        def one(d, carry):
            f[d] = x[d].astype(F32)
            y[d, pl.ds(0, 64), :] = f[d, pl.ds(own, 64, stride=2), :].astype(BF16)
            y[d, pl.ds(64, 8), :] = jnp.broadcast_to(codes[pl.ds(d, 1), :], (8, 128)).astype(BF16)
            return carry

        lax.fori_loop(i * step, (i + 1) * step, one, 0, unroll=8)
        outs[i].start()
    for i in outs:
        i.wait()


CHUNKS = 4


def pack(sc, slots, target):
    n = slots.shape[0]
    return pl.pallas_call(
        pack_kernel,
        in_specs=[sm(), hbm(), hbm()],
        out_specs=hbm(),
        out_shape=pltpu.HBM((n, 72, 128), BF16),
        scratch_shapes=[
            pltpu.VMEM((n, 128, 128), BF16),
            pltpu.VMEM((n, 72, 128), BF16),
            pltpu.VMEM((n, 64), jnp.int32),
            pltpu.VMEM((n, 128, 128), F32),
            pltpu.VMEM((n, 128), F32),
            pltpu.SemaphoreType.DMA((CHUNKS,)),
            pltpu.SemaphoreType.DMA((CHUNKS,)),
            pltpu.SemaphoreType.DMA,
        ],
        compiler_params=pltpu.CompilerParams(vmem_limit_bytes=16 * MIB),
    )(sc, far(slots), far(target))


def edge_kernel(sc, visc, mask, fric, to_a, to_b, v, m, d, s, sem):
    _, odd = place(sc)
    copies = []
    for side in range(2):
        at = pl.ds(side * (ROWS - 8), 8)
        copies.append(pltpu.make_async_copy(visc.at[:, at, :], v.at[side], sem.at[side * 3]))
        copies.append(pltpu.make_async_copy(mask.at[at, :], m.at[side], sem.at[side * 3 + 1]))
        copies.append(pltpu.make_async_copy(fric.at[at, :], d.at[side], sem.at[side * 3 + 2]))
    for c in copies:
        c.start()
    for c in copies:
        c.wait()
    for side in range(2):
        for i in range(4):
            s[side, pl.ds(3 * i, 3), :] = v[side, i, pl.ds(5 * side, 3), :]
        s[side, pl.ds(12, 2), :] = m[side, pl.ds(6 * side, 2), :].astype(F32)
        s[side, pl.ds(14, 2), :] = d[side, pl.ds(6 * side, 2), :]
    to_a[...] = s[1 - odd].astype(BF16)
    to_b[...] = s[odd].astype(BF16)


def edge_rows(sc, visc, mask, fric):
    return pl.pallas_call(
        edge_kernel,
        in_specs=[sm(), hbm(), hbm(), hbm()],
        out_specs=[vm()] * 2,
        out_shape=[kept(16, 1024, dtype=BF16)] * 2,
        scratch_shapes=[
            pltpu.VMEM((2, 4, 8, 1024), F32),
            pltpu.VMEM((2, 8, 1024), jnp.int32),
            pltpu.VMEM((2, 8, 1024), F32),
            pltpu.VMEM((2, 16, 1024), F32),
            pltpu.SemaphoreType.DMA((6,)),
        ],
        compiler_params=pltpu.CompilerParams(vmem_limit_bytes=8 * MIB),
    )(sc, far(visc), far(mask), far(fric))


def spread(dst, at, x):
    n = x.shape[0]
    for k in range(8):
        dst[pl.ds(at + k, n, stride=8), :] = x[:, k * 128 : (k + 1) * 128]


def weights(c):
    return jnp.where(c == 0, 4.0, 1.0), jnp.where(c == 0, 1.0, 4.0)


def coefficient_row(view, m, drag, r, pairs, fz, fr, fc, invs):
    lane, sub = lanes()
    last, first = lane == 127, lane == 0
    end = last & (sub == 7)
    start = first & (sub == 0)
    prev = None
    for l in range(8):
        c = view(l, 0)
        fe = 0.5 * (c + jnp.where(end, 0.0, east(c, last)))
        fw = 0.5 * (c + jnp.where(start, 0.0, west(c, first)))
        south = 0.5 * (c + view(l, 1))
        north = 0.5 * (c + view(l, -1))
        below = 4.0 * c if l == 0 else prev
        above = 4.0 * (c + view(l + 1, 0)) if l < 7 else 4.0 * c
        fz[r, at(l), :] = above
        fr[r, at(l), :] = south
        fc[r, at(l), :] = jnp.where(end, 0.0, fe)
        rows_, cols_, both = north + south, fe + fw, below + above
        if l == 0:
            both = both + drag
        for (rw, cw), inv, shift in zip(pairs, *invs):
            diag = both + rw * rows_ + cw * cols_
            inv[r + shift, at(l), :] = jnp.where(m, 0.7 / diag, 0.0)
        prev = above


GROUPS = ((3, 16), (16, 32), (32, 48), (48, 65))
INSIDE = pl.ds(3, 62)
RIM = (8, 32, 128)
N_FIELDS = 5


def coef_kernel(sc, visc, other, fric, mask, bvel, svel, *refs):
    outs, rest = refs[:11], refs[11:]
    fields, (wo, wx, svm, msk, rim, rimd, drg, v, bv, sem, sem2) = rest[:N_FIELDS], rest[N_FIELDS:]
    fz, fr, fc, inv_own, inv_oth = fields
    own, _ = place(sc)
    for i in range(4):
        for src, to in ((visc, own * 4 + i), (other, (1 - own) * 4 + i)):
            for h in range(0, ROWS, 16):
                spread(v.at[to], h * 8, src[i, h : h + 16, :].astype(F32))
    for h in range(0, ROWS, 16):
        spread(msk, h * 8, mask[h : h + 16, :].astype(F32))
        spread(drg, h * 8, fric[h : h + 16, :])
        spread(svm, h * 8, svel[own, h : h + 16, :])
        spread(bv.at[0], h * 8, bvel[own, h : h + 16, :])
        spread(bv.at[1], h * 8, bvel[1 - own, h : h + 16, :])
    for l in range(8):
        rim[l, pl.ds(0, 16), :] = v[l, pl.ds(0, 16), :]
        rim[l, pl.ds(16, 16), :] = v[l, pl.ds((ROWS - 2) * 8, 16), :]
    rimd[pl.ds(0, 8), :] = drg[row(0), :]
    rimd[pl.ds(8, 8), :] = drg[row(ROWS - 1), :]
    pairs = (weights(own), weights(1 - own))

    def strips(r):
        m, d = msk[row(r), :], drg[row(r), :]
        svm[row(r), :] = svm[row(r), :] * m
        for c, w in enumerate((wo, wx)):
            w[row(r), :] = (-m * d) * bv[c, row(r), :]
        return m, d

    def step(r, carry):
        m, d = strips(r)
        invs = ((inv_own, inv_oth), (0, 0))
        coefficient_row(lambda l, j: v[l, row(r + j), :], m > 0.5, d, r + 2, pairs, fz, fr, fc, invs)
        return carry

    strips(0)
    strips(ROWS - 1)
    copies = []
    for i, (src, dst) in enumerate(zip((msk, rim, rimd), outs[8:])):
        copies.append(pltpu.make_async_copy(src, dst, sem2.at[i]))
    for c in copies:
        c.start()
    for k, (a, b) in enumerate(GROUPS):
        lax.fori_loop(a - 2, b - 2, step, 0)
        part = pl.ds(a, b - a)
        for i, src in enumerate(fields):
            copies.append(pltpu.make_async_copy(src.at[part], outs[i].at[part], sem.at[k, i]))
            copies[-1].start()
    for i, (src, dst) in enumerate(zip((wo, wx, svm), outs[5:])):
        copies.append(pltpu.make_async_copy(src, dst, sem2.at[3 + i]))
        copies[-1].start()
    for c in copies:
        c.wait()


def coefficients(sc, visc, other, fric, mask, bvel, svel):
    shapes = (FIELD,) * N_FIELDS + (STRIP,) * 4 + (RIM, (16, 128))
    return pl.pallas_call(
        coef_kernel,
        in_specs=[sm()] + [vm()] * 6,
        out_specs=[hbm()] * 11,
        out_shape=[pltpu.HBM(x, F32) for x in shapes],
        scratch_shapes=[pltpu.VMEM(x, F32) for x in shapes]
        + [
            pltpu.VMEM(STRIP, F32),
            pltpu.VMEM((8, (ROWS + 1) * 8, 128), F32),
            pltpu.VMEM((2, *STRIP), F32),
            pltpu.SemaphoreType.DMA((len(GROUPS), N_FIELDS)),
            pltpu.SemaphoreType.DMA((6,)),
        ],
        compiler_params=pltpu.CompilerParams(vmem_limit_bytes=32 * MIB),
    )(sc, visc, other, fric, mask, bvel, svel)


def ghost_kernel(sc, ea, eb, ea2, eb2, msk, rim, rimd, fz0, fr0, fc0, inv0, fz, fr, fc, inv, gx, g, u):
    own, odd = place(sc)
    pairs = (weights(own), weights(1 - own))
    for kind, pair in enumerate(((ea, ea2), (eb, eb2))):
        side = jnp.where((odd + kind) % 2 == 1, 0, 1)
        for who, e in enumerate(pair):
            spread(g.at[side, who], 0, e[...].astype(F32))
    for side in range(2):
        to = 0 if side == 0 else 2
        for who in range(2):
            base = (own if who == 0 else 1 - own) * 4
            for i in range(4):
                u[side, base + i, pl.ds(to * 8, 24), :] = g[side, who, pl.ds(i * 24, 24), :]
        for l in range(8):
            u[side, l, pl.ds(24 * (1 - side), 16), :] = rim[l, pl.ds(16 * side, 16), :]
        for j in range(3):
            if side == 0:
                r, ghost, inside = j, j, 0
            else:
                r, ghost, inside = ROWS + 1 + j, j - 1, ROWS - 1
            if (side == 0 and j == 2) or (side == 1 and j == 0):
                m, d = msk[row(inside), :], rimd[pl.ds(8 * side, 8), :]
            else:
                m, d = g[side, 0, pl.ds((12 + ghost) * 8, 8), :], g[side, 0, pl.ds((14 + ghost) * 8, 8), :]
            invs = ((inv, gx), (0, 0 if side == 0 else 3 - (ROWS + 1)))
            coefficient_row(lambda l, s: u[side, l, row(j + 1 + s), :], m > 0.5, d, r, pairs, fz, fr, fc, invs)


def ghosts(sc, ea, eb, ea2, eb2, msk, rim, rimd, fz, fr, fc, inv):
    return pl.pallas_call(
        ghost_kernel,
        in_specs=[sm()] + [vm()] * 11,
        out_specs=[vm()] * 5,
        out_shape=[kept(*FIELD)] * 4 + [kept(6, 64, 128)],
        scratch_shapes=[pltpu.VMEM((2, 2, 128, 128), F32), pltpu.VMEM((2, 8, 40, 128), F32)],
        input_output_aliases={8: 0, 9: 1, 10: 2, 11: 3},
        compiler_params=pltpu.CompilerParams(vmem_limit_bytes=24 * MIB),
    )(sc, *(near(x) for x in (ea, eb, ea2, eb2, msk, rim, rimd, fz, fr, fc, inv)))


PARTS = 4


def misfit_kernel(sc, got_h, svm_h, *refs):
    n_kept = len(KEPT)
    here, (m_out, ea, eb), refs = refs[:n_kept], refs[n_kept : n_kept + 3], refs[n_kept + 3 :]
    kept_, (got, svm, hot, rhs, pc, acc, sem, sem2) = refs[:n_kept], refs[n_kept:]
    _, odd = place(sc)
    n = got.shape[0] // PARTS
    parts = [
        pltpu.make_async_copy(got_h.at[pl.ds(i * n, n)], got.at[pl.ds(i * n, n)], sem.at[i]) for i in range(PARTS)
    ]
    strips = pltpu.make_async_copy(svm_h, svm, sem.at[PARTS])
    rest = []
    for i, (x, y) in enumerate(zip(here, kept_)):
        if KEPT[i] == FIELD:
            x, y = x.at[INSIDE], y.at[INSIDE]
        rest.append(pltpu.make_async_copy(x, y, sem2.at[i]))
    for c in (*parts, strips, *rest):
        c.start()
    msk = kept_[0]
    p = lax.broadcasted_iota(jnp.int32, (512, 128), 0)
    pc[...] = code_of(p).astype(F32)
    rhs[:, pl.ds(128, 128)] = jnp.ones((rhs.shape[0], 128), BF16)
    lane = lax.broadcasted_iota(jnp.int32, (8, 128), 1)
    for part in range(PARTS):
        parts[part].wait()
        for b in range(n // 2):
            s = part * n + 2 * b
            for h in range(2):
                rhs[pl.ds((2 * b + h) * 64, 64), pl.ds(0, 128)] = got[s + h, pl.ds(0, 64), :]
            c = jnp.where(lane < 64, got[s, pl.ds(64, 8), :].astype(F32), got[s + 1, pl.ds(64, 8), :].astype(F32))
            same = pc[...].reshape(64, 8, 128) == c[None]
            hot[:, pl.ds(b * 128, 128)] = jnp.where(same, 1.0, 0.0).reshape(512, 128).astype(BF16)
        sums = jnp.dot(hot[...], rhs[...], preferred_element_type=F32)
        acc[...] = sums if part == 0 else acc[...] + sums
    strips.wait()
    rest[0].wait()
    m_out[...] = acc[:, 128:] * svm[...] - msk[...] * acc[:, :128]
    for kind, e in enumerate((ea, eb)):
        start = jnp.where((odd + kind) % 2 == 0, ROWS - 2, 0)
        for r in range(2):
            e[pl.ds(r * 8, 8), :] = m_out[row(start + r), :]
    for c in rest[1:]:
        c.wait()


KEPT = (STRIP, RIM, (16, 128), STRIP) + (FIELD,) * 4


def misfit(sc, got, svm, *rest):
    k = got.shape[0] // PARTS * 64
    return pl.pallas_call(
        misfit_kernel,
        in_specs=[sm()] + [hbm()] * (2 + len(KEPT)),
        out_specs=[vm()] * (3 + len(KEPT)),
        out_shape=[kept(*STRIP), kept(16, 128), kept(16, 128)] + [kept(*x) for x in KEPT],
        scratch_shapes=[
            pltpu.VMEM(got.shape, BF16),
            pltpu.VMEM(STRIP, F32),
            pltpu.VMEM((512, k), BF16),
            pltpu.VMEM((k, 256), BF16),
            pltpu.VMEM((512, 128), F32),
            pltpu.VMEM((512, 256), F32),
            pltpu.SemaphoreType.DMA((PARTS + 1,)),
            pltpu.SemaphoreType.DMA((len(KEPT),)),
        ],
        compiler_params=pltpu.CompilerParams(vmem_limit_bytes=24 * MIB),
    )(sc, *(far(x) for x in (got, svm, *rest)))


class Sweeps:
    def __init__(self, sc, t1, t2, c, coefs, state, turned):
        self.own, self.odd = place(sc)
        self.fz, self.fr, self.fc, self.inv, self.wgt = coefs
        self.a1, self.a2, self.a3, self.acc = state
        self.turned = turned
        self.thick = [jnp.where(self.own == l // 4, t1[l % 4], t2[l % 4]) for l in range(8)]
        self.rw, self.cw = weights(c)
        lane, _ = lanes()
        self.last, self.first_lane = lane == 127, lane == 0

    def turn(self, k, r, slot=0):
        a = (self.a1, self.a2)[k]
        for l in range(8):
            x, f = a[r, at(l), :], self.fc[r, at(l), :]
            self.turned[k, slot, l] = self.cw * (f * east(x, self.last) + west(f * x, self.first_lane))

    def neighbours(self, k, l, r, slot):
        a = (self.a1, self.a2)[k]
        n = None
        if l < 7:
            n = self.fz[r, at(l), :] * a[r, at(l + 1), :]
        if l > 0:
            t = self.fz[r, at(l - 1), :] * a[r, at(l - 1), :]
            n = t if n is None else n + t
        rows_ = self.fr[r, at(l), :] * a[r + 1, at(l), :] + self.fr[r - 1, at(l), :] * a[r - 1, at(l), :]
        return self.inv[r, at(l), :] * (n + self.rw * rows_ + self.turned[k, slot, l])

    def first(self, r, m):
        for l in range(8):
            self.a1[r, at(l), :] = self.inv[r, at(l), :] * (self.thick[l] * m)

    def second(self, r, slot=0):
        for l in range(8):
            self.a2[r, at(l), :] = 1.3 * self.a1[r, at(l), :] + self.neighbours(0, l, r, slot)

    def third(self, r, slot=0):
        total = None
        for l in range(8):
            y = 0.3 * self.a2[r, at(l), :] + (self.a1[r, at(l), :] + self.neighbours(1, l, r, slot))
            self.a3[pl.ds(pl.multiple_of((r - 2) * 64 + l * 8, 8), 8), :] = y
            total = self.thick[l] * y if l == 0 else total + self.thick[l] * y
        self.acc[row(r - 2), :] = self.wgt[row(r - 2), :] * total

    def interior(self, m):
        for r in (1, EXT - 2):
            self.a1[r] = jnp.zeros((64, 128), F32)

        def stage(p, static):
            for k, back in ((1, 4), (1, 3), (0, 2), (0, 1), (None, 0)):
                q = p - back
                if static and not (2 if k == 1 else 1) <= q <= (31 if k == 1 else 32):
                    continue
                for j in range(2):
                    r = 2 * q + j
                    if back == 4:
                        self.third(r, j)
                    elif back == 2:
                        self.second(r, j)
                    elif back:
                        self.turn(k, r, j)
                    else:
                        self.first(r, m[row(r - 2), :])

        def step(p, carry):
            stage(p, False)
            return carry

        for p in range(1, 6):
            stage(p, True)
        lax.fori_loop(6, 33, step, 0)
        for p in range(33, 36):
            stage(p, True)

    def edges(self, ga, gb):
        up = jnp.where(self.odd == 1, ga[...], gb[...])
        down = jnp.where(self.odd == 1, gb[...], ga[...])
        for ghost, firsts, seconds, thirds in (
            (up, (0, 1), (1, 2), (2, 3)),
            (down, (66, 67), (65, 66), (64, 65)),
        ):
            for i, r in enumerate(firsts):
                self.first(r, ghost[i * 8 : i * 8 + 8, :])
            for r in seconds:
                self.turn(0, r)
                self.second(r)
            for r in thirds:
                self.turn(1, r)
                self.third(r)


def gather_rows(dst, src, first, stride):
    for h in range(0, ROWS, 8):
        for k in range(8):
            dst[pl.ds(h, 8), pl.ds(k * 128, 128)] = src[pl.ds(h * stride + first + k, 8, stride=stride), :]


TURNED = (2, 2, 8, 8, 128)
STATE = (FIELD, FIELD, (ROWS * 64, 128), STRIP)
N_STATE = len(STATE)
STAGE = (4, ROWS, 1024)


def own_kernel(sc, t1, t2, invx_h, wgtx_h, gx, m, *refs):
    coefs, state, (invx, wgtx, turned, sem) = refs[:5], refs[5:9], refs[9:]
    own, _ = place(sc)
    copies = (
        pltpu.make_async_copy(invx_h.at[INSIDE], invx.at[INSIDE], sem.at[0]),
        pltpu.make_async_copy(wgtx_h, wgtx, sem.at[1]),
    )
    for c in copies:
        c.start()
    Sweeps(sc, t1, t2, own, coefs, state, turned).interior(m)
    for c in copies:
        c.wait()
    invx[pl.ds(0, 3)] = gx[pl.ds(0, 3)]
    invx[pl.ds(ROWS + 1, 3)] = gx[pl.ds(3, 3)]


def own_sweeps(sc, t1, t2, invx, wgtx, gx, m, coefs):
    return pl.pallas_call(
        own_kernel,
        in_specs=[sm()] * 3 + [hbm()] * 2 + [vm()] * 7,
        out_specs=[vm()] * 6,
        out_shape=[kept(*s) for s in (*STATE, FIELD, STRIP)],
        scratch_shapes=[pltpu.VMEM(TURNED, F32), pltpu.SemaphoreType.DMA((2,))],
        compiler_params=pltpu.CompilerParams(vmem_limit_bytes=24 * MIB),
    )(sc, t1, t2, far(invx), far(wgtx), *(near(x) for x in (gx, m, *coefs)))


def both_kernel(sc, t1, t2, ga, gb, m, *refs):
    (fz, fr, fc, inv, wgt, invx, wgtx), refs = refs[:7], refs[7 + N_STATE :]
    done, todo, adj, (stage, turned, sem) = refs[:4], refs[4:8], refs[8], refs[9:]
    own, _ = place(sc)
    Sweeps(sc, t1, t2, own, (fz, fr, fc, inv, wgt), done, turned).edges(ga, gb)
    for i in range(4):
        gather_rows(stage.at[i], done[2], (own * 4 + i) * 8, 64)
    copy = pltpu.make_async_copy(stage, adj.at[own], sem)
    copy.start()
    Sweeps(sc, t1, t2, 1 - own, (fz, fr, fc, invx, wgtx), todo, turned).interior(m)
    copy.wait()


def both_sweeps(sc, t1, t2, ga, gb, m, coefs, others, state):
    return pl.pallas_call(
        both_kernel,
        in_specs=[sm()] * 3 + [vm()] * (3 + 7 + N_STATE),
        out_specs=[vm()] * (2 * N_STATE) + [hbm()],
        out_shape=[kept(*s) for s in STATE] * 2 + [pltpu.HBM((2, *STAGE), F32)],
        scratch_shapes=[pltpu.VMEM(STAGE, F32), pltpu.VMEM(TURNED, F32), pltpu.SemaphoreType.DMA],
        input_output_aliases={13 + i: i for i in range(N_STATE)},
        compiler_params=pltpu.CompilerParams(vmem_limit_bytes=24 * MIB),
    )(sc, t1, t2, *(near(x) for x in (ga, gb, m, *coefs, *others, *state)))


def last_kernel(sc, t1, t2, g, racc, fz, fr, fc, inv, wgt, *refs):
    state, (adj, grad), (stage, turned, sem) = refs[5:9], refs[9:11], refs[11:]
    _, _, a3, acc = state
    own, _ = place(sc)
    Sweeps(sc, t1, t2, 1 - own, (fz, fr, fc, inv, wgt), state, turned).edges(
        g.at[pl.ds(0, 16), :], g.at[pl.ds(16, 16), :]
    )
    for i in range(4):
        gather_rows(stage.at[i], a3, (own * 4 + i) * 8, 64)
    copy = pltpu.make_async_copy(stage, adj.at[1 - own], sem)
    copy.start()
    acc[...] = acc[...] + racc[...]
    gather_rows(grad, acc, 0, 8)
    copy.wait()


def last_sweeps(sc, t1, t2, g, racc, coefs, state, adj):
    return pl.pallas_call(
        last_kernel,
        in_specs=[sm()] * 3 + [vm()] * 11 + [hbm()],
        out_specs=[vm()] * 4 + [hbm(), vm()],
        out_shape=[kept(*s) for s in STATE]
        + [pltpu.HBM((2, *STAGE), F32), jax.ShapeDtypeStruct((ROWS, 1024), F32)],
        scratch_shapes=[pltpu.VMEM(STAGE, F32), pltpu.VMEM(TURNED, F32), pltpu.SemaphoreType.DMA],
        input_output_aliases={10: 0, 11: 1, 12: 2, 13: 3, 14: 4},
        compiler_params=pltpu.CompilerParams(vmem_limit_bytes=24 * MIB),
    )(sc, t1, t2, *(near(x) for x in (g, racc, *coefs, *state)), far(adj))[4:]


def swaps(tiles, offset, across):
    perm = []
    for t in range(offset, tiles - 1, 2):
        for layer in range(2):
            a, b = t * 2 + layer, (t + 1) * 2 + (1 - layer if across else layer)
            perm += [(a, b), (b, a)]
    return perm


def swap_layers(x):
    return lax.ppermute(x, "layer", [(0, 1), (1, 0)])


def body(viscosity, friction, base_vel, surf_vel, layer_thick, ice_mask, obs_slots, obs_target):
    tiles = lax.axis_size("tile")
    own = lax.axis_index("layer")
    odd = lax.axis_index("tile") % 2
    sc = (own + 2 * odd).astype(jnp.int32).reshape(1)

    def swap(x, kind, across=False):
        return lax.ppermute(x, PAIR, swaps(tiles, kind, across))

    other = swap_layers(viscosity.astype(BF16))
    payload = pack(sc, obs_slots.reshape(tiles, 128, 128), obs_target)
    got = lax.all_to_all(payload, "tile", split_axis=0, concat_axis=0, tiled=True)
    thick_other = swap_layers(layer_thick)

    to_a, to_b = edge_rows(sc, viscosity, ice_mask, friction)
    near_rows = (swap(to_a, 0), swap(to_b, 1), swap(to_a, 0, True), swap(to_b, 1, True))
    fz, fr, fc, inv, invx, wgt, wgtx, svm, msk, rim, rimd = coefficients(
        sc, viscosity, other, friction, ice_mask, base_vel, surf_vel
    )
    got, near_rows, thick_other = lax.optimization_barrier((got, near_rows, thick_other))
    m_own, ea, eb, msk, rim, rimd, wgt, fz, fr, fc, inv = misfit(
        sc, got, svm, msk, rim, rimd, wgt, fz, fr, fc, inv
    )
    fz, fr, fc, inv, gx = ghosts(sc, *near_rows, msk, rim, rimd, fz, fr, fc, inv)
    th = (sc, layer_thick, thick_other)

    ga, gb = swap(ea, 0), swap(eb, 1)
    m_oth = swap_layers(m_own)
    *state, invx, wgtx = own_sweeps(*th, invx, wgtx, gx, m_own, (fz, fr, fc, inv, wgt))
    g_oth = swap_layers(jnp.concatenate([ga, gb]))
    *both, adj = both_sweeps(*th, ga, gb, m_oth, (fz, fr, fc, inv, wgt), (invx, wgtx), state)
    adjoint, gradient = last_sweeps(*th, g_oth, both[3], (fz, fr, fc, invx, wgtx), both[4:], adj)
    return adjoint, gradient


def solution(mesh):
    in_specs = (
        P("layer", "tile", None),
        P("tile", None),
        P(None, "tile", None),
        P(None, "tile", None),
        P("layer"),
        P("tile", None),
        P("tile", None, None, None),
        P("tile", None),
    )
    out_specs = (P(None, "layer", "tile", None), P("tile", None))

    return jax.shard_map(body, mesh=mesh, in_specs=in_specs, out_specs=out_specs, check_vma=False)
```

time: 88.6 us -> 82.5 us (0.931)
  Pallas kernels: 37.1 us -> 31 us
    pallas_call x3, Pallas kernels: 21.4 us -> 14.7 us  [the longest x1 5.62 us: both_sweeps(): pl.pallas_call(both_kernel, in_specs=[sm()] * 3 + [vm()] * (3 + 7 + N_STA...]
  transfers between devices with their start and end apart: 11 -> 11, of which waited for: 2 -> 2; matrix products, arithmetic and copies ran while one was open for 0% -> 0% of each run, Pallas kernels for 29% -> 25%
where the time goes in v4:
time: 82.5 us; the launch traced here: 82.1 us
  starting transfers between devices  34 us (41%)
  Pallas kernels  31 us (38%)
  waiting for transfers between devices  16.1 us (20%)
  between operations  0.9 us (1%)
    ppermute x6, starting transfers between devices, swap(): return lax.ppermute(x, PAIR, swaps(tiles, kind, across))  18.1 us
    ppermute x4, waiting for transfers between devices, swap_layers(): return lax.ppermute(x, 'layer', [(0, 1), (1, 0)])  13.8 us
    all_to_all x1, starting transfers between devices, body(): lax.all_to_all(payload, 'tile', split_axis=0, concat_axis=0, tiled=True)  11.7 us
    pallas_call x1, Pallas kernels, coefficients(): pl.pallas_call(coef_kernel, in_specs=[sm()] + [vm()] * 6, out_specs=[hbm(...  8.91 us
    pallas_call x1, Pallas kernels, both_sweeps(): pl.pallas_call(both_kernel, in_specs=[sm()] * 3 + [vm()] * (3 + 7 + N_STA...  5.62 us
    pallas_call x1, Pallas kernels, own_sweeps(): pl.pallas_call(own_kernel, in_specs=[sm()] * 3 + [hbm()] * 2 + [vm()] * 7...  4.88 us
    ppermute x4, starting transfers between devices, swap_layers(): return lax.ppermute(x, 'layer', [(0, 1), (1, 0)])  4.22 us
    pallas_call x1, Pallas kernels, misfit(): pl.pallas_call(misfit_kernel, in_specs=[sm()] + [hbm()] * (2 + len(KEPT))...  4.18 us
  transfers between devices with their start and end apart: 11, of which 2 were waited for; matrix products, arithmetic and copies ran while one was open for 0% of the time, Pallas kernels for 25%

profile of v4, /device:TPU:2, one launch (start us, length us, event | category | flops | bytes accessed | tf_op | source)
XLA Modules:
  0.0 82.1 jit_solution(11310760390875188094)
XLA Ops:
  0.6 0.0 copy-start
  0.7 2.8 %shard_map.95 = bf16[64,72,128]{2,1,0:T(8,128)(2,1)} custom-call(s32[1]{0:T(128)} %bitcast.sc, bf16[64,128,128]{2,1,0:T(8,128)(2,1)} %bitcast.2, s32[64,64]{1,0:T(8,128)} %target.1), custom_call_target="tpu_custom_call" | custom-call | tf_op jit(solution)/shard_map/pallas_call | solution.py:114
  3.5 0.0 copy-start.6
  3.5 0.0 copy-start.1
  3.5 0.0 copy-start.2
  3.5 0.0 copy-start.3
  3.6 0.0 copy-start.4
  3.6 11.7 %all-to-all-start = ((bf16[64,72,128]{2,1,0:T(8,128)(2,1)}), bf16[64,72,128]{2,1,0:T(8,128)(2,1)}, u32[]{:S(2)}, u32[]{:S(2)}) async-start(bf16[64,72,128]{2,1,0:T(8,128)(2,1)} %shard_map.95), calls=%async_computation | async-start | bytes 2359296 | tf_op jit(solution)/shard_map/all_to_all | solution.py:606
  15.2 0.0 copy-start.5
  15.3 0.1 convert_element_type.3
  15.3 1.1 %collective-permute-start.5 = (bf16[4,64,1024]{2,1,0:T(8,128)(2,1)S(1)}, bf16[4,64,1024]{2,1,0:T(8,128)(2,1)S(1)}, u32[]{:S(2)}, u32[]{:S(2)}) collective-permute-start(bf16[4,64,1024]{2,1,0:T(8,128)(2,1)S(1)} %convert_element_type.3), channel_id=1, source_target_pairs={{0,1},{1,0},{2,3},{3,2},{4,5},{5,4},{6,7},{7,6},{8,9},{9,8},{10,11... | collective-permute-start | bytes 1572872 | tf_op jit(solution)/shard_map/ppermute | solution.py:592
  16.4 1.1 %shard_map.96 = (bf16[16,1024]{1,0:T(8,128)(2,1)S(1)}, bf16[16,1024]{1,0:T(8,128)(2,1)S(1)}) custom-call(s32[1]{0:T(128)} %bitcast.sc, f32[4,64,1024]{2,1,0:T(8,128)} %visc.3, s32[64,1024]{1,0:T(8,128)} %mask.3, f32[64,1024]{1,0:T(8,128)} %fric.3), custom_call_target="tpu_custom_call" | custom-call | tf_op jit(solution)/shard_map/pallas_call | solution.py:155
  17.5 0.1 collective-permute-start
  17.6 7.7 %collective-permute-start.1 = (bf16[16,1024]{1,0:T(8,128)(2,1)S(1)}, bf16[16,1024]{1,0:T(8,128)(2,1)S(1)}, u32[]{:S(2)}, u32[]{:S(2)}) collective-permute-start(bf16[16,1024]{1,0:T(8,128)(2,1)S(1)} %get-tuple-element.52), channel_id=1, source_target_pairs={{2,4},{4,2},{3,5},{5,3},{6,8},{8,6},{7,9},{9,7},{10,12},{12,10},{1... | collective-permute-start | bytes 98312 | tf_op jit(solution)/shard_map/ppermute | solution.py:602
  25.3 0.1 collective-permute-start.2
  25.4 3.0 %collective-permute-start.3 = (bf16[16,1024]{1,0:T(8,128)(2,1)S(1)}, bf16[16,1024]{1,0:T(8,128)(2,1)S(1)}, u32[]{:S(2)}, u32[]{:S(2)}) collective-permute-start(bf16[16,1024]{1,0:T(8,128)(2,1)S(1)} %get-tuple-element.52), channel_id=1, source_target_pairs={{2,5},{5,2},{3,4},{4,3},{6,9},{9,6},{7,8},{8,7},{10,13},{13,10},{1... | collective-permute-start | bytes 98312 | tf_op jit(solution)/shard_map/ppermute | solution.py:602
  28.5 13.8 %collective-permute-done.5.other = bf16[4,64,1024]{2,1,0:T(8,128)(2,1)S(1)} collective-permute-done((bf16[4,64,1024]{2,1,0:T(8,128)(2,1)S(1)}, bf16[4,64,1024]{2,1,0:T(8,128)(2,1)S(1)}, u32[]{:S(2)}, u32[]{:S(2)}) %collective-permute-start.5) | collective-permute-done | bytes 524320 | tf_op jit(solution)/shard_map/ppermute | solution.py:592
  42.3 1.0 %collective-permute-start.4 = (f32[4]{0:T(128)S(1)}, f32[4]{0:T(128)S(1)}, u32[]{:S(2)}, u32[]{:S(2)}) collective-permute-start(f32[4]{0:T(128)S(1)} %copy-done.6), channel_id=1, source_target_pairs={{0,1},{1,0},{2,3},{3,2},{4,5},{5,4},{6,7},{7,6},{8,9},{9,8},{10,11... | collective-permute-start | bytes 56 | tf_op jit(solution)/shard_map/ppermute | solution.py:592
  43.3 8.9 %shard_map.97 = (f32[68,64,128]{2,1,0:T(8,128)}, f32[68,64,128]{2,1,0:T(8,128)}, f32[68,64,128]{2,1,0:T(8,128)}, f32[68,64,128]{2,1,0:T(8,128)}, f32[68,64,128]{...) custom-call(s32[1]{0:T(128)} %bitcast.sc, ...), custom_call_target="tpu_custom_call" | custom-call | tf_op jit(solution)/shard_map/pallas_call | solution.py:270
  52.2 0.0 collective-permute-done.ea
  52.3 0.0 collective-permute-done.3.eb2
  52.3 0.0 all-to-all-done.got_h
  52.3 4.2 %shard_map.98 = (f32[512,128]{1,0:T(8,128)S(1)}, f32[16,128]{1,0:T(8,128)S(1)}, f32[16,128]{1,0:T(8,128)S(1)}, f32[512,128]{1,0:T(8,128)S(1)}, f32[8,32,128]{2,1...) custom-call(s32[1]{0:T(128)} %bitcast.sc, ...), custom_call_target="tpu_custom_call" | custom-call | tf_op jit(solution)/shard_map/pallas_call | solution.py:379
  56.5 1.1 %collective-permute-start.9 = (f32[512,128]{1,0:T(8,128)S(1)}, f32[512,128]{1,0:T(8,128)S(1)}, u32[]{:S(2)}, u32[]{:S(2)}) collective-permute-start(f32[512,128]{1,0:T(8,128)S(1)} %get-tuple-element.66.m), channel_id=1, source_target_pairs={{0,1},{1,0},{2,3},{3,2},{4,5},{5,4},{6,7},{7,6},{8,9},{9,8},{10,11... | collective-permute-start | bytes 786440 | tf_op jit(solution)/shard_map/ppermute | solution.py:592
  57.6 0.0 collective-permute-start.6
  57.6 7.2 %collective-permute-start.7 = (f32[16,128]{1,0:T(8,128)S(1)}, f32[16,128]{1,0:T(8,128)S(1)}, u32[]{:S(2)}, u32[]{:S(2)}) collective-permute-start(f32[16,128]{1,0:T(8,128)S(1)} %get-tuple-element.65), channel_id=1, source_target_pairs={{2,4},{4,2},{3,5},{5,3},{6,8},{8,6},{7,9},{9,7},{10,12},{12,10},{1... | collective-permute-start | bytes 24584 | tf_op jit(solution)/shard_map/ppermute | solution.py:602
  64.8 2.2 %collective-permute-done.7.gb = f32[16,128]{1,0:T(8,128)S(1)} collective-permute-done((f32[16,128]{1,0:T(8,128)S(1)}, f32[16,128]{1,0:T(8,128)S(1)}, u32[]{:S(2)}, u32[]{:S(2)}) %collective-permute-start.7) | collective-permute-done | bytes 8224 | tf_op jit(solution)/shard_map/ppermute | solution.py:602
  67.0 1.0 %collective-permute-start.8 = (f32[32,128]{1,0:T(8,128)S(1)}, f32[32,128]{1,0:T(8,128)S(1)}, u32[]{:S(2)}, u32[]{:S(2)}) collective-permute-start(f32[32,128]{1,0:T(8,128)S(1)} %pad_maximum_fusion), channel_id=1, source_target_pairs={{0,1},{1,0},{2,3},{3,2},{4,5},{5,4},{6,7},{7,6},{8,9},{9,8},{10,11... | collective-permute-start | bytes 49160 | tf_op jit(solution)/shard_map/ppermute | solution.py:592
  68.1 0.3 shard_map.99
  68.4 4.9 %shard_map.100 = (f32[68,64,128]{2,1,0:T(8,128)S(1)}, f32[68,64,128]{2,1,0:T(8,128)S(1)}, f32[4096,128]{1,0:T(8,128)S(1)}, f32[512,128]{1,0:T(8,128)S(1)}, f32[6...) custom-call(s32[1]{0:T(128)} %bitcast.sc, f32[4]{0:T(128)S(1)} %copy-done.6, f32[4]{0:T(128)S(1)} %collective-permute-done.4.t2, ...), custom_call_target="tpu_custom_call" | custom-call | tf_op jit(solution)/shard_map/pallas_call | solution.py:518
  73.3 5.6 %shard_map.101 = (f32[68,64,128]{2,1,0:T(8,128)S(1)}, f32[68,64,128]{2,1,0:T(8,128)S(1)}, f32[4096,128]{1,0:T(8,128)S(1)}, f32[512,128]{1,0:T(8,128)S(1)}, f32[6...) custom-call(s32[1]{0:T(128)} %bitcast.sc, ...), custom_call_target="tpu_custom_call", output_to_operand_aliasing={{0}: (13, {}), {1}: (14, {}), {2}: (15, {}), {3}: (16, {})} | custom-call | tf_op jit(solution)/shard_map/pallas_call | solution.py:542
  78.9 3.1 %shard_map.102 = (f32[68,64,128]{2,1,0:T(8,128)S(1)}, f32[68,64,128]{2,1,0:T(8,128)S(1)}, f32[4096,128]{1,0:T(8,128)S(1)}, f32[512,128]{1,0:T(8,128)S(1)}, f32[2...) custom-call(s32[1]{0:T(128)} %bitcast.sc, ...), custom_call_target="tpu_custom_call", output_to_operand_aliasing={{0}: (10, {}), {1}: (11, {}), {2}: (12, {}), {3}: (13, {}),... | custom-call | tf_op jit(solution)/shard_map/pallas_call | solution.py:570
  (14 shorter events, 0.0 us)
Async XLA Ops:
  0.6 14.6 %copy-start = (f32[4,64,1024]{2,1,0:T(8,128)S(1)}, f32[4,64,1024]{2,1,0:T(8,128)}, u32[]{:S(2)}) copy-start(f32[4,64,1024]{2,1,0:T(8,128)} %visc.3) | copy-start | bytes 3145732
  3.5 38.7 %copy-start.6 = (f32[4]{0:T(128)S(1)}, f32[4]{0:T(128)}, u32[]{:S(2)}) copy-start(f32[4]{0:T(128)} %t1.5) | copy-start | bytes 52
  3.5 39.8 %copy-start.1 = (f32[4,64,1024]{2,1,0:T(8,128)S(1)}, f32[4,64,1024]{2,1,0:T(8,128)}, u32[]{:S(2)}) copy-start(f32[4,64,1024]{2,1,0:T(8,128)} %visc.3) | copy-start | bytes 3145732
  3.5 39.7 %copy-start.2 = (f32[64,1024]{1,0:T(8,128)S(1)}, f32[64,1024]{1,0:T(8,128)}, u32[]{:S(2)}) copy-start(f32[64,1024]{1,0:T(8,128)} %fric.3) | copy-start | bytes 786436
  3.5 39.7 %copy-start.3 = (s32[64,1024]{1,0:T(8,128)S(1)}, s32[64,1024]{1,0:T(8,128)}, u32[]{:S(2)}) copy-start(s32[64,1024]{1,0:T(8,128)} %mask.3) | copy-start | bytes 786436
  3.6 39.7 %copy-start.4 = (f32[2,64,1024]{2,1,0:T(8,128)S(1)}, f32[2,64,1024]{2,1,0:T(8,128)}, u32[]{:S(2)}) copy-start(f32[2,64,1024]{2,1,0:T(8,128)} %bvel.1) | copy-start | bytes 1572868
  3.6 48.7 %all-to-all-start = ((bf16[64,72,128]{2,1,0:T(8,128)(2,1)}), bf16[64,72,128]{2,1,0:T(8,128)(2,1)}, u32[]{:S(2)}, u32[]{:S(2)}) async-start(bf16[64,72,128]{2,1,0:T(8,128)(2,1)} %shard_map.95), calls=%async_computation | async-start | bytes 2359296 | tf_op jit(solution)/shard_map/all_to_all | solution.py:606
  15.2 28.1 %copy-start.5 = (f32[2,64,1024]{2,1,0:T(8,128)S(1)}, f32[2,64,1024]{2,1,0:T(8,128)}, u32[]{:S(2)}) copy-start(f32[2,64,1024]{2,1,0:T(8,128)} %svel.1) | copy-start | bytes 1572868
  15.3 26.9 %collective-permute-start.5 = (bf16[4,64,1024]{2,1,0:T(8,128)(2,1)S(1)}, bf16[4,64,1024]{2,1,0:T(8,128)(2,1)S(1)}, u32[]{:S(2)}, u32[]{:S(2)}) collective-permute-start(bf16[4,64,1024]{2,1,0:T(8,128)(2,1)S(1)} %convert_element_type.3), channel_id=1, source_target_pairs={{0,1},{1,0},{2,3},{3,2},{4,5},{5,4},{6,7},{7,6},{8,9},{9,8},{10,11... | collective-permute-start | bytes 1572872 | tf_op jit(solution)/shard_map/ppermute | solution.py:592
  17.5 34.7 %collective-permute-start = (bf16[16,1024]{1,0:T(8,128)(2,1)S(1)}, bf16[16,1024]{1,0:T(8,128)(2,1)S(1)}, u32[]{:S(2)}, u32[]{:S(2)}) collective-permute-start(bf16[16,1024]{1,0:T(8,128)(2,1)S(1)} %get-tuple-element.51), channel_id=1, source_target_pairs={{0,2},{2,0},{1,3},{3,1},{4,6},{6,4},{5,7},{7,5},{8,10},{10,8},{9,1... | collective-permute-start | bytes 98312 | tf_op jit(solution)/shard_map/ppermute | solution.py:602
  17.6 34.6 %collective-permute-start.1 = (bf16[16,1024]{1,0:T(8,128)(2,1)S(1)}, bf16[16,1024]{1,0:T(8,128)(2,1)S(1)}, u32[]{:S(2)}, u32[]{:S(2)}) collective-permute-start(bf16[16,1024]{1,0:T(8,128)(2,1)S(1)} %get-tuple-element.52), channel_id=1, source_target_pairs={{2,4},{4,2},{3,5},{5,3},{6,8},{8,6},{7,9},{9,7},{10,12},{12,10},{1... | collective-permute-start | bytes 98312 | tf_op jit(solution)/shard_map/ppermute | solution.py:602
  25.3 26.9 %collective-permute-start.2 = (bf16[16,1024]{1,0:T(8,128)(2,1)S(1)}, bf16[16,1024]{1,0:T(8,128)(2,1)S(1)}, u32[]{:S(2)}, u32[]{:S(2)}) collective-permute-start(bf16[16,1024]{1,0:T(8,128)(2,1)S(1)} %get-tuple-element.51), channel_id=1, source_target_pairs={{0,3},{3,0},{1,2},{2,1},{4,7},{7,4},{5,6},{6,5},{8,11},{11,8},{9,1... | collective-permute-start | bytes 98312 | tf_op jit(solution)/shard_map/ppermute | solution.py:602
  25.4 26.8 %collective-permute-start.3 = (bf16[16,1024]{1,0:T(8,128)(2,1)S(1)}, bf16[16,1024]{1,0:T(8,128)(2,1)S(1)}, u32[]{:S(2)}, u32[]{:S(2)}) collective-permute-start(bf16[16,1024]{1,0:T(8,128)(2,1)S(1)} %get-tuple-element.52), channel_id=1, source_target_pairs={{2,5},{5,2},{3,4},{4,3},{6,9},{9,6},{7,8},{8,7},{10,13},{13,10},{1... | collective-permute-start | bytes 98312 | tf_op jit(solution)/shard_map/ppermute | solution.py:602
  42.3 10.0 %collective-permute-start.4 = (f32[4]{0:T(128)S(1)}, f32[4]{0:T(128)S(1)}, u32[]{:S(2)}, u32[]{:S(2)}) collective-permute-start(f32[4]{0:T(128)S(1)} %copy-done.6), channel_id=1, source_target_pairs={{0,1},{1,0},{2,3},{3,2},{4,5},{5,4},{6,7},{7,6},{8,9},{9,8},{10,11... | collective-permute-start | bytes 56 | tf_op jit(solution)/shard_map/ppermute | solution.py:592
  56.5 16.8 %collective-permute-start.9 = (f32[512,128]{1,0:T(8,128)S(1)}, f32[512,128]{1,0:T(8,128)S(1)}, u32[]{:S(2)}, u32[]{:S(2)}) collective-permute-start(f32[512,128]{1,0:T(8,128)S(1)} %get-tuple-element.66.m), channel_id=1, source_target_pairs={{0,1},{1,0},{2,3},{3,2},{4,5},{5,4},{6,7},{7,6},{8,9},{9,8},{10,11... | collective-permute-start | bytes 786440 | tf_op jit(solution)/shard_map/ppermute | solution.py:592
  57.6 7.2 %collective-permute-start.6 = (f32[16,128]{1,0:T(8,128)S(1)}, f32[16,128]{1,0:T(8,128)S(1)}, u32[]{:S(2)}, u32[]{:S(2)}) collective-permute-start(f32[16,128]{1,0:T(8,128)S(1)} %get-tuple-element.64), channel_id=1, source_target_pairs={{0,2},{2,0},{1,3},{3,1},{4,6},{6,4},{5,7},{7,5},{8,10},{10,8},{9,1... | collective-permute-start | bytes 24584 | tf_op jit(solution)/shard_map/ppermute | solution.py:602
  57.6 9.5 %collective-permute-start.7 = (f32[16,128]{1,0:T(8,128)S(1)}, f32[16,128]{1,0:T(8,128)S(1)}, u32[]{:S(2)}, u32[]{:S(2)}) collective-permute-start(f32[16,128]{1,0:T(8,128)S(1)} %get-tuple-element.65), channel_id=1, source_target_pairs={{2,4},{4,2},{3,5},{5,3},{6,8},{8,6},{7,9},{9,7},{10,12},{12,10},{1... | collective-permute-start | bytes 24584 | tf_op jit(solution)/shard_map/ppermute | solution.py:602
  67.0 11.9 %collective-permute-start.8 = (f32[32,128]{1,0:T(8,128)S(1)}, f32[32,128]{1,0:T(8,128)S(1)}, u32[]{:S(2)}, u32[]{:S(2)}) collective-permute-start(f32[32,128]{1,0:T(8,128)S(1)} %pad_maximum_fusion), channel_id=1, source_target_pairs={{0,1},{1,0},{2,3},{3,2},{4,5},{5,4},{6,7},{7,6},{8,9},{9,8},{10,11... | collective-permute-start | bytes 49160 | tf_op jit(solution)/shard_map/ppermute | solution.py:592

commit v5 on v4

--- a/solution.py
+++ b/solution.py
@@ -10,7 +10,6 @@
 BF16 = jnp.bfloat16
 ROWS = 64
 EXT = 68
-PAIR = ("tile", "layer")
 FIELD = (EXT, 64, 128)
 STRIP = (ROWS * 8, 128)
 MIB = 1 << 20
@@ -72,8 +71,11 @@
     return jnp.where(t < 512, (128 + (t & 127)) << (t >> 7), 0)
 
 
-def pack_kernel(sc, slots, target, o, x, y, t, f, codes, sin, sout, st):
+def pack_kernel(sc, slots, target, visc, o, narrow, x, y, t, f, codes, vx, vy, sin, sout, st, vin, vout):
     own, _ = place(sc)
+    layers = visc.shape[0]
+    takes = [pltpu.make_async_copy(visc.at[i], vx.at[i], vin.at[i]) for i in range(layers)]
+    gives = [pltpu.make_async_copy(vy.at[i], narrow.at[i], vout.at[i]) for i in range(layers)]
     n = slots.shape[0]
     step = n // CHUNKS
     tin = pltpu.make_async_copy(target, t, st)
@@ -86,8 +88,12 @@
         pltpu.make_async_copy(y.at[pl.ds(i * step, step)], o.at[pl.ds(i * step, step)], sout.at[i])
         for i in range(CHUNKS)
     ]
-    for i in ins:
+    for i in (*takes, *ins):
         i.start()
+    for i in range(layers):
+        takes[i].wait()
+        vy[i] = vx[i].astype(BF16)
+        gives[i].start()
     tin.wait()
     c = code_of(t[...]).astype(F32)
     codes[...] = jnp.concatenate([c, c], axis=1)
@@ -102,32 +108,36 @@
 
         lax.fori_loop(i * step, (i + 1) * step, one, 0, unroll=8)
         outs[i].start()
-    for i in outs:
+    for i in (*gives, *outs):
         i.wait()
 
 
-CHUNKS = 4
-
-
-def pack(sc, slots, target):
+CHUNKS = 8
+
+
+def pack(sc, slots, target, visc):
     n = slots.shape[0]
     return pl.pallas_call(
         pack_kernel,
-        in_specs=[sm(), hbm(), hbm()],
-        out_specs=hbm(),
-        out_shape=pltpu.HBM((n, 72, 128), BF16),
+        in_specs=[sm(), hbm(), hbm(), hbm()],
+        out_specs=[hbm(), hbm()],
+        out_shape=[pltpu.HBM((n, 72, 128), BF16), pltpu.HBM(visc.shape, BF16)],
         scratch_shapes=[
             pltpu.VMEM((n, 128, 128), BF16),
             pltpu.VMEM((n, 72, 128), BF16),
             pltpu.VMEM((n, 64), jnp.int32),
             pltpu.VMEM((n, 128, 128), F32),
             pltpu.VMEM((n, 128), F32),
+            pltpu.VMEM(visc.shape, F32),
+            pltpu.VMEM(visc.shape, BF16),
             pltpu.SemaphoreType.DMA((CHUNKS,)),
             pltpu.SemaphoreType.DMA((CHUNKS,)),
             pltpu.SemaphoreType.DMA,
+            pltpu.SemaphoreType.DMA((visc.shape[0],)),
+            pltpu.SemaphoreType.DMA((visc.shape[0],)),
         ],
         compiler_params=pltpu.CompilerParams(vmem_limit_bytes=16 * MIB),
-    )(sc, far(slots), far(target))
+    )(sc, far(slots), far(target), far(visc))
 
 
 def edge_kernel(sc, visc, mask, fric, to_a, to_b, v, m, d, s, sem):
@@ -204,7 +214,7 @@
         prev = above
 
 
-GROUPS = ((3, 16), (16, 32), (32, 48), (48, 65))
+GROUPS = ((3, 16), (16, 32), (32, 48), (48, 60), (60, 65))
 INSIDE = pl.ds(3, 62)
 RIM = (8, 32, 128)
 N_FIELDS = 5
@@ -284,10 +294,10 @@
     )(sc, visc, other, fric, mask, bvel, svel)
 
 
-def ghost_kernel(sc, ea, eb, ea2, eb2, msk, rim, rimd, fz0, fr0, fc0, inv0, fz, fr, fc, inv, gx, g, u):
+def ghost_kernel(sc, ea, eb, relayed, msk, rim, rimd, fz0, fr0, fc0, inv0, fz, fr, fc, inv, gx, g, u):
     own, odd = place(sc)
     pairs = (weights(own), weights(1 - own))
-    for kind, pair in enumerate(((ea, ea2), (eb, eb2))):
+    for kind, pair in enumerate(((ea, relayed.at[pl.ds(0, 16)]), (eb, relayed.at[pl.ds(16, 16)]))):
         side = jnp.where((odd + kind) % 2 == 1, 0, 1)
         for who, e in enumerate(pair):
             spread(g.at[side, who], 0, e[...].astype(F32))
@@ -312,16 +322,16 @@
             coefficient_row(lambda l, s: u[side, l, row(j + 1 + s), :], m > 0.5, d, r, pairs, fz, fr, fc, invs)
 
 
-def ghosts(sc, ea, eb, ea2, eb2, msk, rim, rimd, fz, fr, fc, inv):
+def ghosts(sc, ea, eb, relayed, msk, rim, rimd, fz, fr, fc, inv):
     return pl.pallas_call(
         ghost_kernel,
-        in_specs=[sm()] + [vm()] * 11,
+        in_specs=[sm()] + [vm()] * 10,
         out_specs=[vm()] * 5,
         out_shape=[kept(*FIELD)] * 4 + [kept(6, 64, 128)],
         scratch_shapes=[pltpu.VMEM((2, 2, 128, 128), F32), pltpu.VMEM((2, 8, 40, 128), F32)],
-        input_output_aliases={8: 0, 9: 1, 10: 2, 11: 3},
+        input_output_aliases={7: 0, 8: 1, 9: 2, 10: 3},
         compiler_params=pltpu.CompilerParams(vmem_limit_bytes=24 * MIB),
-    )(sc, *(near(x) for x in (ea, eb, ea2, eb2, msk, rim, rimd, fz, fr, fc, inv)))
+    )(sc, *(near(x) for x in (ea, eb, relayed, msk, rim, rimd, fz, fr, fc, inv)))
 
 
 PARTS = 4
@@ -330,7 +340,7 @@
 def misfit_kernel(sc, got_h, svm_h, *refs):
     n_kept = len(KEPT)
     here, (m_out, ea, eb), refs = refs[:n_kept], refs[n_kept : n_kept + 3], refs[n_kept + 3 :]
-    kept_, (got, svm, hot, rhs, pc, acc, sem, sem2) = refs[:n_kept], refs[n_kept:]
+    kept_, (got, svm, hot, rhs, pc, sem, sem2) = refs[:n_kept], refs[n_kept:]
     _, odd = place(sc)
     n = got.shape[0] // PARTS
     parts = [
@@ -349,20 +359,20 @@
     pc[...] = code_of(p).astype(F32)
     rhs[:, pl.ds(128, 128)] = jnp.ones((rhs.shape[0], 128), BF16)
     lane = lax.broadcasted_iota(jnp.int32, (8, 128), 1)
+    for part in parts:
+        part.wait()
     for part in range(PARTS):
-        parts[part].wait()
         for b in range(n // 2):
             s = part * n + 2 * b
             for h in range(2):
-                rhs[pl.ds((2 * b + h) * 64, 64), pl.ds(0, 128)] = got[s + h, pl.ds(0, 64), :]
+                rhs[pl.ds((s + h) * 64, 64), pl.ds(0, 128)] = got[s + h, pl.ds(0, 64), :]
             c = jnp.where(lane < 64, got[s, pl.ds(64, 8), :].astype(F32), got[s + 1, pl.ds(64, 8), :].astype(F32))
             same = pc[...].reshape(64, 8, 128) == c[None]
-            hot[:, pl.ds(b * 128, 128)] = jnp.where(same, 1.0, 0.0).reshape(512, 128).astype(BF16)
-        sums = jnp.dot(hot[...], rhs[...], preferred_element_type=F32)
-        acc[...] = sums if part == 0 else acc[...] + sums
+            hot[:, pl.ds(s * 64, 128)] = jnp.where(same, 1.0, 0.0).reshape(512, 128).astype(BF16)
+    sums = jnp.dot(hot[...], rhs[...], preferred_element_type=F32)
     strips.wait()
     rest[0].wait()
-    m_out[...] = acc[:, 128:] * svm[...] - msk[...] * acc[:, :128]
+    m_out[...] = sums[:, 128:] * svm[...] - msk[...] * sums[:, :128]
     for kind, e in enumerate((ea, eb)):
         start = jnp.where((odd + kind) % 2 == 0, ROWS - 2, 0)
         for r in range(2):
@@ -375,7 +385,7 @@
 
 
 def misfit(sc, got, svm, *rest):
-    k = got.shape[0] // PARTS * 64
+    k = got.shape[0] * 64
     return pl.pallas_call(
         misfit_kernel,
         in_specs=[sm()] + [hbm()] * (2 + len(KEPT)),
@@ -387,7 +397,6 @@
             pltpu.VMEM((512, k), BF16),
             pltpu.VMEM((k, 256), BF16),
             pltpu.VMEM((512, 128), F32),
-            pltpu.VMEM((512, 256), F32),
             pltpu.SemaphoreType.DMA((PARTS + 1,)),
             pltpu.SemaphoreType.DMA((len(KEPT),)),
         ],
@@ -435,7 +444,7 @@
         total = None
         for l in range(8):
             y = 0.3 * self.a2[r, at(l), :] + (self.a1[r, at(l), :] + self.neighbours(1, l, r, slot))
-            self.a3[pl.ds(pl.multiple_of((r - 2) * 64 + l * 8, 8), 8), :] = y
+            self.a3[l, row(r - 2), :] = y
             total = self.thick[l] * y if l == 0 else total + self.thick[l] * y
         self.acc[row(r - 2), :] = self.wgt[row(r - 2), :] * total
 
@@ -486,14 +495,17 @@
                 self.third(r)
 
 
-def gather_rows(dst, src, first, stride):
-    for h in range(0, ROWS, 8):
+INNER, OUTER = range(8, ROWS - 8, 8), (0, ROWS - 8)
+
+
+def gather_rows(dst, src, rows=range(0, ROWS, 8)):
+    for h in rows:
         for k in range(8):
-            dst[pl.ds(h, 8), pl.ds(k * 128, 128)] = src[pl.ds(h * stride + first + k, 8, stride=stride), :]
+            dst[pl.ds(h, 8), pl.ds(k * 128, 128)] = src[pl.ds(h * 8 + k, 8, stride=8), :]
 
 
 TURNED = (2, 2, 8, 8, 128)
-STATE = (FIELD, FIELD, (ROWS * 64, 128), STRIP)
+STATE = (FIELD, FIELD, (8, (ROWS + 1) * 8, 128), STRIP)
 N_STATE = len(STATE)
 STAGE = (4, ROWS, 1024)
 
@@ -531,7 +543,7 @@
     own, _ = place(sc)
     Sweeps(sc, t1, t2, own, (fz, fr, fc, inv, wgt), done, turned).edges(ga, gb)
     for i in range(4):
-        gather_rows(stage.at[i], done[2], (own * 4 + i) * 8, 64)
+        gather_rows(stage.at[i], done[2].at[own * 4 + i])
     copy = pltpu.make_async_copy(stage, adj.at[own], sem)
     copy.start()
     Sweeps(sc, t1, t2, 1 - own, (fz, fr, fc, invx, wgtx), todo, turned).interior(m)
@@ -551,40 +563,58 @@
 
 
 def last_kernel(sc, t1, t2, g, racc, fz, fr, fc, inv, wgt, *refs):
-    state, (adj, grad), (stage, turned, sem) = refs[5:9], refs[9:11], refs[11:]
+    state, (adj, grad), (stage, sum_, turned, sem) = refs[5:9], refs[9:11], refs[11:]
     _, _, a3, acc = state
     own, _ = place(sc)
+    to = adj.at[1 - own]
+    spans = (pl.ds(8, ROWS - 16), pl.ds(0, 8), pl.ds(ROWS - 8, 8))
+    copies = [pltpu.make_async_copy(stage.at[:, x, :], to.at[:, x, :], sem.at[i]) for i, x in enumerate(spans)]
+    copies += [pltpu.make_async_copy(sum_.at[x, :], grad.at[x, :], sem.at[3 + i]) for i, x in enumerate(spans)]
+    for i in range(4):
+        gather_rows(stage.at[i], a3.at[own * 4 + i], INNER)
+    copies[0].start()
+    for r in INNER:
+        acc[pl.ds(r * 8, 64), :] = acc[pl.ds(r * 8, 64), :] + racc[pl.ds(r * 8, 64), :]
+    gather_rows(sum_, acc, INNER)
+    copies[3].start()
     Sweeps(sc, t1, t2, 1 - own, (fz, fr, fc, inv, wgt), state, turned).edges(
         g.at[pl.ds(0, 16), :], g.at[pl.ds(16, 16), :]
     )
     for i in range(4):
-        gather_rows(stage.at[i], a3, (own * 4 + i) * 8, 64)
-    copy = pltpu.make_async_copy(stage, adj.at[1 - own], sem)
-    copy.start()
-    acc[...] = acc[...] + racc[...]
-    gather_rows(grad, acc, 0, 8)
-    copy.wait()
+        gather_rows(stage.at[i], a3.at[own * 4 + i], OUTER)
+    copies[1].start()
+    copies[2].start()
+    for r in OUTER:
+        acc[pl.ds(r * 8, 64), :] = acc[pl.ds(r * 8, 64), :] + racc[pl.ds(r * 8, 64), :]
+    gather_rows(sum_, acc, OUTER)
+    copies[4].start()
+    copies[5].start()
+    for c in copies:
+        c.wait()
 
 
 def last_sweeps(sc, t1, t2, g, racc, coefs, state, adj):
     return pl.pallas_call(
         last_kernel,
         in_specs=[sm()] * 3 + [vm()] * 11 + [hbm()],
-        out_specs=[vm()] * 4 + [hbm(), vm()],
+        out_specs=[vm()] * 4 + [hbm(), hbm()],
         out_shape=[kept(*s) for s in STATE]
-        + [pltpu.HBM((2, *STAGE), F32), jax.ShapeDtypeStruct((ROWS, 1024), F32)],
-        scratch_shapes=[pltpu.VMEM(STAGE, F32), pltpu.VMEM(TURNED, F32), pltpu.SemaphoreType.DMA],
+        + [pltpu.HBM((2, *STAGE), F32), pltpu.HBM((ROWS, 1024), F32)],
+        scratch_shapes=[
+            pltpu.VMEM(STAGE, F32),
+            pltpu.VMEM((ROWS, 1024), F32),
+            pltpu.VMEM(TURNED, F32),
+            pltpu.SemaphoreType.DMA((6,)),
+        ],
         input_output_aliases={10: 0, 11: 1, 12: 2, 13: 3, 14: 4},
         compiler_params=pltpu.CompilerParams(vmem_limit_bytes=24 * MIB),
     )(sc, t1, t2, *(near(x) for x in (g, racc, *coefs, *state)), far(adj))[4:]
 
 
-def swaps(tiles, offset, across):
+def swaps(tiles, offset):
     perm = []
     for t in range(offset, tiles - 1, 2):
-        for layer in range(2):
-            a, b = t * 2 + layer, (t + 1) * 2 + (1 - layer if across else layer)
-            perm += [(a, b), (b, a)]
+        perm += [(t, t + 1), (t + 1, t)]
     return perm
 
 
@@ -598,16 +628,17 @@
     odd = lax.axis_index("tile") % 2
     sc = (own + 2 * odd).astype(jnp.int32).reshape(1)
 
-    def swap(x, kind, across=False):
-        return lax.ppermute(x, PAIR, swaps(tiles, kind, across))
-
-    other = swap_layers(viscosity.astype(BF16))
-    payload = pack(sc, obs_slots.reshape(tiles, 128, 128), obs_target)
+    def swap(x, kind):
+        return lax.ppermute(x, "tile", swaps(tiles, kind))
+
+    payload, narrow = pack(sc, obs_slots.reshape(tiles, 128, 128), obs_target, viscosity)
+    other = swap_layers(narrow)
     got = lax.all_to_all(payload, "tile", split_axis=0, concat_axis=0, tiled=True)
     thick_other = swap_layers(layer_thick)
 
     to_a, to_b = edge_rows(sc, viscosity, ice_mask, friction)
-    near_rows = (swap(to_a, 0), swap(to_b, 1), swap(to_a, 0, True), swap(to_b, 1, True))
+    near_rows = (swap(to_a, 0), swap(to_b, 1))
+    relayed = swap_layers(jnp.concatenate(near_rows))
     fz, fr, fc, inv, invx, wgt, wgtx, svm, msk, rim, rimd = coefficients(
         sc, viscosity, other, friction, ice_mask, base_vel, surf_vel
     )
@@ -615,7 +646,7 @@
     m_own, ea, eb, msk, rim, rimd, wgt, fz, fr, fc, inv = misfit(
         sc, got, svm, msk, rim, rimd, wgt, fz, fr, fc, inv
     )
-    fz, fr, fc, inv, gx = ghosts(sc, *near_rows, msk, rim, rimd, fz, fr, fc, inv)
+    fz, fr, fc, inv, gx = ghosts(sc, *near_rows, relayed, msk, rim, rimd, fz, fr, fc, inv)
     th = (sc, layer_thick, thick_other)
 
     ga, gb = swap(ea, 0), swap(eb, 1)

time: 82.5 us -> 80.1 us (0.971)
  starting transfers between devices: 34 us -> 30.5 us
  waiting for transfers between devices: 16.1 us -> 18.4 us
  Pallas kernels: 31 us -> 29.7 us
    ppermute x6 -> x4, starting transfers between devices: 18.1 us -> 14.4 us  [swap(): return lax.ppermute(x, 'tile', swaps(tiles, kind))]
    ppermute x4 -> x5, waiting for transfers between devices: 13.8 us -> 16.7 us  [swap_layers(): return lax.ppermute(x, 'layer', [(0, 1), (1, 0)])]
    pallas_call x1, Pallas kernels: 3.15 us -> 2.06 us  [last_sweeps(): pl.pallas_call(last_kernel, in_specs=[sm()] * 3 + [vm()] * 11 + [hbm()],...]
    ppermute x6 -> x4, waiting for transfers between devices: 2.25 us -> 1.76 us  [swap(): return lax.ppermute(x, 'tile', swaps(tiles, kind))]
    ppermute x4 -> x5, starting transfers between devices: 4.22 us -> 4.49 us  [swap_layers(): return lax.ppermute(x, 'layer', [(0, 1), (1, 0)])]
  transfers between devices with their start and end apart: 11 -> 10, of which waited for: 2 -> 3; matrix products, arithmetic and copies ran while one was open for 0% -> 0% of each run, Pallas kernels for 25% -> 25%
where the time goes in v5:
time: 80.1 us; the launch traced here: 79.5 us
  starting transfers between devices  30.5 us (38%)
  Pallas kernels  29.7 us (37%)
  waiting for transfers between devices  18.4 us (23%)
  between operations  0.87 us (1%)
    ppermute x5, waiting for transfers between devices, swap_layers(): return lax.ppermute(x, 'layer', [(0, 1), (1, 0)])  16.7 us
    ppermute x4, starting transfers between devices, swap(): return lax.ppermute(x, 'tile', swaps(tiles, kind))  14.4 us
    all_to_all x1, starting transfers between devices, body(): lax.all_to_all(payload, 'tile', split_axis=0, concat_axis=0, tiled=True)  11.7 us
    pallas_call x1, Pallas kernels, coefficients(): pl.pallas_call(coef_kernel, in_specs=[sm()] + [vm()] * 6, out_specs=[hbm(...  8.39 us
    pallas_call x1, Pallas kernels, both_sweeps(): pl.pallas_call(both_kernel, in_specs=[sm()] * 3 + [vm()] * (3 + 7 + N_STA...  5.18 us
    pallas_call x1, Pallas kernels, own_sweeps(): pl.pallas_call(own_kernel, in_specs=[sm()] * 3 + [hbm()] * 2 + [vm()] * 7...  4.89 us
    ppermute x5, starting transfers between devices, swap_layers(): return lax.ppermute(x, 'layer', [(0, 1), (1, 0)])  4.49 us
    pallas_call x1, Pallas kernels, misfit(): pl.pallas_call(misfit_kernel, in_specs=[sm()] + [hbm()] * (2 + len(KEPT))...  4.31 us
  transfers between devices with their start and end apart: 10, of which 3 were waited for; matrix products, arithmetic and copies ran while one was open for 0% of the time, Pallas kernels for 25%

profile of v5, /device:TPU:2, one launch (start us, length us, event | category | flops | bytes accessed | tf_op | source)
XLA Modules:
  0.0 79.5 jit_solution(5594070717879593466)
XLA Ops:
  0.6 3.4 %shard_map.95 = (bf16[64,72,128]{2,1,0:T(8,128)(2,1)}, bf16[4,64,1024]{2,1,0:T(8,128)(2,1)}) custom-call(s32[1]{0:T(128)} %bitcast.sc, bf16[64,128,128]{2,1,0:T(8,128)(2,1)} %bitcast.2, s32[64,64]{1,0:T(8,128)} %target.1, f32[4,64,1024]{2,1,0:T(8,128)} %visc.5), custom_call_target="tpu_custom_call" | custom-call | tf_op jit(solution)/shard_map/pallas_call | solution.py:120
  4.1 0.0 copy-start.5
  4.1 0.0 copy-start
  4.1 0.0 copy-start.1
  4.1 0.0 copy-start.2
  4.1 0.0 copy-start.3
  4.2 0.0 copy-start.4
  4.2 11.7 %all-to-all-start = ((bf16[64,72,128]{2,1,0:T(8,128)(2,1)}), bf16[64,72,128]{2,1,0:T(8,128)(2,1)}, u32[]{:S(2)}, u32[]{:S(2)}) async-start(bf16[64,72,128]{2,1,0:T(8,128)(2,1)} %get-tuple-element.51), calls=%async_computation | async-start | bytes 2359296 | tf_op jit(solution)/shard_map/all_to_all | solution.py:636
  15.8 1.1 %collective-permute-start.3 = (bf16[4,64,1024]{2,1,0:T(8,128)(2,1)}, bf16[4,64,1024]{2,1,0:T(8,128)(2,1)S(1)}, u32[]{:S(2)}, u32[]{:S(2)}) collective-permute-start(bf16[4,64,1024]{2,1,0:T(8,128)(2,1)} %get-tuple-element.56), channel_id=1, source_target_pairs={{0,1},{1,0},{2,3},{3,2},{4,5},{5,4},{6,7},{7,6},{8,9},{9,8},{10,11... | collective-permute-start | bytes 1572872 | tf_op jit(solution)/shard_map/ppermute | solution.py:622
  16.9 1.1 %shard_map.96 = (bf16[16,1024]{1,0:T(8,128)(2,1)S(1)}, bf16[16,1024]{1,0:T(8,128)(2,1)S(1)}) custom-call(s32[1]{0:T(128)} %bitcast.sc, f32[4,64,1024]{2,1,0:T(8,128)} %visc.5, s32[64,1024]{1,0:T(8,128)} %mask.3, f32[64,1024]{1,0:T(8,128)} %fric.3), custom_call_target="tpu_custom_call" | custom-call | tf_op jit(solution)/shard_map/pallas_call | solution.py:165
  18.0 0.1 collective-permute-start
  18.1 7.7 %collective-permute-start.1 = (bf16[16,1024]{1,0:T(8,128)(2,1)S(1)}, bf16[16,1024]{1,0:T(8,128)(2,1)S(1)}, u32[]{:S(2)}, u32[]{:S(2)}) collective-permute-start(bf16[16,1024]{1,0:T(8,128)(2,1)S(1)} %get-tuple-element.53), channel_id=1, source_target_pairs={{2,4},{4,2},{6,8},{8,6},{10,12},{12,10},{14,16},{16,14},{18,20},{2... | collective-permute-start | bytes 98312 | tf_op jit(solution)/shard_map/ppermute | solution.py:632
  25.8 0.1 collective-permute-start.2
  25.9 16.3 %collective-permute-done.3.other = bf16[4,64,1024]{2,1,0:T(8,128)(2,1)S(1)} collective-permute-done((bf16[4,64,1024]{2,1,0:T(8,128)(2,1)}, bf16[4,64,1024]{2,1,0:T(8,128)(2,1)S(1)}, u32[]{:S(2)}, u32[]{:S(2)}) %collective-permute-start.3) | collective-permute-done | bytes 524320 | tf_op jit(solution)/shard_map/ppermute | solution.py:622
  42.2 8.4 %shard_map.97 = (f32[68,64,128]{2,1,0:T(8,128)}, f32[68,64,128]{2,1,0:T(8,128)}, f32[68,64,128]{2,1,0:T(8,128)}, f32[68,64,128]{2,1,0:T(8,128)}, f32[68,64,128]{...) custom-call(s32[1]{0:T(128)} %bitcast.sc, ...), custom_call_target="tpu_custom_call" | custom-call | tf_op jit(solution)/shard_map/pallas_call | solution.py:280
  50.6 0.0 collective-permute-done.2.t2
  50.6 0.0 collective-permute-done.ea
  50.7 0.0 all-to-all-done.got_h
  50.7 4.3 %shard_map.98 = (f32[512,128]{1,0:T(8,128)S(1)}, f32[16,128]{1,0:T(8,128)S(1)}, f32[16,128]{1,0:T(8,128)S(1)}, f32[512,128]{1,0:T(8,128)S(1)}, f32[8,32,128]{2,1...) custom-call(s32[1]{0:T(128)} %bitcast.sc, ...), custom_call_target="tpu_custom_call" | custom-call | tf_op jit(solution)/shard_map/pallas_call | solution.py:389
  55.0 1.1 %collective-permute-start.7 = (f32[512,128]{1,0:T(8,128)S(1)}, f32[512,128]{1,0:T(8,128)S(1)}, u32[]{:S(2)}, u32[]{:S(2)}) collective-permute-start(f32[512,128]{1,0:T(8,128)S(1)} %get-tuple-element.68.m), channel_id=1, source_target_pairs={{0,1},{1,0},{2,3},{3,2},{4,5},{5,4},{6,7},{7,6},{8,9},{9,8},{10,11... | collective-permute-start | bytes 786440 | tf_op jit(solution)/shard_map/ppermute | solution.py:622
  56.1 0.0 collective-permute-start.4
  56.1 6.6 %collective-permute-start.5 = (f32[16,128]{1,0:T(8,128)S(1)}, f32[16,128]{1,0:T(8,128)S(1)}, u32[]{:S(2)}, u32[]{:S(2)}) collective-permute-start(f32[16,128]{1,0:T(8,128)S(1)} %get-tuple-element.67), channel_id=1, source_target_pairs={{2,4},{4,2},{6,8},{8,6},{10,12},{12,10},{14,16},{16,14},{18,20},{2... | collective-permute-start | bytes 24584 | tf_op jit(solution)/shard_map/ppermute | solution.py:632
  62.7 1.1 %collective-permute-start.8 = (bf16[32,1024]{1,0:T(8,128)(2,1)S(1)}, bf16[32,1024]{1,0:T(8,128)(2,1)S(1)}, u32[]{:S(2)}, u32[]{:S(2)}) collective-permute-start(bf16[32,1024]{1,0:T(8,128)(2,1)S(1)} %pad_maximum_fusion), channel_id=1, source_target_pairs={{0,1},{1,0},{2,3},{3,2},{4,5},{5,4},{6,7},{7,6},{8,9},{9,8},{10,11... | collective-permute-start | bytes 196616 | tf_op jit(solution)/shard_map/ppermute | solution.py:622
  63.8 0.0 collective-permute-done.4.ga
  63.8 1.8 %collective-permute-done.5.gb = f32[16,128]{1,0:T(8,128)S(1)} collective-permute-done((f32[16,128]{1,0:T(8,128)S(1)}, f32[16,128]{1,0:T(8,128)S(1)}, u32[]{:S(2)}, u32[]{:S(2)}) %collective-permute-start.5) | collective-permute-done | bytes 8224 | tf_op jit(solution)/shard_map/ppermute | solution.py:632
  65.6 1.1 %collective-permute-start.6 = (f32[32,128]{1,0:T(8,128)S(1)}, f32[32,128]{1,0:T(8,128)S(1)}, u32[]{:S(2)}, u32[]{:S(2)}) collective-permute-start(f32[32,128]{1,0:T(8,128)S(1)} %pad_maximum_fusion.1), channel_id=1, source_target_pairs={{0,1},{1,0},{2,3},{3,2},{4,5},{5,4},{6,7},{7,6},{8,9},{9,8},{10,11... | collective-permute-start | bytes 49160 | tf_op jit(solution)/shard_map/ppermute | solution.py:622
  66.7 0.4 collective-permute-done.8.relayed
  67.1 0.3 shard_map.99
  67.4 4.9 %shard_map.100 = (f32[68,64,128]{2,1,0:T(8,128)S(1)}, f32[68,64,128]{2,1,0:T(8,128)S(1)}, f32[8,520,128]{2,1,0:T(8,128)S(1)}, f32[512,128]{1,0:T(8,128)S(1)}, f3...) custom-call(s32[1]{0:T(128)} %bitcast.sc, f32[4]{0:T(128)S(1)} %copy-done.5, f32[4]{0:T(128)S(1)} %collective-permute-done.2.t2, ...), custom_call_target="tpu_custom_call" | custom-call | tf_op jit(solution)/shard_map/pallas_call | solution.py:530
  72.3 5.2 %shard_map.101 = (f32[68,64,128]{2,1,0:T(8,128)S(1)}, f32[68,64,128]{2,1,0:T(8,128)S(1)}, f32[8,520,128]{2,1,0:T(8,128)S(1)}, f32[512,128]{1,0:T(8,128)S(1)}, f3...) custom-call(s32[1]{0:T(128)} %bitcast.sc, ...), custom_call_target="tpu_custom_call", output_to_operand_aliasing={{0}: (13, {}), {1}: (14, {}), {2}: (15, {}), {3}: (16, {})} | custom-call | tf_op jit(solution)/shard_map/pallas_call | solution.py:554
  77.5 0.0 collective-permute-done.6.g
  77.5 2.1 %shard_map.102 = (f32[68,64,128]{2,1,0:T(8,128)S(1)}, f32[68,64,128]{2,1,0:T(8,128)S(1)}, f32[8,520,128]{2,1,0:T(8,128)S(1)}, f32[512,128]{1,0:T(8,128)S(1)}, f3...) custom-call(s32[1]{0:T(128)} %bitcast.sc, ...), custom_call_target="tpu_custom_call", output_to_operand_aliasing={{0}: (10, {}), {1}: (11, {}), {2}: (12, {}), {3}: (13, {}),... | custom-call | tf_op jit(solution)/shard_map/pallas_call | solution.py:597
  (10 shorter events, 0.0 us)
Async XLA Ops:
  4.1 21.7 %copy-start.5 = (f32[4]{0:T(128)S(1)}, f32[4]{0:T(128)}, u32[]{:S(2)}) copy-start(f32[4]{0:T(128)} %t1.5) | copy-start | bytes 52
  4.1 38.1 %copy-start = (f32[4,64,1024]{2,1,0:T(8,128)S(1)}, f32[4,64,1024]{2,1,0:T(8,128)}, u32[]{:S(2)}) copy-start(f32[4,64,1024]{2,1,0:T(8,128)} %visc.5) | copy-start | bytes 3145732
  4.1 38.1 %copy-start.1 = (f32[64,1024]{1,0:T(8,128)S(1)}, f32[64,1024]{1,0:T(8,128)}, u32[]{:S(2)}) copy-start(f32[64,1024]{1,0:T(8,128)} %fric.3) | copy-start | bytes 786436
  4.1 38.1 %copy-start.2 = (s32[64,1024]{1,0:T(8,128)S(1)}, s32[64,1024]{1,0:T(8,128)}, u32[]{:S(2)}) copy-start(s32[64,1024]{1,0:T(8,128)} %mask.3) | copy-start | bytes 786436
  4.1 38.1 %copy-start.3 = (f32[2,64,1024]{2,1,0:T(8,128)S(1)}, f32[2,64,1024]{2,1,0:T(8,128)}, u32[]{:S(2)}) copy-start(f32[2,64,1024]{2,1,0:T(8,128)} %bvel.1) | copy-start | bytes 1572868
  4.2 38.1 %copy-start.4 = (f32[2,64,1024]{2,1,0:T(8,128)S(1)}, f32[2,64,1024]{2,1,0:T(8,128)}, u32[]{:S(2)}) copy-start(f32[2,64,1024]{2,1,0:T(8,128)} %svel.1) | copy-start | bytes 1572868
  4.2 46.5 %all-to-all-start = ((bf16[64,72,128]{2,1,0:T(8,128)(2,1)}), bf16[64,72,128]{2,1,0:T(8,128)(2,1)}, u32[]{:S(2)}, u32[]{:S(2)}) async-start(bf16[64,72,128]{2,1,0:T(8,128)(2,1)} %get-tuple-element.51), calls=%async_computation | async-start | bytes 2359296 | tf_op jit(solution)/shard_map/all_to_all | solution.py:636
  15.8 26.4 %collective-permute-start.3 = (bf16[4,64,1024]{2,1,0:T(8,128)(2,1)}, bf16[4,64,1024]{2,1,0:T(8,128)(2,1)S(1)}, u32[]{:S(2)}, u32[]{:S(2)}) collective-permute-start(bf16[4,64,1024]{2,1,0:T(8,128)(2,1)} %get-tuple-element.56), channel_id=1, source_target_pairs={{0,1},{1,0},{2,3},{3,2},{4,5},{5,4},{6,7},{7,6},{8,9},{9,8},{10,11... | collective-permute-start | bytes 1572872 | tf_op jit(solution)/shard_map/ppermute | solution.py:622
  18.0 32.6 %collective-permute-start = (bf16[16,1024]{1,0:T(8,128)(2,1)S(1)}, bf16[16,1024]{1,0:T(8,128)(2,1)S(1)}, u32[]{:S(2)}, u32[]{:S(2)}) collective-permute-start(bf16[16,1024]{1,0:T(8,128)(2,1)S(1)} %get-tuple-element.52), channel_id=1, source_target_pairs={{0,2},{2,0},{4,6},{6,4},{8,10},{10,8},{12,14},{14,12},{16,18},{18,... | collective-permute-start | bytes 98312 | tf_op jit(solution)/shard_map/ppermute | solution.py:632
  18.1 32.5 %collective-permute-start.1 = (bf16[16,1024]{1,0:T(8,128)(2,1)S(1)}, bf16[16,1024]{1,0:T(8,128)(2,1)S(1)}, u32[]{:S(2)}, u32[]{:S(2)}) collective-permute-start(bf16[16,1024]{1,0:T(8,128)(2,1)S(1)} %get-tuple-element.53), channel_id=1, source_target_pairs={{2,4},{4,2},{6,8},{8,6},{10,12},{12,10},{14,16},{16,14},{18,20},{2... | collective-permute-start | bytes 98312 | tf_op jit(solution)/shard_map/ppermute | solution.py:632
  25.8 24.8 %collective-permute-start.2 = (f32[4]{0:T(128)S(1)}, f32[4]{0:T(128)S(1)}, u32[]{:S(2)}, u32[]{:S(2)}) collective-permute-start(f32[4]{0:T(128)S(1)} %copy-done.5), channel_id=1, source_target_pairs={{0,1},{1,0},{2,3},{3,2},{4,5},{5,4},{6,7},{7,6},{8,9},{9,8},{10,11... | collective-permute-start | bytes 56 | tf_op jit(solution)/shard_map/ppermute | solution.py:622
  55.0 17.3 %collective-permute-start.7 = (f32[512,128]{1,0:T(8,128)S(1)}, f32[512,128]{1,0:T(8,128)S(1)}, u32[]{:S(2)}, u32[]{:S(2)}) collective-permute-start(f32[512,128]{1,0:T(8,128)S(1)} %get-tuple-element.68.m), channel_id=1, source_target_pairs={{0,1},{1,0},{2,3},{3,2},{4,5},{5,4},{6,7},{7,6},{8,9},{9,8},{10,11... | collective-permute-start | bytes 786440 | tf_op jit(solution)/shard_map/ppermute | solution.py:622
  56.1 7.7 %collective-permute-start.4 = (f32[16,128]{1,0:T(8,128)S(1)}, f32[16,128]{1,0:T(8,128)S(1)}, u32[]{:S(2)}, u32[]{:S(2)}) collective-permute-start(f32[16,128]{1,0:T(8,128)S(1)} %get-tuple-element.66), channel_id=1, source_target_pairs={{0,2},{2,0},{4,6},{6,4},{8,10},{10,8},{12,14},{14,12},{16,18},{18,... | collective-permute-start | bytes 24584 | tf_op jit(solution)/shard_map/ppermute | solution.py:632
  56.1 9.5 %collective-permute-start.5 = (f32[16,128]{1,0:T(8,128)S(1)}, f32[16,128]{1,0:T(8,128)S(1)}, u32[]{:S(2)}, u32[]{:S(2)}) collective-permute-start(f32[16,128]{1,0:T(8,128)S(1)} %get-tuple-element.67), channel_id=1, source_target_pairs={{2,4},{4,2},{6,8},{8,6},{10,12},{12,10},{14,16},{16,14},{18,20},{2... | collective-permute-start | bytes 24584 | tf_op jit(solution)/shard_map/ppermute | solution.py:632
  62.7 4.3 %collective-permute-start.8 = (bf16[32,1024]{1,0:T(8,128)(2,1)S(1)}, bf16[32,1024]{1,0:T(8,128)(2,1)S(1)}, u32[]{:S(2)}, u32[]{:S(2)}) collective-permute-start(bf16[32,1024]{1,0:T(8,128)(2,1)S(1)} %pad_maximum_fusion), channel_id=1, source_target_pairs={{0,1},{1,0},{2,3},{3,2},{4,5},{5,4},{6,7},{7,6},{8,9},{9,8},{10,11... | collective-permute-start | bytes 196616 | tf_op jit(solution)/shard_map/ppermute | solution.py:622
  65.6 11.9 %collective-permute-start.6 = (f32[32,128]{1,0:T(8,128)S(1)}, f32[32,128]{1,0:T(8,128)S(1)}, u32[]{:S(2)}, u32[]{:S(2)}) collective-permute-start(f32[32,128]{1,0:T(8,128)S(1)} %pad_maximum_fusion.1), channel_id=1, source_target_pairs={{0,1},{1,0},{2,3},{3,2},{4,5},{5,4},{6,7},{7,6},{8,9},{9,8},{10,11... | collective-permute-start | bytes 49160 | tf_op jit(solution)/shard_map/ppermute | solution.py:622

commit v6 on v5

--- a/solution.py
+++ b/solution.py
@@ -71,11 +71,38 @@
     return jnp.where(t < 512, (128 + (t & 127)) << (t >> 7), 0)
 
 
-def pack_kernel(sc, slots, target, visc, o, narrow, x, y, t, f, codes, vx, vy, sin, sout, st, vin, vout):
-    own, _ = place(sc)
+def narrow_kernel(visc, narrow, vx, vy, vin, vout):
     layers = visc.shape[0]
     takes = [pltpu.make_async_copy(visc.at[i], vx.at[i], vin.at[i]) for i in range(layers)]
     gives = [pltpu.make_async_copy(vy.at[i], narrow.at[i], vout.at[i]) for i in range(layers)]
+    for i in takes:
+        i.start()
+    for i in range(layers):
+        takes[i].wait()
+        vy[i] = vx[i].astype(BF16)
+        gives[i].start()
+    for i in gives:
+        i.wait()
+
+
+def narrowed(visc):
+    return pl.pallas_call(
+        narrow_kernel,
+        in_specs=[hbm()],
+        out_specs=hbm(),
+        out_shape=pltpu.HBM(visc.shape, BF16),
+        scratch_shapes=[
+            pltpu.VMEM(visc.shape, F32),
+            pltpu.VMEM(visc.shape, BF16),
+            pltpu.SemaphoreType.DMA((visc.shape[0],)),
+            pltpu.SemaphoreType.DMA((visc.shape[0],)),
+        ],
+        compiler_params=pltpu.CompilerParams(vmem_limit_bytes=8 * MIB),
+    )(far(visc))
+
+
+def pack_kernel(sc, slots, target, o, x, y, t, f, codes, sin, sout, st):
+    own, _ = place(sc)
     n = slots.shape[0]
     step = n // CHUNKS
     tin = pltpu.make_async_copy(target, t, st)
@@ -88,12 +115,8 @@
         pltpu.make_async_copy(y.at[pl.ds(i * step, step)], o.at[pl.ds(i * step, step)], sout.at[i])
         for i in range(CHUNKS)
     ]
-    for i in (*takes, *ins):
+    for i in ins:
         i.start()
-    for i in range(layers):
-        takes[i].wait()
-        vy[i] = vx[i].astype(BF16)
-        gives[i].start()
     tin.wait()
     c = code_of(t[...]).astype(F32)
     codes[...] = jnp.concatenate([c, c], axis=1)
@@ -108,36 +131,32 @@
 
         lax.fori_loop(i * step, (i + 1) * step, one, 0, unroll=8)
         outs[i].start()
-    for i in (*gives, *outs):
+    for i in outs:
         i.wait()
 
 
 CHUNKS = 8
 
 
-def pack(sc, slots, target, visc):
+def pack(sc, slots, target):
     n = slots.shape[0]
     return pl.pallas_call(
         pack_kernel,
-        in_specs=[sm(), hbm(), hbm(), hbm()],
-        out_specs=[hbm(), hbm()],
-        out_shape=[pltpu.HBM((n, 72, 128), BF16), pltpu.HBM(visc.shape, BF16)],
+        in_specs=[sm(), hbm(), hbm()],
+        out_specs=hbm(),
+        out_shape=pltpu.HBM((n, 72, 128), BF16),
         scratch_shapes=[
             pltpu.VMEM((n, 128, 128), BF16),
             pltpu.VMEM((n, 72, 128), BF16),
             pltpu.VMEM((n, 64), jnp.int32),
             pltpu.VMEM((n, 128, 128), F32),
             pltpu.VMEM((n, 128), F32),
-            pltpu.VMEM(visc.shape, F32),
-            pltpu.VMEM(visc.shape, BF16),
             pltpu.SemaphoreType.DMA((CHUNKS,)),
             pltpu.SemaphoreType.DMA((CHUNKS,)),
             pltpu.SemaphoreType.DMA,
-            pltpu.SemaphoreType.DMA((visc.shape[0],)),
-            pltpu.SemaphoreType.DMA((visc.shape[0],)),
         ],
         compiler_params=pltpu.CompilerParams(vmem_limit_bytes=16 * MIB),
-    )(sc, far(slots), far(target), far(visc))
+    )(sc, far(slots), far(target))
 
 
 def edge_kernel(sc, visc, mask, fric, to_a, to_b, v, m, d, s, sem):
@@ -216,6 +235,8 @@
 
 GROUPS = ((3, 16), (16, 32), (32, 48), (48, 60), (60, 65))
 INSIDE = pl.ds(3, 62)
+EARLY = pl.ds(3, 13)
+LATER = ((16, 16), (32, 16), (48, 17))
 RIM = (8, 32, 128)
 N_FIELDS = 5
 
@@ -350,7 +371,7 @@
     rest = []
     for i, (x, y) in enumerate(zip(here, kept_)):
         if KEPT[i] == FIELD:
-            x, y = x.at[INSIDE], y.at[INSIDE]
+            x, y = x.at[EARLY], y.at[EARLY]
         rest.append(pltpu.make_async_copy(x, y, sem2.at[i]))
     for c in (*parts, strips, *rest):
         c.start()
@@ -448,7 +469,7 @@
             total = self.thick[l] * y if l == 0 else total + self.thick[l] * y
         self.acc[row(r - 2), :] = self.wgt[row(r - 2), :] * total
 
-    def interior(self, m):
+    def interior(self, m, ready=()):
         for r in (1, EXT - 2):
             self.a1[r] = jnp.zeros((64, 128), F32)
 
@@ -474,7 +495,12 @@
 
         for p in range(1, 6):
             stage(p, True)
-        lax.fori_loop(6, 33, step, 0)
+        at_ = 6
+        for upto, wait in ready:
+            lax.fori_loop(at_, upto, step, 0)
+            wait()
+            at_ = upto
+        lax.fori_loop(at_, 33, step, 0)
         for p in range(33, 36):
             stage(p, True)
 
@@ -510,31 +536,50 @@
 STAGE = (4, ROWS, 1024)
 
 
-def own_kernel(sc, t1, t2, invx_h, wgtx_h, gx, m, *refs):
-    coefs, state, (invx, wgtx, turned, sem) = refs[:5], refs[5:9], refs[9:]
+def own_kernel(sc, t1, t2, fz_h, fr_h, fc_h, inv_h, invx_h, wgtx_h, gx, m, wgt, *refs):
+    fields, state, (invx, wgtx, turned, sem, sem2) = refs[4:8], refs[8:12], refs[12:]
     own, _ = place(sc)
+    groups = []
+    for i, (first, rows) in enumerate(LATER):
+        part = pl.ds(first, rows)
+        pairs = zip((fz_h, fr_h, fc_h, inv_h), fields)
+        groups.append([pltpu.make_async_copy(x.at[part], y.at[part], sem.at[i, j]) for j, (x, y) in enumerate(pairs)])
     copies = (
-        pltpu.make_async_copy(invx_h.at[INSIDE], invx.at[INSIDE], sem.at[0]),
-        pltpu.make_async_copy(wgtx_h, wgtx, sem.at[1]),
+        pltpu.make_async_copy(invx_h.at[INSIDE], invx.at[INSIDE], sem2.at[0]),
+        pltpu.make_async_copy(wgtx_h, wgtx, sem2.at[1]),
     )
-    for c in copies:
+    for c in (*groups[0], *groups[1], *groups[2], *copies):
         c.start()
-    Sweeps(sc, t1, t2, own, coefs, state, turned).interior(m)
+
+    def waiting(group):
+        def wait():
+            for c in group:
+                c.wait()
+
+        return wait
+
+    ready = [(first // 2, waiting(group)) for (first, _), group in zip(LATER, groups)]
+    Sweeps(sc, t1, t2, own, (*fields, wgt), state, turned).interior(m, ready)
     for c in copies:
         c.wait()
     invx[pl.ds(0, 3)] = gx[pl.ds(0, 3)]
     invx[pl.ds(ROWS + 1, 3)] = gx[pl.ds(3, 3)]
 
 
-def own_sweeps(sc, t1, t2, invx, wgtx, gx, m, coefs):
+def own_sweeps(sc, t1, t2, stored, invx, wgtx, gx, m, wgt, fields):
     return pl.pallas_call(
         own_kernel,
-        in_specs=[sm()] * 3 + [hbm()] * 2 + [vm()] * 7,
-        out_specs=[vm()] * 6,
-        out_shape=[kept(*s) for s in (*STATE, FIELD, STRIP)],
-        scratch_shapes=[pltpu.VMEM(TURNED, F32), pltpu.SemaphoreType.DMA((2,))],
+        in_specs=[sm()] * 3 + [hbm()] * 6 + [vm()] * 7,
+        out_specs=[vm()] * 10,
+        out_shape=[kept(*s) for s in (*(FIELD,) * 4, *STATE, FIELD, STRIP)],
+        scratch_shapes=[
+            pltpu.VMEM(TURNED, F32),
+            pltpu.SemaphoreType.DMA((len(LATER), 4)),
+            pltpu.SemaphoreType.DMA((2,)),
+        ],
+        input_output_aliases={12 + i: i for i in range(4)},
         compiler_params=pltpu.CompilerParams(vmem_limit_bytes=24 * MIB),
-    )(sc, t1, t2, far(invx), far(wgtx), *(near(x) for x in (gx, m, *coefs)))
+    )(sc, t1, t2, *(far(x) for x in (*stored, invx, wgtx)), *(near(x) for x in (gx, m, wgt, *fields)))
 
 
 def both_kernel(sc, t1, t2, ga, gb, m, *refs):
@@ -631,8 +676,8 @@
     def swap(x, kind):
         return lax.ppermute(x, "tile", swaps(tiles, kind))
 
-    payload, narrow = pack(sc, obs_slots.reshape(tiles, 128, 128), obs_target, viscosity)
-    other = swap_layers(narrow)
+    other = swap_layers(narrowed(viscosity))
+    payload = pack(sc, obs_slots.reshape(tiles, 128, 128), obs_target)
     got = lax.all_to_all(payload, "tile", split_axis=0, concat_axis=0, tiled=True)
     thick_other = swap_layers(layer_thick)
 
@@ -642,6 +687,7 @@
     fz, fr, fc, inv, invx, wgt, wgtx, svm, msk, rim, rimd = coefficients(
         sc, viscosity, other, friction, ice_mask, base_vel, surf_vel
     )
+    stored = (fz, fr, fc, inv)
     got, near_rows, thick_other = lax.optimization_barrier((got, near_rows, thick_other))
     m_own, ea, eb, msk, rim, rimd, wgt, fz, fr, fc, inv = misfit(
         sc, got, svm, msk, rim, rimd, wgt, fz, fr, fc, inv
@@ -651,7 +697,7 @@
 
     ga, gb = swap(ea, 0), swap(eb, 1)
     m_oth = swap_layers(m_own)
-    *state, invx, wgtx = own_sweeps(*th, invx, wgtx, gx, m_own, (fz, fr, fc, inv, wgt))
+    fz, fr, fc, inv, *state, invx, wgtx = own_sweeps(*th, stored, invx, wgtx, gx, m_own, wgt, (fz, fr, fc, inv))
     g_oth = swap_layers(jnp.concatenate([ga, gb]))
     *both, adj = both_sweeps(*th, ga, gb, m_oth, (fz, fr, fc, inv, wgt), (invx, wgtx), state)
     adjoint, gradient = last_sweeps(*th, g_oth, both[3], (fz, fr, fc, invx, wgtx), both[4:], adj)

time: 80.1 us -> 80.1 us (level)
  Pallas kernels: 29.7 us -> 31.3 us
  waiting for transfers between devices: 18.4 us -> 17.5 us
    pallas_call x2 -> x3, Pallas kernels: 8.33 us -> 10.8 us  [the longest x1 5.96 us: own_sweeps(): pl.pallas_call(own_kernel, in_specs=[sm()] * 3 + [hbm()] * 6 + [vm()] * 7...]
    ppermute x5, waiting for transfers between devices: 16.7 us -> 15 us  [swap_layers(): return lax.ppermute(x, 'layer', [(0, 1), (1, 0)])]
    pallas_call x1, Pallas kernels: 4.31 us -> 3.37 us  [misfit(): pl.pallas_call(misfit_kernel, in_specs=[sm()] + [hbm()] * (2 + len(KEPT))...]
  transfers between devices with their start and end apart: 10 -> 10, of which waited for: 3 -> 2; matrix products, arithmetic and copies ran while one was open for 0% -> 0% of each run, Pallas kernels for 25% -> 29%
where the time goes in v6:
time: 80.1 us; the launch traced here: 79.5 us
  Pallas kernels  31.3 us (39%)
  starting transfers between devices  29.7 us (37%)
  waiting for transfers between devices  17.5 us (22%)
  between operations  0.88 us (1%)
    ppermute x5, waiting for transfers between devices, swap_layers(): return lax.ppermute(x, 'layer', [(0, 1), (1, 0)])  15 us
    ppermute x4, starting transfers between devices, swap(): return lax.ppermute(x, 'tile', swaps(tiles, kind))  13.7 us
    all_to_all x1, starting transfers between devices, body(): lax.all_to_all(payload, 'tile', split_axis=0, concat_axis=0, tiled=True)  11.7 us
    pallas_call x1, Pallas kernels, coefficients(): pl.pallas_call(coef_kernel, in_specs=[sm()] + [vm()] * 6, out_specs=[hbm(...  8.39 us
    pallas_call x1, Pallas kernels, own_sweeps(): pl.pallas_call(own_kernel, in_specs=[sm()] * 3 + [hbm()] * 6 + [vm()] * 7...  5.96 us
    pallas_call x1, Pallas kernels, both_sweeps(): pl.pallas_call(both_kernel, in_specs=[sm()] * 3 + [vm()] * (3 + 7 + N_STA...  5.18 us
    ppermute x5, starting transfers between devices, swap_layers(): return lax.ppermute(x, 'layer', [(0, 1), (1, 0)])  4.39 us
    pallas_call x1, Pallas kernels, misfit(): pl.pallas_call(misfit_kernel, in_specs=[sm()] + [hbm()] * (2 + len(KEPT))...  3.37 us
  transfers between devices with their start and end apart: 10, of which 2 were waited for; matrix products, arithmetic and copies ran while one was open for 0% of the time, Pallas kernels for 29%

profile of v6, /device:TPU:2, one launch (start us, length us, event | category | flops | bytes accessed | tf_op | source)
XLA Modules:
  0.0 79.5 jit_solution(10521590117137584640)
XLA Ops:
  0.6 2.9 %shard_map.95 = bf16[64,72,128]{2,1,0:T(8,128)(2,1)} custom-call(s32[1]{0:T(128)} %bitcast.sc, bf16[64,128,128]{2,1,0:T(8,128)(2,1)} %bitcast.2, s32[64,64]{1,0:T(8,128)} %target.1), custom_call_target="tpu_custom_call" | custom-call | tf_op jit(solution)/shard_map/pallas_call | solution.py:143
  3.6 0.0 copy-start.5
  3.6 0.0 copy-start
  3.6 0.0 copy-start.1
  3.6 0.0 copy-start.2
  3.6 0.0 copy-start.3
  3.6 0.0 copy-start.4
  3.7 11.7 %all-to-all-start = ((bf16[64,72,128]{2,1,0:T(8,128)(2,1)}), bf16[64,72,128]{2,1,0:T(8,128)(2,1)}, u32[]{:S(2)}, u32[]{:S(2)}) async-start(bf16[64,72,128]{2,1,0:T(8,128)(2,1)} %shard_map.95), calls=%async_computation | async-start | bytes 2359296 | tf_op jit(solution)/shard_map/all_to_all | solution.py:681
  15.3 1.9 %shard_map.97 = bf16[4,64,1024]{2,1,0:T(8,128)(2,1)} custom-call(f32[4,64,1024]{2,1,0:T(8,128)} %visc.5), custom_call_target="tpu_custom_call" | custom-call | tf_op jit(solution)/shard_map/pallas_call | solution.py:89
  17.2 1.1 %collective-permute-start.3 = (bf16[4,64,1024]{2,1,0:T(8,128)(2,1)}, bf16[4,64,1024]{2,1,0:T(8,128)(2,1)S(1)}, u32[]{:S(2)}, u32[]{:S(2)}) collective-permute-start(bf16[4,64,1024]{2,1,0:T(8,128)(2,1)} %shard_map.97), channel_id=1, source_target_pairs={{0,1},{1,0},{2,3},{3,2},{4,5},{5,4},{6,7},{7,6},{8,9},{9,8},{10,11... | collective-permute-start | bytes 1572872 | tf_op jit(solution)/shard_map/ppermute | solution.py:667
  18.3 1.1 %shard_map.96 = (bf16[16,1024]{1,0:T(8,128)(2,1)S(1)}, bf16[16,1024]{1,0:T(8,128)(2,1)S(1)}) custom-call(s32[1]{0:T(128)} %bitcast.sc, f32[4,64,1024]{2,1,0:T(8,128)} %visc.5, s32[64,1024]{1,0:T(8,128)} %mask.3, f32[64,1024]{1,0:T(8,128)} %fric.3), custom_call_target="tpu_custom_call" | custom-call | tf_op jit(solution)/shard_map/pallas_call | solution.py:184
  19.5 0.1 collective-permute-start
  19.6 7.7 %collective-permute-start.1 = (bf16[16,1024]{1,0:T(8,128)(2,1)S(1)}, bf16[16,1024]{1,0:T(8,128)(2,1)S(1)}, u32[]{:S(2)}, u32[]{:S(2)}) collective-permute-start(bf16[16,1024]{1,0:T(8,128)(2,1)S(1)} %get-tuple-element.54), channel_id=1, source_target_pairs={{2,4},{4,2},{6,8},{8,6},{10,12},{12,10},{14,16},{16,14},{18,20},{2... | collective-permute-start | bytes 98312 | tf_op jit(solution)/shard_map/ppermute | solution.py:677
  27.3 0.1 collective-permute-start.2
  27.4 15.0 %collective-permute-done.3.other = bf16[4,64,1024]{2,1,0:T(8,128)(2,1)S(1)} collective-permute-done((bf16[4,64,1024]{2,1,0:T(8,128)(2,1)}, bf16[4,64,1024]{2,1,0:T(8,128)(2,1)S(1)}, u32[]{:S(2)}, u32[]{:S(2)}) %collective-permute-start.3) | collective-permute-done | bytes 524320 | tf_op jit(solution)/shard_map/ppermute | solution.py:667
  42.4 8.4 %shard_map.98 = (f32[68,64,128]{2,1,0:T(8,128)}, f32[68,64,128]{2,1,0:T(8,128)}, f32[68,64,128]{2,1,0:T(8,128)}, f32[68,64,128]{2,1,0:T(8,128)}, f32[68,64,128]{...) custom-call(s32[1]{0:T(128)} %bitcast.sc, ...), custom_call_target="tpu_custom_call" | custom-call | tf_op jit(solution)/shard_map/pallas_call | solution.py:301
  50.8 0.0 collective-permute-done.ea
  50.8 0.0 collective-permute-done.1.eb
  50.8 3.4 %shard_map.99 = (f32[512,128]{1,0:T(8,128)S(1)}, f32[16,128]{1,0:T(8,128)S(1)}, f32[16,128]{1,0:T(8,128)S(1)}, f32[512,128]{1,0:T(8,128)S(1)}, f32[8,32,128]{2,1...) custom-call(s32[1]{0:T(128)} %bitcast.sc, ...), custom_call_target="tpu_custom_call" | custom-call | tf_op jit(solution)/shard_map/pallas_call | solution.py:410
  54.2 1.1 %collective-permute-start.7 = (f32[512,128]{1,0:T(8,128)S(1)}, f32[512,128]{1,0:T(8,128)S(1)}, u32[]{:S(2)}, u32[]{:S(2)}) collective-permute-start(f32[512,128]{1,0:T(8,128)S(1)} %get-tuple-element.68.m), channel_id=1, source_target_pairs={{0,1},{1,0},{2,3},{3,2},{4,5},{5,4},{6,7},{7,6},{8,9},{9,8},{10,11... | collective-permute-start | bytes 786440 | tf_op jit(solution)/shard_map/ppermute | solution.py:667
  55.3 0.0 collective-permute-start.4
  55.3 5.9 %collective-permute-start.5 = (f32[16,128]{1,0:T(8,128)S(1)}, f32[16,128]{1,0:T(8,128)S(1)}, u32[]{:S(2)}, u32[]{:S(2)}) collective-permute-start(f32[16,128]{1,0:T(8,128)S(1)} %get-tuple-element.67), channel_id=1, source_target_pairs={{2,4},{4,2},{6,8},{8,6},{10,12},{12,10},{14,16},{16,14},{18,20},{2... | collective-permute-start | bytes 24584 | tf_op jit(solution)/shard_map/ppermute | solution.py:677
  61.3 1.1 %collective-permute-start.8 = (bf16[32,1024]{1,0:T(8,128)(2,1)S(1)}, bf16[32,1024]{1,0:T(8,128)(2,1)S(1)}, u32[]{:S(2)}, u32[]{:S(2)}) collective-permute-start(bf16[32,1024]{1,0:T(8,128)(2,1)S(1)} %pad_maximum_fusion), channel_id=1, source_target_pairs={{0,1},{1,0},{2,3},{3,2},{4,5},{5,4},{6,7},{7,6},{8,9},{9,8},{10,11... | collective-permute-start | bytes 196616 | tf_op jit(solution)/shard_map/ppermute | solution.py:667
  62.4 2.5 %collective-permute-done.5.gb = f32[16,128]{1,0:T(8,128)S(1)} collective-permute-done((f32[16,128]{1,0:T(8,128)S(1)}, f32[16,128]{1,0:T(8,128)S(1)}, u32[]{:S(2)}, u32[]{:S(2)}) %collective-permute-start.5) | collective-permute-done | bytes 8224 | tf_op jit(solution)/shard_map/ppermute | solution.py:677
  64.9 1.0 %collective-permute-start.6 = (f32[32,128]{1,0:T(8,128)S(1)}, f32[32,128]{1,0:T(8,128)S(1)}, u32[]{:S(2)}, u32[]{:S(2)}) collective-permute-start(f32[32,128]{1,0:T(8,128)S(1)} %pad_maximum_fusion.1), channel_id=1, source_target_pairs={{0,1},{1,0},{2,3},{3,2},{4,5},{5,4},{6,7},{7,6},{8,9},{9,8},{10,11... | collective-permute-start | bytes 49160 | tf_op jit(solution)/shard_map/ppermute | solution.py:667
  65.9 0.0 collective-permute-done.8.relayed
  65.9 0.3 shard_map.100
  66.2 6.0 %shard_map.101 = (f32[68,64,128]{2,1,0:T(8,128)S(1)}, f32[68,64,128]{2,1,0:T(8,128)S(1)}, f32[68,64,128]{2,1,0:T(8,128)S(1)}, f32[68,64,128]{2,1,0:T(8,128)S(1)}...) custom-call(s32[1]{0:T(128)} %bitcast.sc, ...), custom_call_target="tpu_custom_call", output_to_operand_aliasing={{0}: (12, {}), {1}: (13, {}), {2}: (14, {}), {3}: (15, {})} | custom-call | tf_op jit(solution)/shard_map/pallas_call | solution.py:570
  72.2 0.0 collective-permute-done.7.m
  72.2 5.2 %shard_map.102 = (f32[68,64,128]{2,1,0:T(8,128)S(1)}, f32[68,64,128]{2,1,0:T(8,128)S(1)}, f32[8,520,128]{2,1,0:T(8,128)S(1)}, f32[512,128]{1,0:T(8,128)S(1)}, f3...) custom-call(s32[1]{0:T(128)} %bitcast.sc, ...), custom_call_target="tpu_custom_call", output_to_operand_aliasing={{0}: (13, {}), {1}: (14, {}), {2}: (15, {}), {3}: (16, {})} | custom-call | tf_op jit(solution)/shard_map/pallas_call | solution.py:599
  77.4 0.0 collective-permute-done.6.g
  77.4 2.1 %shard_map.103 = (f32[68,64,128]{2,1,0:T(8,128)S(1)}, f32[68,64,128]{2,1,0:T(8,128)S(1)}, f32[8,520,128]{2,1,0:T(8,128)S(1)}, f32[512,128]{1,0:T(8,128)S(1)}, f3...) custom-call(s32[1]{0:T(128)} %bitcast.sc, ...), custom_call_target="tpu_custom_call", output_to_operand_aliasing={{0}: (10, {}), {1}: (11, {}), {2}: (12, {}), {3}: (13, {}),... | custom-call | tf_op jit(solution)/shard_map/pallas_call | solution.py:642
  (11 shorter events, 0.0 us)
Async XLA Ops:
  3.6 23.7 %copy-start.5 = (f32[4]{0:T(128)S(1)}, f32[4]{0:T(128)}, u32[]{:S(2)}) copy-start(f32[4]{0:T(128)} %t1.5) | copy-start | bytes 52
  3.6 38.8 %copy-start = (f32[4,64,1024]{2,1,0:T(8,128)S(1)}, f32[4,64,1024]{2,1,0:T(8,128)}, u32[]{:S(2)}) copy-start(f32[4,64,1024]{2,1,0:T(8,128)} %visc.5) | copy-start | bytes 3145732
  3.6 38.8 %copy-start.1 = (f32[64,1024]{1,0:T(8,128)S(1)}, f32[64,1024]{1,0:T(8,128)}, u32[]{:S(2)}) copy-start(f32[64,1024]{1,0:T(8,128)} %fric.3) | copy-start | bytes 786436
  3.6 38.7 %copy-start.2 = (s32[64,1024]{1,0:T(8,128)S(1)}, s32[64,1024]{1,0:T(8,128)}, u32[]{:S(2)}) copy-start(s32[64,1024]{1,0:T(8,128)} %mask.3) | copy-start | bytes 786436
  3.6 38.7 %copy-start.3 = (f32[2,64,1024]{2,1,0:T(8,128)S(1)}, f32[2,64,1024]{2,1,0:T(8,128)}, u32[]{:S(2)}) copy-start(f32[2,64,1024]{2,1,0:T(8,128)} %bvel.1) | copy-start | bytes 1572868
  3.6 38.7 %copy-start.4 = (f32[2,64,1024]{2,1,0:T(8,128)S(1)}, f32[2,64,1024]{2,1,0:T(8,128)}, u32[]{:S(2)}) copy-start(f32[2,64,1024]{2,1,0:T(8,128)} %svel.1) | copy-start | bytes 1572868
  3.7 47.2 %all-to-all-start = ((bf16[64,72,128]{2,1,0:T(8,128)(2,1)}), bf16[64,72,128]{2,1,0:T(8,128)(2,1)}, u32[]{:S(2)}, u32[]{:S(2)}) async-start(bf16[64,72,128]{2,1,0:T(8,128)(2,1)} %shard_map.95), calls=%async_computation | async-start | bytes 2359296 | tf_op jit(solution)/shard_map/all_to_all | solution.py:681
  17.2 25.1 %collective-permute-start.3 = (bf16[4,64,1024]{2,1,0:T(8,128)(2,1)}, bf16[4,64,1024]{2,1,0:T(8,128)(2,1)S(1)}, u32[]{:S(2)}, u32[]{:S(2)}) collective-permute-start(bf16[4,64,1024]{2,1,0:T(8,128)(2,1)} %shard_map.97), channel_id=1, source_target_pairs={{0,1},{1,0},{2,3},{3,2},{4,5},{5,4},{6,7},{7,6},{8,9},{9,8},{10,11... | collective-permute-start | bytes 1572872 | tf_op jit(solution)/shard_map/ppermute | solution.py:667
  19.5 31.3 %collective-permute-start = (bf16[16,1024]{1,0:T(8,128)(2,1)S(1)}, bf16[16,1024]{1,0:T(8,128)(2,1)S(1)}, u32[]{:S(2)}, u32[]{:S(2)}) collective-permute-start(bf16[16,1024]{1,0:T(8,128)(2,1)S(1)} %get-tuple-element.53), channel_id=1, source_target_pairs={{0,2},{2,0},{4,6},{6,4},{8,10},{10,8},{12,14},{14,12},{16,18},{18,... | collective-permute-start | bytes 98312 | tf_op jit(solution)/shard_map/ppermute | solution.py:677
  19.6 31.3 %collective-permute-start.1 = (bf16[16,1024]{1,0:T(8,128)(2,1)S(1)}, bf16[16,1024]{1,0:T(8,128)(2,1)S(1)}, u32[]{:S(2)}, u32[]{:S(2)}) collective-permute-start(bf16[16,1024]{1,0:T(8,128)(2,1)S(1)} %get-tuple-element.54), channel_id=1, source_target_pairs={{2,4},{4,2},{6,8},{8,6},{10,12},{12,10},{14,16},{16,14},{18,20},{2... | collective-permute-start | bytes 98312 | tf_op jit(solution)/shard_map/ppermute | solution.py:677
  27.3 23.5 %collective-permute-start.2 = (f32[4]{0:T(128)S(1)}, f32[4]{0:T(128)S(1)}, u32[]{:S(2)}, u32[]{:S(2)}) collective-permute-start(f32[4]{0:T(128)S(1)} %copy-done.5), channel_id=1, source_target_pairs={{0,1},{1,0},{2,3},{3,2},{4,5},{5,4},{6,7},{7,6},{8,9},{9,8},{10,11... | collective-permute-start | bytes 56 | tf_op jit(solution)/shard_map/ppermute | solution.py:667
  54.2 18.0 %collective-permute-start.7 = (f32[512,128]{1,0:T(8,128)S(1)}, f32[512,128]{1,0:T(8,128)S(1)}, u32[]{:S(2)}, u32[]{:S(2)}) collective-permute-start(f32[512,128]{1,0:T(8,128)S(1)} %get-tuple-element.68.m), channel_id=1, source_target_pairs={{0,1},{1,0},{2,3},{3,2},{4,5},{5,4},{6,7},{7,6},{8,9},{9,8},{10,11... | collective-permute-start | bytes 786440 | tf_op jit(solution)/shard_map/ppermute | solution.py:667
  55.3 7.1 %collective-permute-start.4 = (f32[16,128]{1,0:T(8,128)S(1)}, f32[16,128]{1,0:T(8,128)S(1)}, u32[]{:S(2)}, u32[]{:S(2)}) collective-permute-start(f32[16,128]{1,0:T(8,128)S(1)} %get-tuple-element.66), channel_id=1, source_target_pairs={{0,2},{2,0},{4,6},{6,4},{8,10},{10,8},{12,14},{14,12},{16,18},{18,... | collective-permute-start | bytes 24584 | tf_op jit(solution)/shard_map/ppermute | solution.py:677
  55.3 9.6 %collective-permute-start.5 = (f32[16,128]{1,0:T(8,128)S(1)}, f32[16,128]{1,0:T(8,128)S(1)}, u32[]{:S(2)}, u32[]{:S(2)}) collective-permute-start(f32[16,128]{1,0:T(8,128)S(1)} %get-tuple-element.67), channel_id=1, source_target_pairs={{2,4},{4,2},{6,8},{8,6},{10,12},{12,10},{14,16},{16,14},{18,20},{2... | collective-permute-start | bytes 24584 | tf_op jit(solution)/shard_map/ppermute | solution.py:677
  61.3 4.6 %collective-permute-start.8 = (bf16[32,1024]{1,0:T(8,128)(2,1)S(1)}, bf16[32,1024]{1,0:T(8,128)(2,1)S(1)}, u32[]{:S(2)}, u32[]{:S(2)}) collective-permute-start(bf16[32,1024]{1,0:T(8,128)(2,1)S(1)} %pad_maximum_fusion), channel_id=1, source_target_pairs={{0,1},{1,0},{2,3},{3,2},{4,5},{5,4},{6,7},{7,6},{8,9},{9,8},{10,11... | collective-permute-start | bytes 196616 | tf_op jit(solution)/shard_map/ppermute | solution.py:667
  64.9 12.5 %collective-permute-start.6 = (f32[32,128]{1,0:T(8,128)S(1)}, f32[32,128]{1,0:T(8,128)S(1)}, u32[]{:S(2)}, u32[]{:S(2)}) collective-permute-start(f32[32,128]{1,0:T(8,128)S(1)} %pad_maximum_fusion.1), channel_id=1, source_target_pairs={{0,1},{1,0},{2,3},{3,2},{4,5},{5,4},{6,7},{7,6},{8,9},{9,8},{10,11... | collective-permute-start | bytes 49160 | tf_op jit(solution)/shard_map/ppermute | solution.py:667

commit v7 on v6

--- a/solution.py
+++ b/solution.py
@@ -71,57 +71,49 @@
     return jnp.where(t < 512, (128 + (t & 127)) << (t >> 7), 0)
 
 
-def narrow_kernel(visc, narrow, vx, vy, vin, vout):
+def narrow_kernel(visc, slots, target, narrow, x, t, vx, vy, vin, vout, st):
     layers = visc.shape[0]
     takes = [pltpu.make_async_copy(visc.at[i], vx.at[i], vin.at[i]) for i in range(layers)]
     gives = [pltpu.make_async_copy(vy.at[i], narrow.at[i], vout.at[i]) for i in range(layers)]
-    for i in takes:
+    fetch = [pltpu.make_async_copy(target, t, st.at[0]), pltpu.make_async_copy(slots, x, st.at[1])]
+    for i in (*takes, *fetch):
         i.start()
     for i in range(layers):
         takes[i].wait()
         vy[i] = vx[i].astype(BF16)
         gives[i].start()
-    for i in gives:
+    for i in (*gives, *fetch):
         i.wait()
 
 
-def narrowed(visc):
+def narrowed(visc, slots, target):
     return pl.pallas_call(
         narrow_kernel,
-        in_specs=[hbm()],
-        out_specs=hbm(),
-        out_shape=pltpu.HBM(visc.shape, BF16),
+        in_specs=[hbm()] * 3,
+        out_specs=[hbm(), vm(), vm()],
+        out_shape=[pltpu.HBM(visc.shape, BF16), kept(*slots.shape, dtype=BF16), kept(*target.shape, dtype=jnp.int32)],
         scratch_shapes=[
             pltpu.VMEM(visc.shape, F32),
             pltpu.VMEM(visc.shape, BF16),
             pltpu.SemaphoreType.DMA((visc.shape[0],)),
             pltpu.SemaphoreType.DMA((visc.shape[0],)),
+            pltpu.SemaphoreType.DMA((2,)),
         ],
         compiler_params=pltpu.CompilerParams(vmem_limit_bytes=8 * MIB),
-    )(far(visc))
-
-
-def pack_kernel(sc, slots, target, o, x, y, t, f, codes, sin, sout, st):
+    )(far(visc), far(slots), far(target))
+
+
+def pack_kernel(sc, x, t, o, y, f, codes, sout):
     own, _ = place(sc)
-    n = slots.shape[0]
+    n = x.shape[0]
     step = n // CHUNKS
-    tin = pltpu.make_async_copy(target, t, st)
-    tin.start()
-    ins = [
-        pltpu.make_async_copy(slots.at[pl.ds(i * step, step)], x.at[pl.ds(i * step, step)], sin.at[i])
-        for i in range(CHUNKS)
-    ]
     outs = [
         pltpu.make_async_copy(y.at[pl.ds(i * step, step)], o.at[pl.ds(i * step, step)], sout.at[i])
         for i in range(CHUNKS)
     ]
-    for i in ins:
-        i.start()
-    tin.wait()
     c = code_of(t[...]).astype(F32)
     codes[...] = jnp.concatenate([c, c], axis=1)
     for i in range(CHUNKS):
-        ins[i].wait()
 
         def one(d, carry):
             f[d] = x[d].astype(F32)
@@ -142,21 +134,17 @@
     n = slots.shape[0]
     return pl.pallas_call(
         pack_kernel,
-        in_specs=[sm(), hbm(), hbm()],
+        in_specs=[sm(), vm(), vm()],
         out_specs=hbm(),
         out_shape=pltpu.HBM((n, 72, 128), BF16),
         scratch_shapes=[
-            pltpu.VMEM((n, 128, 128), BF16),
             pltpu.VMEM((n, 72, 128), BF16),
-            pltpu.VMEM((n, 64), jnp.int32),
             pltpu.VMEM((n, 128, 128), F32),
             pltpu.VMEM((n, 128), F32),
             pltpu.SemaphoreType.DMA((CHUNKS,)),
-            pltpu.SemaphoreType.DMA((CHUNKS,)),
-            pltpu.SemaphoreType.DMA,
         ],
         compiler_params=pltpu.CompilerParams(vmem_limit_bytes=16 * MIB),
-    )(sc, far(slots), far(target))
+    )(sc, near(slots), near(target))
 
 
 def edge_kernel(sc, visc, mask, fric, to_a, to_b, v, m, d, s, sem):
@@ -235,8 +223,8 @@
 
 GROUPS = ((3, 16), (16, 32), (32, 48), (48, 60), (60, 65))
 INSIDE = pl.ds(3, 62)
-EARLY = pl.ds(3, 13)
-LATER = ((16, 16), (32, 16), (48, 17))
+EARLY = pl.ds(3, 29)
+LATER = ((32, 16), (48, 17))
 RIM = (8, 32, 128)
 N_FIELDS = 5
 
@@ -548,7 +536,7 @@
         pltpu.make_async_copy(invx_h.at[INSIDE], invx.at[INSIDE], sem2.at[0]),
         pltpu.make_async_copy(wgtx_h, wgtx, sem2.at[1]),
     )
-    for c in (*groups[0], *groups[1], *groups[2], *copies):
+    for c in (*groups[0], *groups[1], *copies):
         c.start()
 
     def waiting(group):
@@ -676,8 +664,9 @@
     def swap(x, kind):
         return lax.ppermute(x, "tile", swaps(tiles, kind))
 
-    other = swap_layers(narrowed(viscosity))
-    payload = pack(sc, obs_slots.reshape(tiles, 128, 128), obs_target)
+    narrow, slots, target = narrowed(viscosity, obs_slots.reshape(tiles, 128, 128), obs_target)
+    other = swap_layers(narrow)
+    payload = pack(sc, slots, target)
     got = lax.all_to_all(payload, "tile", split_axis=0, concat_axis=0, tiled=True)
     thick_other = swap_layers(layer_thick)
 

time: 80.1 us -> 79.7 us (level)
  Pallas kernels: 31.3 us -> 29.2 us
  starting transfers between devices: 29.7 us -> 30.6 us
    ppermute x5, waiting for transfers between devices: 15 us -> 16.7 us  [swap_layers(): return lax.ppermute(x, 'layer', [(0, 1), (1, 0)])]
    pallas_call x2, Pallas kernels: 4.86 us -> 3.5 us  [the longest x1 2.04 us: narrowed(): pl.pallas_call(narrow_kernel, in_specs=[hbm()] * 3, out_specs=[hbm(), vm(...]
    pallas_call x1, Pallas kernels: 5.96 us -> 4.98 us  [own_sweeps(): pl.pallas_call(own_kernel, in_specs=[sm()] * 3 + [hbm()] * 6 + [vm()] * 7...]
    ppermute x4, waiting for transfers between devices: 2.52 us -> 1.62 us  [swap(): return lax.ppermute(x, 'tile', swaps(tiles, kind))]
  transfers between devices with their start and end apart: 10 -> 10, of which waited for: 2 -> 3; matrix products, arithmetic and copies ran while one was open for 0% -> 0% of each run, Pallas kernels for 29% -> 25%
where the time goes in v7:
time: 79.7 us; the launch traced here: 79.1 us
  starting transfers between devices  30.6 us (38%)
  Pallas kernels  29.2 us (37%)
  waiting for transfers between devices  18.3 us (23%)
  between operations  0.89 us (1%)
    ppermute x5, waiting for transfers between devices, swap_layers(): return lax.ppermute(x, 'layer', [(0, 1), (1, 0)])  16.7 us
    ppermute x4, starting transfers between devices, swap(): return lax.ppermute(x, 'tile', swaps(tiles, kind))  14.5 us
    all_to_all x1, starting transfers between devices, body(): lax.all_to_all(payload, 'tile', split_axis=0, concat_axis=0, tiled=True)  11.7 us
    pallas_call x1, Pallas kernels, coefficients(): pl.pallas_call(coef_kernel, in_specs=[sm()] + [vm()] * 6, out_specs=[hbm(...  8.38 us
    pallas_call x1, Pallas kernels, both_sweeps(): pl.pallas_call(both_kernel, in_specs=[sm()] * 3 + [vm()] * (3 + 7 + N_STA...  5.18 us
    pallas_call x1, Pallas kernels, own_sweeps(): pl.pallas_call(own_kernel, in_specs=[sm()] * 3 + [hbm()] * 6 + [vm()] * 7...  4.98 us
    ppermute x5, starting transfers between devices, swap_layers(): return lax.ppermute(x, 'layer', [(0, 1), (1, 0)])  4.49 us
    pallas_call x1, Pallas kernels, misfit(): pl.pallas_call(misfit_kernel, in_specs=[sm()] + [hbm()] * (2 + len(KEPT))...  3.68 us
  transfers between devices with their start and end apart: 10, of which 3 were waited for; matrix products, arithmetic and copies ran while one was open for 0% of the time, Pallas kernels for 25%

profile of v7, /device:TPU:2, one launch (start us, length us, event | category | flops | bytes accessed | tf_op | source)
XLA Modules:
  0.0 79.1 jit_solution(6248827985771177179)
XLA Ops:
  0.6 2.0 %shard_map.95 = (bf16[4,64,1024]{2,1,0:T(8,128)(2,1)}, bf16[64,128,128]{2,1,0:T(8,128)(2,1)S(1)}, s32[64,64]{1,0:T(8,128)S(1)}) custom-call(f32[4,64,1024]{2,1,0:T(8,128)} %visc.5, bf16[64,128,128]{2,1,0:T(8,128)(2,1)} %bitcast.2, s32[64,64]{1,0:T(8,128)} %target.1), custom_call_target="tpu_custom_call" | custom-call | tf_op jit(solution)/shard_map/pallas_call | solution.py:90
  2.7 1.5 %shard_map.96 = bf16[64,72,128]{2,1,0:T(8,128)(2,1)} custom-call(s32[1]{0:T(128)} %bitcast.sc, bf16[64,128,128]{2,1,0:T(8,128)(2,1)S(1)} %get-tuple-element.56.x, s32[64,64]{1,0:T(8,128)S(1)} %get-tuple-element.57.t), custom_call_target="tpu_custom_call" | custom-call | tf_op jit(solution)/shard_map/pallas_call | solution.py:135
  4.2 0.0 copy-start.5
  4.2 0.0 copy-start
  4.2 0.0 copy-start.1
  4.2 0.0 copy-start.2
  4.2 0.0 copy-start.3
  4.2 0.0 copy-start.4
  4.2 11.7 %all-to-all-start = ((bf16[64,72,128]{2,1,0:T(8,128)(2,1)}), bf16[64,72,128]{2,1,0:T(8,128)(2,1)}, u32[]{:S(2)}, u32[]{:S(2)}) async-start(bf16[64,72,128]{2,1,0:T(8,128)(2,1)} %shard_map.96), calls=%async_computation | async-start | bytes 2359296 | tf_op jit(solution)/shard_map/all_to_all | solution.py:670
  15.9 1.1 %collective-permute-start.3 = (bf16[4,64,1024]{2,1,0:T(8,128)(2,1)S(1)}, bf16[4,64,1024]{2,1,0:T(8,128)(2,1)S(1)}, u32[]{:S(2)}, u32[]{:S(2)}) collective-permute-start(bf16[4,64,1024]{2,1,0:T(8,128)(2,1)S(1)} %copy-done.6), channel_id=1, source_target_pairs={{0,1},{1,0},{2,3},{3,2},{4,5},{5,4},{6,7},{7,6},{8,9},{9,8},{10,11... | collective-permute-start | bytes 1572872 | tf_op jit(solution)/shard_map/ppermute | solution.py:655
  17.0 1.1 %shard_map.97 = (bf16[16,1024]{1,0:T(8,128)(2,1)S(1)}, bf16[16,1024]{1,0:T(8,128)(2,1)S(1)}) custom-call(s32[1]{0:T(128)} %bitcast.sc, f32[4,64,1024]{2,1,0:T(8,128)} %visc.5, s32[64,1024]{1,0:T(8,128)} %mask.3, f32[64,1024]{1,0:T(8,128)} %fric.3), custom_call_target="tpu_custom_call" | custom-call | tf_op jit(solution)/shard_map/pallas_call | solution.py:172
  18.1 0.1 collective-permute-start
  18.2 7.7 %collective-permute-start.1 = (bf16[16,1024]{1,0:T(8,128)(2,1)S(1)}, bf16[16,1024]{1,0:T(8,128)(2,1)S(1)}, u32[]{:S(2)}, u32[]{:S(2)}) collective-permute-start(bf16[16,1024]{1,0:T(8,128)(2,1)S(1)} %get-tuple-element.59), channel_id=1, source_target_pairs={{2,4},{4,2},{6,8},{8,6},{10,12},{12,10},{14,16},{16,14},{18,20},{2... | collective-permute-start | bytes 98312 | tf_op jit(solution)/shard_map/ppermute | solution.py:665
  25.9 0.1 collective-permute-start.2
  26.0 16.1 %collective-permute-done.3.other = bf16[4,64,1024]{2,1,0:T(8,128)(2,1)S(1)} collective-permute-done((bf16[4,64,1024]{2,1,0:T(8,128)(2,1)S(1)}, bf16[4,64,1024]{2,1,0:T(8,128)(2,1)S(1)}, u32[]{:S(2)}, u32[]{:S(2)}) %collective-permute-start.3) | collective-permute-done | bytes 524320 | tf_op jit(solution)/shard_map/ppermute | solution.py:655
  42.2 8.4 %shard_map.98 = (f32[68,64,128]{2,1,0:T(8,128)}, f32[68,64,128]{2,1,0:T(8,128)}, f32[68,64,128]{2,1,0:T(8,128)}, f32[68,64,128]{2,1,0:T(8,128)}, f32[68,64,128]{...) custom-call(s32[1]{0:T(128)} %bitcast.sc, ...), custom_call_target="tpu_custom_call" | custom-call | tf_op jit(solution)/shard_map/pallas_call | solution.py:289
  50.6 0.0 collective-permute-done.2.t2
  50.6 0.0 collective-permute-done.ea
  50.6 0.0 all-to-all-done.got_h
  50.6 3.7 %shard_map.99 = (f32[512,128]{1,0:T(8,128)S(1)}, f32[16,128]{1,0:T(8,128)S(1)}, f32[16,128]{1,0:T(8,128)S(1)}, f32[512,128]{1,0:T(8,128)S(1)}, f32[8,32,128]{2,1...) custom-call(s32[1]{0:T(128)} %bitcast.sc, ...), custom_call_target="tpu_custom_call" | custom-call | tf_op jit(solution)/shard_map/pallas_call | solution.py:398
  54.3 1.1 %collective-permute-start.7 = (f32[512,128]{1,0:T(8,128)S(1)}, f32[512,128]{1,0:T(8,128)S(1)}, u32[]{:S(2)}, u32[]{:S(2)}) collective-permute-start(f32[512,128]{1,0:T(8,128)S(1)} %get-tuple-element.74.m), channel_id=1, source_target_pairs={{0,1},{1,0},{2,3},{3,2},{4,5},{5,4},{6,7},{7,6},{8,9},{9,8},{10,11... | collective-permute-start | bytes 786440 | tf_op jit(solution)/shard_map/ppermute | solution.py:655
  55.4 0.0 collective-permute-start.4
  55.4 6.7 %collective-permute-start.5 = (f32[16,128]{1,0:T(8,128)S(1)}, f32[16,128]{1,0:T(8,128)S(1)}, u32[]{:S(2)}, u32[]{:S(2)}) collective-permute-start(f32[16,128]{1,0:T(8,128)S(1)} %get-tuple-element.73), channel_id=1, source_target_pairs={{2,4},{4,2},{6,8},{8,6},{10,12},{12,10},{14,16},{16,14},{18,20},{2... | collective-permute-start | bytes 24584 | tf_op jit(solution)/shard_map/ppermute | solution.py:665
  62.2 1.1 %collective-permute-start.8 = (bf16[32,1024]{1,0:T(8,128)(2,1)S(1)}, bf16[32,1024]{1,0:T(8,128)(2,1)S(1)}, u32[]{:S(2)}, u32[]{:S(2)}) collective-permute-start(bf16[32,1024]{1,0:T(8,128)(2,1)S(1)} %pad_maximum_fusion), channel_id=1, source_target_pairs={{0,1},{1,0},{2,3},{3,2},{4,5},{5,4},{6,7},{7,6},{8,9},{9,8},{10,11... | collective-permute-start | bytes 196616 | tf_op jit(solution)/shard_map/ppermute | solution.py:655
  63.3 0.0 collective-permute-done.4.ga
  63.3 1.6 %collective-permute-done.5.gb = f32[16,128]{1,0:T(8,128)S(1)} collective-permute-done((f32[16,128]{1,0:T(8,128)S(1)}, f32[16,128]{1,0:T(8,128)S(1)}, u32[]{:S(2)}, u32[]{:S(2)}) %collective-permute-start.5) | collective-permute-done | bytes 8224 | tf_op jit(solution)/shard_map/ppermute | solution.py:665
  64.9 1.1 %collective-permute-start.6 = (f32[32,128]{1,0:T(8,128)S(1)}, f32[32,128]{1,0:T(8,128)S(1)}, u32[]{:S(2)}, u32[]{:S(2)}) collective-permute-start(f32[32,128]{1,0:T(8,128)S(1)} %pad_maximum_fusion.1), channel_id=1, source_target_pairs={{0,1},{1,0},{2,3},{3,2},{4,5},{5,4},{6,7},{7,6},{8,9},{9,8},{10,11... | collective-permute-start | bytes 49160 | tf_op jit(solution)/shard_map/ppermute | solution.py:655
  66.0 0.5 collective-permute-done.8.relayed
  66.5 0.3 shard_map.100
  66.8 5.0 %shard_map.101 = (f32[68,64,128]{2,1,0:T(8,128)S(1)}, f32[68,64,128]{2,1,0:T(8,128)S(1)}, f32[68,64,128]{2,1,0:T(8,128)S(1)}, f32[68,64,128]{2,1,0:T(8,128)S(1)}...) custom-call(s32[1]{0:T(128)} %bitcast.sc, ...), custom_call_target="tpu_custom_call", output_to_operand_aliasing={{0}: (12, {}), {1}: (13, {}), {2}: (14, {}), {3}: (15, {})} | custom-call | tf_op jit(solution)/shard_map/pallas_call | solution.py:558
  71.8 5.2 %shard_map.102 = (f32[68,64,128]{2,1,0:T(8,128)S(1)}, f32[68,64,128]{2,1,0:T(8,128)S(1)}, f32[8,520,128]{2,1,0:T(8,128)S(1)}, f32[512,128]{1,0:T(8,128)S(1)}, f3...) custom-call(s32[1]{0:T(128)} %bitcast.sc, ...), custom_call_target="tpu_custom_call", output_to_operand_aliasing={{0}: (13, {}), {1}: (14, {}), {2}: (15, {}), {3}: (16, {})} | custom-call | tf_op jit(solution)/shard_map/pallas_call | solution.py:587
  77.0 2.1 %shard_map.103 = (f32[68,64,128]{2,1,0:T(8,128)S(1)}, f32[68,64,128]{2,1,0:T(8,128)S(1)}, f32[8,520,128]{2,1,0:T(8,128)S(1)}, f32[512,128]{1,0:T(8,128)S(1)}, f3...) custom-call(s32[1]{0:T(128)} %bitcast.sc, ...), custom_call_target="tpu_custom_call", output_to_operand_aliasing={{0}: (10, {}), {1}: (11, {}), {2}: (12, {}), {3}: (13, {}),... | custom-call | tf_op jit(solution)/shard_map/pallas_call | solution.py:630
  (13 shorter events, 0.0 us)
Async XLA Ops:
  2.7 13.2 %copy-start.6 = (bf16[4,64,1024]{2,1,0:T(8,128)(2,1)S(1)}, bf16[4,64,1024]{2,1,0:T(8,128)(2,1)}, u32[]{:S(2)}) copy-start(bf16[4,64,1024]{2,1,0:T(8,128)(2,1)} %get-tuple-element.62) | copy-start | bytes 1572868
  4.2 21.7 %copy-start.5 = (f32[4]{0:T(128)S(1)}, f32[4]{0:T(128)}, u32[]{:S(2)}) copy-start(f32[4]{0:T(128)} %t1.5) | copy-start | bytes 52
  4.2 38.0 %copy-start = (f32[4,64,1024]{2,1,0:T(8,128)S(1)}, f32[4,64,1024]{2,1,0:T(8,128)}, u32[]{:S(2)}) copy-start(f32[4,64,1024]{2,1,0:T(8,128)} %visc.5) | copy-start | bytes 3145732
  4.2 38.0 %copy-start.1 = (f32[64,1024]{1,0:T(8,128)S(1)}, f32[64,1024]{1,0:T(8,128)}, u32[]{:S(2)}) copy-start(f32[64,1024]{1,0:T(8,128)} %fric.3) | copy-start | bytes 786436
  4.2 37.9 %copy-start.2 = (s32[64,1024]{1,0:T(8,128)S(1)}, s32[64,1024]{1,0:T(8,128)}, u32[]{:S(2)}) copy-start(s32[64,1024]{1,0:T(8,128)} %mask.3) | copy-start | bytes 786436
  4.2 37.9 %copy-start.3 = (f32[2,64,1024]{2,1,0:T(8,128)S(1)}, f32[2,64,1024]{2,1,0:T(8,128)}, u32[]{:S(2)}) copy-start(f32[2,64,1024]{2,1,0:T(8,128)} %bvel.1) | copy-start | bytes 1572868
  4.2 37.9 %copy-start.4 = (f32[2,64,1024]{2,1,0:T(8,128)S(1)}, f32[2,64,1024]{2,1,0:T(8,128)}, u32[]{:S(2)}) copy-start(f32[2,64,1024]{2,1,0:T(8,128)} %svel.1) | copy-start | bytes 1572868
  4.2 46.4 %all-to-all-start = ((bf16[64,72,128]{2,1,0:T(8,128)(2,1)}), bf16[64,72,128]{2,1,0:T(8,128)(2,1)}, u32[]{:S(2)}, u32[]{:S(2)}) async-start(bf16[64,72,128]{2,1,0:T(8,128)(2,1)} %shard_map.96), calls=%async_computation | async-start | bytes 2359296 | tf_op jit(solution)/shard_map/all_to_all | solution.py:670
  15.9 26.2 %collective-permute-start.3 = (bf16[4,64,1024]{2,1,0:T(8,128)(2,1)S(1)}, bf16[4,64,1024]{2,1,0:T(8,128)(2,1)S(1)}, u32[]{:S(2)}, u32[]{:S(2)}) collective-permute-start(bf16[4,64,1024]{2,1,0:T(8,128)(2,1)S(1)} %copy-done.6), channel_id=1, source_target_pairs={{0,1},{1,0},{2,3},{3,2},{4,5},{5,4},{6,7},{7,6},{8,9},{9,8},{10,11... | collective-permute-start | bytes 1572872 | tf_op jit(solution)/shard_map/ppermute | solution.py:655
  18.1 32.4 %collective-permute-start = (bf16[16,1024]{1,0:T(8,128)(2,1)S(1)}, bf16[16,1024]{1,0:T(8,128)(2,1)S(1)}, u32[]{:S(2)}, u32[]{:S(2)}) collective-permute-start(bf16[16,1024]{1,0:T(8,128)(2,1)S(1)} %get-tuple-element.58), channel_id=1, source_target_pairs={{0,2},{2,0},{4,6},{6,4},{8,10},{10,8},{12,14},{14,12},{16,18},{18,... | collective-permute-start | bytes 98312 | tf_op jit(solution)/shard_map/ppermute | solution.py:665
  18.2 32.4 %collective-permute-start.1 = (bf16[16,1024]{1,0:T(8,128)(2,1)S(1)}, bf16[16,1024]{1,0:T(8,128)(2,1)S(1)}, u32[]{:S(2)}, u32[]{:S(2)}) collective-permute-start(bf16[16,1024]{1,0:T(8,128)(2,1)S(1)} %get-tuple-element.59), channel_id=1, source_target_pairs={{2,4},{4,2},{6,8},{8,6},{10,12},{12,10},{14,16},{16,14},{18,20},{2... | collective-permute-start | bytes 98312 | tf_op jit(solution)/shard_map/ppermute | solution.py:665
  25.9 24.6 %collective-permute-start.2 = (f32[4]{0:T(128)S(1)}, f32[4]{0:T(128)S(1)}, u32[]{:S(2)}, u32[]{:S(2)}) collective-permute-start(f32[4]{0:T(128)S(1)} %copy-done.5), channel_id=1, source_target_pairs={{0,1},{1,0},{2,3},{3,2},{4,5},{5,4},{6,7},{7,6},{8,9},{9,8},{10,11... | collective-permute-start | bytes 56 | tf_op jit(solution)/shard_map/ppermute | solution.py:655
  54.3 17.5 %collective-permute-start.7 = (f32[512,128]{1,0:T(8,128)S(1)}, f32[512,128]{1,0:T(8,128)S(1)}, u32[]{:S(2)}, u32[]{:S(2)}) collective-permute-start(f32[512,128]{1,0:T(8,128)S(1)} %get-tuple-element.74.m), channel_id=1, source_target_pairs={{0,1},{1,0},{2,3},{3,2},{4,5},{5,4},{6,7},{7,6},{8,9},{9,8},{10,11... | collective-permute-start | bytes 786440 | tf_op jit(solution)/shard_map/ppermute | solution.py:655
  55.4 7.9 %collective-permute-start.4 = (f32[16,128]{1,0:T(8,128)S(1)}, f32[16,128]{1,0:T(8,128)S(1)}, u32[]{:S(2)}, u32[]{:S(2)}) collective-permute-start(f32[16,128]{1,0:T(8,128)S(1)} %get-tuple-element.72), channel_id=1, source_target_pairs={{0,2},{2,0},{4,6},{6,4},{8,10},{10,8},{12,14},{14,12},{16,18},{18,... | collective-permute-start | bytes 24584 | tf_op jit(solution)/shard_map/ppermute | solution.py:665
  55.4 9.5 %collective-permute-start.5 = (f32[16,128]{1,0:T(8,128)S(1)}, f32[16,128]{1,0:T(8,128)S(1)}, u32[]{:S(2)}, u32[]{:S(2)}) collective-permute-start(f32[16,128]{1,0:T(8,128)S(1)} %get-tuple-element.73), channel_id=1, source_target_pairs={{2,4},{4,2},{6,8},{8,6},{10,12},{12,10},{14,16},{16,14},{18,20},{2... | collective-permute-start | bytes 24584 | tf_op jit(solution)/shard_map/ppermute | solution.py:665
  62.2 4.3 %collective-permute-start.8 = (bf16[32,1024]{1,0:T(8,128)(2,1)S(1)}, bf16[32,1024]{1,0:T(8,128)(2,1)S(1)}, u32[]{:S(2)}, u32[]{:S(2)}) collective-permute-start(bf16[32,1024]{1,0:T(8,128)(2,1)S(1)} %pad_maximum_fusion), channel_id=1, source_target_pairs={{0,1},{1,0},{2,3},{3,2},{4,5},{5,4},{6,7},{7,6},{8,9},{9,8},{10,11... | collective-permute-start | bytes 196616 | tf_op jit(solution)/shard_map/ppermute | solution.py:655
  64.9 12.1 %collective-permute-start.6 = (f32[32,128]{1,0:T(8,128)S(1)}, f32[32,128]{1,0:T(8,128)S(1)}, u32[]{:S(2)}, u32[]{:S(2)}) collective-permute-start(f32[32,128]{1,0:T(8,128)S(1)} %pad_maximum_fusion.1), channel_id=1, source_target_pairs={{0,1},{1,0},{2,3},{3,2},{4,5},{5,4},{6,7},{7,6},{8,9},{9,8},{10,11... | collective-permute-start | bytes 49160 | tf_op jit(solution)/shard_map/ppermute | solution.py:655

commit v8 on v7

--- a/solution.py
+++ b/solution.py
@@ -223,8 +223,8 @@
 
 GROUPS = ((3, 16), (16, 32), (32, 48), (48, 60), (60, 65))
 INSIDE = pl.ds(3, 62)
-EARLY = pl.ds(3, 29)
-LATER = ((32, 16), (48, 17))
+EARLY = pl.ds(3, 45)
+LATER = ((48, 17),)
 RIM = (8, 32, 128)
 N_FIELDS = 5
 
@@ -536,7 +536,7 @@
         pltpu.make_async_copy(invx_h.at[INSIDE], invx.at[INSIDE], sem2.at[0]),
         pltpu.make_async_copy(wgtx_h, wgtx, sem2.at[1]),
     )
-    for c in (*groups[0], *groups[1], *copies):
+    for c in (*(c for group in groups for c in group), *copies):
         c.start()
 
     def waiting(group):

time: 79.7 us -> 79.9 us (level)
  no operation moved by 1% of the time
where the time goes in v8:
time: 79.9 us; the launch traced here: 79.3 us
  starting transfers between devices  30.6 us (38%)
  Pallas kernels  29.5 us (37%)
  waiting for transfers between devices  18.3 us (23%)
  between operations  0.89 us (1%)
    ppermute x5, waiting for transfers between devices, swap_layers(): return lax.ppermute(x, 'layer', [(0, 1), (1, 0)])  16.7 us
    ppermute x4, starting transfers between devices, swap(): return lax.ppermute(x, 'tile', swaps(tiles, kind))  14.5 us
    all_to_all x1, starting transfers between devices, body(): lax.all_to_all(payload, 'tile', split_axis=0, concat_axis=0, tiled=True)  11.7 us
    pallas_call x1, Pallas kernels, coefficients(): pl.pallas_call(coef_kernel, in_specs=[sm()] + [vm()] * 6, out_specs=[hbm(...  8.38 us
    pallas_call x1, Pallas kernels, both_sweeps(): pl.pallas_call(both_kernel, in_specs=[sm()] * 3 + [vm()] * (3 + 7 + N_STA...  5.18 us
    pallas_call x1, Pallas kernels, own_sweeps(): pl.pallas_call(own_kernel, in_specs=[sm()] * 3 + [hbm()] * 6 + [vm()] * 7...  4.94 us
    ppermute x5, starting transfers between devices, swap_layers(): return lax.ppermute(x, 'layer', [(0, 1), (1, 0)])  4.49 us
    pallas_call x1, Pallas kernels, misfit(): pl.pallas_call(misfit_kernel, in_specs=[sm()] + [hbm()] * (2 + len(KEPT))...  3.99 us
  transfers between devices with their start and end apart: 10, of which 3 were waited for; matrix products, arithmetic and copies ran while one was open for 0% of the time, Pallas kernels for 25%

profile of v8, /device:TPU:2, one launch (start us, length us, event | category | flops | bytes accessed | tf_op | source)
XLA Modules:
  0.0 79.3 jit_solution(3211645586582605402)
XLA Ops:
  0.6 2.0 %shard_map.95 = (bf16[4,64,1024]{2,1,0:T(8,128)(2,1)}, bf16[64,128,128]{2,1,0:T(8,128)(2,1)S(1)}, s32[64,64]{1,0:T(8,128)S(1)}) custom-call(f32[4,64,1024]{2,1,0:T(8,128)} %visc.5, bf16[64,128,128]{2,1,0:T(8,128)(2,1)} %bitcast.2, s32[64,64]{1,0:T(8,128)} %target.1), custom_call_target="tpu_custom_call" | custom-call | tf_op jit(solution)/shard_map/pallas_call | solution.py:90
  2.7 1.5 %shard_map.96 = bf16[64,72,128]{2,1,0:T(8,128)(2,1)} custom-call(s32[1]{0:T(128)} %bitcast.sc, bf16[64,128,128]{2,1,0:T(8,128)(2,1)S(1)} %get-tuple-element.56.x, s32[64,64]{1,0:T(8,128)S(1)} %get-tuple-element.57.t), custom_call_target="tpu_custom_call" | custom-call | tf_op jit(solution)/shard_map/pallas_call | solution.py:135
  4.2 0.0 copy-start.5
  4.2 0.0 copy-start
  4.2 0.0 copy-start.1
  4.2 0.0 copy-start.2
  4.2 0.0 copy-start.3
  4.2 0.0 copy-start.4
  4.2 11.7 %all-to-all-start = ((bf16[64,72,128]{2,1,0:T(8,128)(2,1)}), bf16[64,72,128]{2,1,0:T(8,128)(2,1)}, u32[]{:S(2)}, u32[]{:S(2)}) async-start(bf16[64,72,128]{2,1,0:T(8,128)(2,1)} %shard_map.96), calls=%async_computation | async-start | bytes 2359296 | tf_op jit(solution)/shard_map/all_to_all | solution.py:670
  15.9 1.1 %collective-permute-start.3 = (bf16[4,64,1024]{2,1,0:T(8,128)(2,1)S(1)}, bf16[4,64,1024]{2,1,0:T(8,128)(2,1)S(1)}, u32[]{:S(2)}, u32[]{:S(2)}) collective-permute-start(bf16[4,64,1024]{2,1,0:T(8,128)(2,1)S(1)} %copy-done.6), channel_id=1, source_target_pairs={{0,1},{1,0},{2,3},{3,2},{4,5},{5,4},{6,7},{7,6},{8,9},{9,8},{10,11... | collective-permute-start | bytes 1572872 | tf_op jit(solution)/shard_map/ppermute | solution.py:655
  17.0 1.1 %shard_map.97 = (bf16[16,1024]{1,0:T(8,128)(2,1)S(1)}, bf16[16,1024]{1,0:T(8,128)(2,1)S(1)}) custom-call(s32[1]{0:T(128)} %bitcast.sc, f32[4,64,1024]{2,1,0:T(8,128)} %visc.5, s32[64,1024]{1,0:T(8,128)} %mask.3, f32[64,1024]{1,0:T(8,128)} %fric.3), custom_call_target="tpu_custom_call" | custom-call | tf_op jit(solution)/shard_map/pallas_call | solution.py:172
  18.1 0.1 collective-permute-start
  18.2 7.7 %collective-permute-start.1 = (bf16[16,1024]{1,0:T(8,128)(2,1)S(1)}, bf16[16,1024]{1,0:T(8,128)(2,1)S(1)}, u32[]{:S(2)}, u32[]{:S(2)}) collective-permute-start(bf16[16,1024]{1,0:T(8,128)(2,1)S(1)} %get-tuple-element.59), channel_id=1, source_target_pairs={{2,4},{4,2},{6,8},{8,6},{10,12},{12,10},{14,16},{16,14},{18,20},{2... | collective-permute-start | bytes 98312 | tf_op jit(solution)/shard_map/ppermute | solution.py:665
  25.9 0.1 collective-permute-start.2
  26.0 16.1 %collective-permute-done.3.other = bf16[4,64,1024]{2,1,0:T(8,128)(2,1)S(1)} collective-permute-done((bf16[4,64,1024]{2,1,0:T(8,128)(2,1)S(1)}, bf16[4,64,1024]{2,1,0:T(8,128)(2,1)S(1)}, u32[]{:S(2)}, u32[]{:S(2)}) %collective-permute-start.3) | collective-permute-done | bytes 524320 | tf_op jit(solution)/shard_map/ppermute | solution.py:655
  42.2 8.4 %shard_map.98 = (f32[68,64,128]{2,1,0:T(8,128)}, f32[68,64,128]{2,1,0:T(8,128)}, f32[68,64,128]{2,1,0:T(8,128)}, f32[68,64,128]{2,1,0:T(8,128)}, f32[68,64,128]{...) custom-call(s32[1]{0:T(128)} %bitcast.sc, ...), custom_call_target="tpu_custom_call" | custom-call | tf_op jit(solution)/shard_map/pallas_call | solution.py:289
  50.6 0.0 collective-permute-done.2.t2
  50.6 0.0 collective-permute-done.ea
  50.6 0.0 collective-permute-done.1.eb
  50.6 0.0 all-to-all-done.got_h
  50.6 4.0 %shard_map.99 = (f32[512,128]{1,0:T(8,128)S(1)}, f32[16,128]{1,0:T(8,128)S(1)}, f32[16,128]{1,0:T(8,128)S(1)}, f32[512,128]{1,0:T(8,128)S(1)}, f32[8,32,128]{2,1...) custom-call(s32[1]{0:T(128)} %bitcast.sc, ...), custom_call_target="tpu_custom_call" | custom-call | tf_op jit(solution)/shard_map/pallas_call | solution.py:398
  54.6 1.1 %collective-permute-start.7 = (f32[512,128]{1,0:T(8,128)S(1)}, f32[512,128]{1,0:T(8,128)S(1)}, u32[]{:S(2)}, u32[]{:S(2)}) collective-permute-start(f32[512,128]{1,0:T(8,128)S(1)} %get-tuple-element.74.m), channel_id=1, source_target_pairs={{0,1},{1,0},{2,3},{3,2},{4,5},{5,4},{6,7},{7,6},{8,9},{9,8},{10,11... | collective-permute-start | bytes 786440 | tf_op jit(solution)/shard_map/ppermute | solution.py:655
  55.7 0.0 collective-permute-start.4
  55.7 6.7 %collective-permute-start.5 = (f32[16,128]{1,0:T(8,128)S(1)}, f32[16,128]{1,0:T(8,128)S(1)}, u32[]{:S(2)}, u32[]{:S(2)}) collective-permute-start(f32[16,128]{1,0:T(8,128)S(1)} %get-tuple-element.73), channel_id=1, source_target_pairs={{2,4},{4,2},{6,8},{8,6},{10,12},{12,10},{14,16},{16,14},{18,20},{2... | collective-permute-start | bytes 24584 | tf_op jit(solution)/shard_map/ppermute | solution.py:665
  62.5 1.1 %collective-permute-start.8 = (bf16[32,1024]{1,0:T(8,128)(2,1)S(1)}, bf16[32,1024]{1,0:T(8,128)(2,1)S(1)}, u32[]{:S(2)}, u32[]{:S(2)}) collective-permute-start(bf16[32,1024]{1,0:T(8,128)(2,1)S(1)} %pad_maximum_fusion), channel_id=1, source_target_pairs={{0,1},{1,0},{2,3},{3,2},{4,5},{5,4},{6,7},{7,6},{8,9},{9,8},{10,11... | collective-permute-start | bytes 196616 | tf_op jit(solution)/shard_map/ppermute | solution.py:655
  63.6 1.6 %collective-permute-done.5.gb = f32[16,128]{1,0:T(8,128)S(1)} collective-permute-done((f32[16,128]{1,0:T(8,128)S(1)}, f32[16,128]{1,0:T(8,128)S(1)}, u32[]{:S(2)}, u32[]{:S(2)}) %collective-permute-start.5) | collective-permute-done | bytes 8224 | tf_op jit(solution)/shard_map/ppermute | solution.py:665
  65.2 1.1 %collective-permute-start.6 = (f32[32,128]{1,0:T(8,128)S(1)}, f32[32,128]{1,0:T(8,128)S(1)}, u32[]{:S(2)}, u32[]{:S(2)}) collective-permute-start(f32[32,128]{1,0:T(8,128)S(1)} %pad_maximum_fusion.1), channel_id=1, source_target_pairs={{0,1},{1,0},{2,3},{3,2},{4,5},{5,4},{6,7},{7,6},{8,9},{9,8},{10,11... | collective-permute-start | bytes 49160 | tf_op jit(solution)/shard_map/ppermute | solution.py:655
  66.3 0.5 collective-permute-done.8.relayed
  66.8 0.3 shard_map.100
  67.1 4.9 %shard_map.101 = (f32[68,64,128]{2,1,0:T(8,128)S(1)}, f32[68,64,128]{2,1,0:T(8,128)S(1)}, f32[68,64,128]{2,1,0:T(8,128)S(1)}, f32[68,64,128]{2,1,0:T(8,128)S(1)}...) custom-call(s32[1]{0:T(128)} %bitcast.sc, ...), custom_call_target="tpu_custom_call", output_to_operand_aliasing={{0}: (12, {}), {1}: (13, {}), {2}: (14, {}), {3}: (15, {})} | custom-call | tf_op jit(solution)/shard_map/pallas_call | solution.py:558
  72.1 5.2 %shard_map.102 = (f32[68,64,128]{2,1,0:T(8,128)S(1)}, f32[68,64,128]{2,1,0:T(8,128)S(1)}, f32[8,520,128]{2,1,0:T(8,128)S(1)}, f32[512,128]{1,0:T(8,128)S(1)}, f3...) custom-call(s32[1]{0:T(128)} %bitcast.sc, ...), custom_call_target="tpu_custom_call", output_to_operand_aliasing={{0}: (13, {}), {1}: (14, {}), {2}: (15, {}), {3}: (16, {})} | custom-call | tf_op jit(solution)/shard_map/pallas_call | solution.py:587
  77.3 2.1 %shard_map.103 = (f32[68,64,128]{2,1,0:T(8,128)S(1)}, f32[68,64,128]{2,1,0:T(8,128)S(1)}, f32[8,520,128]{2,1,0:T(8,128)S(1)}, f32[512,128]{1,0:T(8,128)S(1)}, f3...) custom-call(s32[1]{0:T(128)} %bitcast.sc, ...), custom_call_target="tpu_custom_call", output_to_operand_aliasing={{0}: (10, {}), {1}: (11, {}), {2}: (12, {}), {3}: (13, {}),... | custom-call | tf_op jit(solution)/shard_map/pallas_call | solution.py:630
  (13 shorter events, 0.0 us)
Async XLA Ops:
  2.7 13.2 %copy-start.6 = (bf16[4,64,1024]{2,1,0:T(8,128)(2,1)S(1)}, bf16[4,64,1024]{2,1,0:T(8,128)(2,1)}, u32[]{:S(2)}) copy-start(bf16[4,64,1024]{2,1,0:T(8,128)(2,1)} %get-tuple-element.62) | copy-start | bytes 1572868
  4.2 21.7 %copy-start.5 = (f32[4]{0:T(128)S(1)}, f32[4]{0:T(128)}, u32[]{:S(2)}) copy-start(f32[4]{0:T(128)} %t1.5) | copy-start | bytes 52
  4.2 38.0 %copy-start = (f32[4,64,1024]{2,1,0:T(8,128)S(1)}, f32[4,64,1024]{2,1,0:T(8,128)}, u32[]{:S(2)}) copy-start(f32[4,64,1024]{2,1,0:T(8,128)} %visc.5) | copy-start | bytes 3145732
  4.2 38.0 %copy-start.1 = (f32[64,1024]{1,0:T(8,128)S(1)}, f32[64,1024]{1,0:T(8,128)}, u32[]{:S(2)}) copy-start(f32[64,1024]{1,0:T(8,128)} %fric.3) | copy-start | bytes 786436
  4.2 37.9 %copy-start.2 = (s32[64,1024]{1,0:T(8,128)S(1)}, s32[64,1024]{1,0:T(8,128)}, u32[]{:S(2)}) copy-start(s32[64,1024]{1,0:T(8,128)} %mask.3) | copy-start | bytes 786436
  4.2 37.9 %copy-start.3 = (f32[2,64,1024]{2,1,0:T(8,128)S(1)}, f32[2,64,1024]{2,1,0:T(8,128)}, u32[]{:S(2)}) copy-start(f32[2,64,1024]{2,1,0:T(8,128)} %bvel.1) | copy-start | bytes 1572868
  4.2 37.9 %copy-start.4 = (f32[2,64,1024]{2,1,0:T(8,128)S(1)}, f32[2,64,1024]{2,1,0:T(8,128)}, u32[]{:S(2)}) copy-start(f32[2,64,1024]{2,1,0:T(8,128)} %svel.1) | copy-start | bytes 1572868
  4.2 46.4 %all-to-all-start = ((bf16[64,72,128]{2,1,0:T(8,128)(2,1)}), bf16[64,72,128]{2,1,0:T(8,128)(2,1)}, u32[]{:S(2)}, u32[]{:S(2)}) async-start(bf16[64,72,128]{2,1,0:T(8,128)(2,1)} %shard_map.96), calls=%async_computation | async-start | bytes 2359296 | tf_op jit(solution)/shard_map/all_to_all | solution.py:670
  15.9 26.2 %collective-permute-start.3 = (bf16[4,64,1024]{2,1,0:T(8,128)(2,1)S(1)}, bf16[4,64,1024]{2,1,0:T(8,128)(2,1)S(1)}, u32[]{:S(2)}, u32[]{:S(2)}) collective-permute-start(bf16[4,64,1024]{2,1,0:T(8,128)(2,1)S(1)} %copy-done.6), channel_id=1, source_target_pairs={{0,1},{1,0},{2,3},{3,2},{4,5},{5,4},{6,7},{7,6},{8,9},{9,8},{10,11... | collective-permute-start | bytes 1572872 | tf_op jit(solution)/shard_map/ppermute | solution.py:655
  18.1 32.4 %collective-permute-start = (bf16[16,1024]{1,0:T(8,128)(2,1)S(1)}, bf16[16,1024]{1,0:T(8,128)(2,1)S(1)}, u32[]{:S(2)}, u32[]{:S(2)}) collective-permute-start(bf16[16,1024]{1,0:T(8,128)(2,1)S(1)} %get-tuple-element.58), channel_id=1, source_target_pairs={{0,2},{2,0},{4,6},{6,4},{8,10},{10,8},{12,14},{14,12},{16,18},{18,... | collective-permute-start | bytes 98312 | tf_op jit(solution)/shard_map/ppermute | solution.py:665
  18.2 32.4 %collective-permute-start.1 = (bf16[16,1024]{1,0:T(8,128)(2,1)S(1)}, bf16[16,1024]{1,0:T(8,128)(2,1)S(1)}, u32[]{:S(2)}, u32[]{:S(2)}) collective-permute-start(bf16[16,1024]{1,0:T(8,128)(2,1)S(1)} %get-tuple-element.59), channel_id=1, source_target_pairs={{2,4},{4,2},{6,8},{8,6},{10,12},{12,10},{14,16},{16,14},{18,20},{2... | collective-permute-start | bytes 98312 | tf_op jit(solution)/shard_map/ppermute | solution.py:665
  25.9 24.6 %collective-permute-start.2 = (f32[4]{0:T(128)S(1)}, f32[4]{0:T(128)S(1)}, u32[]{:S(2)}, u32[]{:S(2)}) collective-permute-start(f32[4]{0:T(128)S(1)} %copy-done.5), channel_id=1, source_target_pairs={{0,1},{1,0},{2,3},{3,2},{4,5},{5,4},{6,7},{7,6},{8,9},{9,8},{10,11... | collective-permute-start | bytes 56 | tf_op jit(solution)/shard_map/ppermute | solution.py:655
  54.6 17.5 %collective-permute-start.7 = (f32[512,128]{1,0:T(8,128)S(1)}, f32[512,128]{1,0:T(8,128)S(1)}, u32[]{:S(2)}, u32[]{:S(2)}) collective-permute-start(f32[512,128]{1,0:T(8,128)S(1)} %get-tuple-element.74.m), channel_id=1, source_target_pairs={{0,1},{1,0},{2,3},{3,2},{4,5},{5,4},{6,7},{7,6},{8,9},{9,8},{10,11... | collective-permute-start | bytes 786440 | tf_op jit(solution)/shard_map/ppermute | solution.py:655
  55.7 7.9 %collective-permute-start.4 = (f32[16,128]{1,0:T(8,128)S(1)}, f32[16,128]{1,0:T(8,128)S(1)}, u32[]{:S(2)}, u32[]{:S(2)}) collective-permute-start(f32[16,128]{1,0:T(8,128)S(1)} %get-tuple-element.72), channel_id=1, source_target_pairs={{0,2},{2,0},{4,6},{6,4},{8,10},{10,8},{12,14},{14,12},{16,18},{18,... | collective-permute-start | bytes 24584 | tf_op jit(solution)/shard_map/ppermute | solution.py:665
  55.7 9.5 %collective-permute-start.5 = (f32[16,128]{1,0:T(8,128)S(1)}, f32[16,128]{1,0:T(8,128)S(1)}, u32[]{:S(2)}, u32[]{:S(2)}) collective-permute-start(f32[16,128]{1,0:T(8,128)S(1)} %get-tuple-element.73), channel_id=1, source_target_pairs={{2,4},{4,2},{6,8},{8,6},{10,12},{12,10},{14,16},{16,14},{18,20},{2... | collective-permute-start | bytes 24584 | tf_op jit(solution)/shard_map/ppermute | solution.py:665
  62.5 4.3 %collective-permute-start.8 = (bf16[32,1024]{1,0:T(8,128)(2,1)S(1)}, bf16[32,1024]{1,0:T(8,128)(2,1)S(1)}, u32[]{:S(2)}, u32[]{:S(2)}) collective-permute-start(bf16[32,1024]{1,0:T(8,128)(2,1)S(1)} %pad_maximum_fusion), channel_id=1, source_target_pairs={{0,1},{1,0},{2,3},{3,2},{4,5},{5,4},{6,7},{7,6},{8,9},{9,8},{10,11... | collective-permute-start | bytes 196616 | tf_op jit(solution)/shard_map/ppermute | solution.py:655
  65.2 12.1 %collective-permute-start.6 = (f32[32,128]{1,0:T(8,128)S(1)}, f32[32,128]{1,0:T(8,128)S(1)}, u32[]{:S(2)}, u32[]{:S(2)}) collective-permute-start(f32[32,128]{1,0:T(8,128)S(1)} %pad_maximum_fusion.1), channel_id=1, source_target_pairs={{0,1},{1,0},{2,3},{3,2},{4,5},{5,4},{6,7},{7,6},{8,9},{9,8},{10,11... | collective-permute-start | bytes 49160 | tf_op jit(solution)/shard_map/ppermute | solution.py:655

commit v9 on v7

--- a/solution.py
+++ b/solution.py
@@ -10,7 +10,7 @@
 BF16 = jnp.bfloat16
 ROWS = 64
 EXT = 68
-FIELD = (EXT, 64, 128)
+FIELD = (EXT, 72, 128)
 STRIP = (ROWS * 8, 128)
 MIB = 1 << 20
 
@@ -336,7 +336,7 @@
         ghost_kernel,
         in_specs=[sm()] + [vm()] * 10,
         out_specs=[vm()] * 5,
-        out_shape=[kept(*FIELD)] * 4 + [kept(6, 64, 128)],
+        out_shape=[kept(*FIELD)] * 4 + [kept(6, 72, 128)],
         scratch_shapes=[pltpu.VMEM((2, 2, 128, 128), F32), pltpu.VMEM((2, 8, 40, 128), F32)],
         input_output_aliases={7: 0, 8: 1, 9: 2, 10: 3},
         compiler_params=pltpu.CompilerParams(vmem_limit_bytes=24 * MIB),
@@ -459,7 +459,7 @@
 
     def interior(self, m, ready=()):
         for r in (1, EXT - 2):
-            self.a1[r] = jnp.zeros((64, 128), F32)
+            self.a1[r] = jnp.zeros(FIELD[1:], F32)
 
         def stage(p, static):
             for k, back in ((1, 4), (1, 3), (0, 2), (0, 1), (None, 0)):

time: 79.7 us -> 80.5 us (1.010)
  transfers between devices with their start and end apart: 10 -> 10, of which waited for: 3 -> 3; matrix products, arithmetic and copies ran while one was open for 0% -> 0% of each run, Pallas kernels for 25% -> 26%
where the time goes in v9:
time: 80.5 us; the launch traced here: 79.9 us
  starting transfers between devices  30.6 us (38%)
  Pallas kernels  30 us (37%)
  waiting for transfers between devices  18.3 us (23%)
  between operations  0.89 us (1%)
    ppermute x5, waiting for transfers between devices, swap_layers(): return lax.ppermute(x, 'layer', [(0, 1), (1, 0)])  16.7 us
    ppermute x4, starting transfers between devices, swap(): return lax.ppermute(x, 'tile', swaps(tiles, kind))  14.5 us
    all_to_all x1, starting transfers between devices, body(): lax.all_to_all(payload, 'tile', split_axis=0, concat_axis=0, tiled=True)  11.7 us
    pallas_call x1, Pallas kernels, coefficients(): pl.pallas_call(coef_kernel, in_specs=[sm()] + [vm()] * 6, out_specs=[hbm(...  8.47 us
    pallas_call x1, Pallas kernels, both_sweeps(): pl.pallas_call(both_kernel, in_specs=[sm()] * 3 + [vm()] * (3 + 7 + N_STA...  5.54 us
    pallas_call x1, Pallas kernels, own_sweeps(): pl.pallas_call(own_kernel, in_specs=[sm()] * 3 + [hbm()] * 6 + [vm()] * 7...  5.29 us
    ppermute x5, starting transfers between devices, swap_layers(): return lax.ppermute(x, 'layer', [(0, 1), (1, 0)])  4.49 us
    pallas_call x1, Pallas kernels, misfit(): pl.pallas_call(misfit_kernel, in_specs=[sm()] + [hbm()] * (2 + len(KEPT))...  3.75 us
  transfers between devices with their start and end apart: 10, of which 3 were waited for; matrix products, arithmetic and copies ran while one was open for 0% of the time, Pallas kernels for 26%

profile of v9, /device:TPU:2, one launch (start us, length us, event | category | flops | bytes accessed | tf_op | source)
XLA Modules:
  0.0 79.9 jit_solution(5626772543099262917)
XLA Ops:
  0.6 2.0 %shard_map.95 = (bf16[4,64,1024]{2,1,0:T(8,128)(2,1)}, bf16[64,128,128]{2,1,0:T(8,128)(2,1)S(1)}, s32[64,64]{1,0:T(8,128)S(1)}) custom-call(f32[4,64,1024]{2,1,0:T(8,128)} %visc.5, bf16[64,128,128]{2,1,0:T(8,128)(2,1)} %bitcast.2, s32[64,64]{1,0:T(8,128)} %target.1), custom_call_target="tpu_custom_call" | custom-call | tf_op jit(solution)/shard_map/pallas_call | solution.py:90
  2.7 1.5 %shard_map.96 = bf16[64,72,128]{2,1,0:T(8,128)(2,1)} custom-call(s32[1]{0:T(128)} %bitcast.sc, bf16[64,128,128]{2,1,0:T(8,128)(2,1)S(1)} %get-tuple-element.56.x, s32[64,64]{1,0:T(8,128)S(1)} %get-tuple-element.57.t), custom_call_target="tpu_custom_call" | custom-call | tf_op jit(solution)/shard_map/pallas_call | solution.py:135
  4.2 0.0 copy-start.5
  4.2 0.0 copy-start
  4.2 0.0 copy-start.1
  4.2 0.0 copy-start.2
  4.2 0.0 copy-start.3
  4.2 0.0 copy-start.4
  4.2 11.7 %all-to-all-start = ((bf16[64,72,128]{2,1,0:T(8,128)(2,1)}), bf16[64,72,128]{2,1,0:T(8,128)(2,1)}, u32[]{:S(2)}, u32[]{:S(2)}) async-start(bf16[64,72,128]{2,1,0:T(8,128)(2,1)} %shard_map.96), calls=%async_computation | async-start | bytes 2359296 | tf_op jit(solution)/shard_map/all_to_all | solution.py:670
  15.9 1.1 %collective-permute-start.3 = (bf16[4,64,1024]{2,1,0:T(8,128)(2,1)S(1)}, bf16[4,64,1024]{2,1,0:T(8,128)(2,1)S(1)}, u32[]{:S(2)}, u32[]{:S(2)}) collective-permute-start(bf16[4,64,1024]{2,1,0:T(8,128)(2,1)S(1)} %copy-done.6), channel_id=1, source_target_pairs={{0,1},{1,0},{2,3},{3,2},{4,5},{5,4},{6,7},{7,6},{8,9},{9,8},{10,11... | collective-permute-start | bytes 1572872 | tf_op jit(solution)/shard_map/ppermute | solution.py:655
  17.0 1.1 %shard_map.97 = (bf16[16,1024]{1,0:T(8,128)(2,1)S(1)}, bf16[16,1024]{1,0:T(8,128)(2,1)S(1)}) custom-call(s32[1]{0:T(128)} %bitcast.sc, f32[4,64,1024]{2,1,0:T(8,128)} %visc.5, s32[64,1024]{1,0:T(8,128)} %mask.3, f32[64,1024]{1,0:T(8,128)} %fric.3), custom_call_target="tpu_custom_call" | custom-call | tf_op jit(solution)/shard_map/pallas_call | solution.py:172
  18.1 0.1 collective-permute-start
  18.2 7.7 %collective-permute-start.1 = (bf16[16,1024]{1,0:T(8,128)(2,1)S(1)}, bf16[16,1024]{1,0:T(8,128)(2,1)S(1)}, u32[]{:S(2)}, u32[]{:S(2)}) collective-permute-start(bf16[16,1024]{1,0:T(8,128)(2,1)S(1)} %get-tuple-element.59), channel_id=1, source_target_pairs={{2,4},{4,2},{6,8},{8,6},{10,12},{12,10},{14,16},{16,14},{18,20},{2... | collective-permute-start | bytes 98312 | tf_op jit(solution)/shard_map/ppermute | solution.py:665
  25.9 0.1 collective-permute-start.2
  26.0 16.1 %collective-permute-done.3.other = bf16[4,64,1024]{2,1,0:T(8,128)(2,1)S(1)} collective-permute-done((bf16[4,64,1024]{2,1,0:T(8,128)(2,1)S(1)}, bf16[4,64,1024]{2,1,0:T(8,128)(2,1)S(1)}, u32[]{:S(2)}, u32[]{:S(2)}) %collective-permute-start.3) | collective-permute-done | bytes 524320 | tf_op jit(solution)/shard_map/ppermute | solution.py:655
  42.2 8.5 %shard_map.98 = (f32[68,72,128]{2,1,0:T(8,128)}, f32[68,72,128]{2,1,0:T(8,128)}, f32[68,72,128]{2,1,0:T(8,128)}, f32[68,72,128]{2,1,0:T(8,128)}, f32[68,72,128]{...) custom-call(s32[1]{0:T(128)} %bitcast.sc, ...), custom_call_target="tpu_custom_call" | custom-call | tf_op jit(solution)/shard_map/pallas_call | solution.py:289
  50.7 0.0 collective-permute-done.2.t2
  50.7 0.0 collective-permute-done.ea
  50.7 0.0 all-to-all-done.got_h
  50.7 3.7 %shard_map.99 = (f32[512,128]{1,0:T(8,128)S(1)}, f32[16,128]{1,0:T(8,128)S(1)}, f32[16,128]{1,0:T(8,128)S(1)}, f32[512,128]{1,0:T(8,128)S(1)}, f32[8,32,128]{2,1...) custom-call(s32[1]{0:T(128)} %bitcast.sc, ...), custom_call_target="tpu_custom_call" | custom-call | tf_op jit(solution)/shard_map/pallas_call | solution.py:398
  54.5 1.1 %collective-permute-start.7 = (f32[512,128]{1,0:T(8,128)S(1)}, f32[512,128]{1,0:T(8,128)S(1)}, u32[]{:S(2)}, u32[]{:S(2)}) collective-permute-start(f32[512,128]{1,0:T(8,128)S(1)} %get-tuple-element.74.m), channel_id=1, source_target_pairs={{0,1},{1,0},{2,3},{3,2},{4,5},{5,4},{6,7},{7,6},{8,9},{9,8},{10,11... | collective-permute-start | bytes 786440 | tf_op jit(solution)/shard_map/ppermute | solution.py:655
  55.6 6.7 %collective-permute-start.5 = (f32[16,128]{1,0:T(8,128)S(1)}, f32[16,128]{1,0:T(8,128)S(1)}, u32[]{:S(2)}, u32[]{:S(2)}) collective-permute-start(f32[16,128]{1,0:T(8,128)S(1)} %get-tuple-element.73), channel_id=1, source_target_pairs={{2,4},{4,2},{6,8},{8,6},{10,12},{12,10},{14,16},{16,14},{18,20},{2... | collective-permute-start | bytes 24584 | tf_op jit(solution)/shard_map/ppermute | solution.py:665
  62.3 1.1 %collective-permute-start.8 = (bf16[32,1024]{1,0:T(8,128)(2,1)S(1)}, bf16[32,1024]{1,0:T(8,128)(2,1)S(1)}, u32[]{:S(2)}, u32[]{:S(2)}) collective-permute-start(bf16[32,1024]{1,0:T(8,128)(2,1)S(1)} %pad_maximum_fusion), channel_id=1, source_target_pairs={{0,1},{1,0},{2,3},{3,2},{4,5},{5,4},{6,7},{7,6},{8,9},{9,8},{10,11... | collective-permute-start | bytes 196616 | tf_op jit(solution)/shard_map/ppermute | solution.py:655
  63.4 0.0 collective-permute-done.4.ga
  63.4 1.6 %collective-permute-done.5.gb = f32[16,128]{1,0:T(8,128)S(1)} collective-permute-done((f32[16,128]{1,0:T(8,128)S(1)}, f32[16,128]{1,0:T(8,128)S(1)}, u32[]{:S(2)}, u32[]{:S(2)}) %collective-permute-start.5) | collective-permute-done | bytes 8224 | tf_op jit(solution)/shard_map/ppermute | solution.py:665
  65.0 1.1 %collective-permute-start.6 = (f32[32,128]{1,0:T(8,128)S(1)}, f32[32,128]{1,0:T(8,128)S(1)}, u32[]{:S(2)}, u32[]{:S(2)}) collective-permute-start(f32[32,128]{1,0:T(8,128)S(1)} %pad_maximum_fusion.1), channel_id=1, source_target_pairs={{0,1},{1,0},{2,3},{3,2},{4,5},{5,4},{6,7},{7,6},{8,9},{9,8},{10,11... | collective-permute-start | bytes 49160 | tf_op jit(solution)/shard_map/ppermute | solution.py:655
  66.1 0.5 collective-permute-done.8.relayed
  66.7 0.3 shard_map.100
  67.0 5.3 %shard_map.101 = (f32[68,72,128]{2,1,0:T(8,128)S(1)}, f32[68,72,128]{2,1,0:T(8,128)S(1)}, f32[68,72,128]{2,1,0:T(8,128)S(1)}, f32[68,72,128]{2,1,0:T(8,128)S(1)}...) custom-call(s32[1]{0:T(128)} %bitcast.sc, ...), custom_call_target="tpu_custom_call", output_to_operand_aliasing={{0}: (12, {}), {1}: (13, {}), {2}: (14, {}), {3}: (15, {})} | custom-call | tf_op jit(solution)/shard_map/pallas_call | solution.py:558
  72.3 5.5 %shard_map.102 = (f32[68,72,128]{2,1,0:T(8,128)S(1)}, f32[68,72,128]{2,1,0:T(8,128)S(1)}, f32[8,520,128]{2,1,0:T(8,128)S(1)}, f32[512,128]{1,0:T(8,128)S(1)}, f3...) custom-call(s32[1]{0:T(128)} %bitcast.sc, ...), custom_call_target="tpu_custom_call", output_to_operand_aliasing={{0}: (13, {}), {1}: (14, {}), {2}: (15, {}), {3}: (16, {})} | custom-call | tf_op jit(solution)/shard_map/pallas_call | solution.py:587
  77.8 0.0 collective-permute-done.6.g
  77.9 2.1 %shard_map.103 = (f32[68,72,128]{2,1,0:T(8,128)S(1)}, f32[68,72,128]{2,1,0:T(8,128)S(1)}, f32[8,520,128]{2,1,0:T(8,128)S(1)}, f32[512,128]{1,0:T(8,128)S(1)}, f3...) custom-call(s32[1]{0:T(128)} %bitcast.sc, ...), custom_call_target="tpu_custom_call", output_to_operand_aliasing={{0}: (10, {}), {1}: (11, {}), {2}: (12, {}), {3}: (13, {}),... | custom-call | tf_op jit(solution)/shard_map/pallas_call | solution.py:630
  (13 shorter events, 0.0 us)
Async XLA Ops:
  2.7 13.2 %copy-start.6 = (bf16[4,64,1024]{2,1,0:T(8,128)(2,1)S(1)}, bf16[4,64,1024]{2,1,0:T(8,128)(2,1)}, u32[]{:S(2)}) copy-start(bf16[4,64,1024]{2,1,0:T(8,128)(2,1)} %get-tuple-element.62) | copy-start | bytes 1572868
  4.2 21.7 %copy-start.5 = (f32[4]{0:T(128)S(1)}, f32[4]{0:T(128)}, u32[]{:S(2)}) copy-start(f32[4]{0:T(128)} %t1.5) | copy-start | bytes 52
  4.2 38.0 %copy-start = (f32[4,64,1024]{2,1,0:T(8,128)S(1)}, f32[4,64,1024]{2,1,0:T(8,128)}, u32[]{:S(2)}) copy-start(f32[4,64,1024]{2,1,0:T(8,128)} %visc.5) | copy-start | bytes 3145732
  4.2 38.0 %copy-start.1 = (f32[64,1024]{1,0:T(8,128)S(1)}, f32[64,1024]{1,0:T(8,128)}, u32[]{:S(2)}) copy-start(f32[64,1024]{1,0:T(8,128)} %fric.3) | copy-start | bytes 786436
  4.2 37.9 %copy-start.2 = (s32[64,1024]{1,0:T(8,128)S(1)}, s32[64,1024]{1,0:T(8,128)}, u32[]{:S(2)}) copy-start(s32[64,1024]{1,0:T(8,128)} %mask.3) | copy-start | bytes 786436
  4.2 37.9 %copy-start.3 = (f32[2,64,1024]{2,1,0:T(8,128)S(1)}, f32[2,64,1024]{2,1,0:T(8,128)}, u32[]{:S(2)}) copy-start(f32[2,64,1024]{2,1,0:T(8,128)} %bvel.1) | copy-start | bytes 1572868
  4.2 37.9 %copy-start.4 = (f32[2,64,1024]{2,1,0:T(8,128)S(1)}, f32[2,64,1024]{2,1,0:T(8,128)}, u32[]{:S(2)}) copy-start(f32[2,64,1024]{2,1,0:T(8,128)} %svel.1) | copy-start | bytes 1572868
  4.2 46.4 %all-to-all-start = ((bf16[64,72,128]{2,1,0:T(8,128)(2,1)}), bf16[64,72,128]{2,1,0:T(8,128)(2,1)}, u32[]{:S(2)}, u32[]{:S(2)}) async-start(bf16[64,72,128]{2,1,0:T(8,128)(2,1)} %shard_map.96), calls=%async_computation | async-start | bytes 2359296 | tf_op jit(solution)/shard_map/all_to_all | solution.py:670
  15.9 26.2 %collective-permute-start.3 = (bf16[4,64,1024]{2,1,0:T(8,128)(2,1)S(1)}, bf16[4,64,1024]{2,1,0:T(8,128)(2,1)S(1)}, u32[]{:S(2)}, u32[]{:S(2)}) collective-permute-start(bf16[4,64,1024]{2,1,0:T(8,128)(2,1)S(1)} %copy-done.6), channel_id=1, source_target_pairs={{0,1},{1,0},{2,3},{3,2},{4,5},{5,4},{6,7},{7,6},{8,9},{9,8},{10,11... | collective-permute-start | bytes 1572872 | tf_op jit(solution)/shard_map/ppermute | solution.py:655
  18.1 32.5 %collective-permute-start = (bf16[16,1024]{1,0:T(8,128)(2,1)S(1)}, bf16[16,1024]{1,0:T(8,128)(2,1)S(1)}, u32[]{:S(2)}, u32[]{:S(2)}) collective-permute-start(bf16[16,1024]{1,0:T(8,128)(2,1)S(1)} %get-tuple-element.58), channel_id=1, source_target_pairs={{0,2},{2,0},{4,6},{6,4},{8,10},{10,8},{12,14},{14,12},{16,18},{18,... | collective-permute-start | bytes 98312 | tf_op jit(solution)/shard_map/ppermute | solution.py:665
  18.2 32.5 %collective-permute-start.1 = (bf16[16,1024]{1,0:T(8,128)(2,1)S(1)}, bf16[16,1024]{1,0:T(8,128)(2,1)S(1)}, u32[]{:S(2)}, u32[]{:S(2)}) collective-permute-start(bf16[16,1024]{1,0:T(8,128)(2,1)S(1)} %get-tuple-element.59), channel_id=1, source_target_pairs={{2,4},{4,2},{6,8},{8,6},{10,12},{12,10},{14,16},{16,14},{18,20},{2... | collective-permute-start | bytes 98312 | tf_op jit(solution)/shard_map/ppermute | solution.py:665
  25.9 24.7 %collective-permute-start.2 = (f32[4]{0:T(128)S(1)}, f32[4]{0:T(128)S(1)}, u32[]{:S(2)}, u32[]{:S(2)}) collective-permute-start(f32[4]{0:T(128)S(1)} %copy-done.5), channel_id=1, source_target_pairs={{0,1},{1,0},{2,3},{3,2},{4,5},{5,4},{6,7},{7,6},{8,9},{9,8},{10,11... | collective-permute-start | bytes 56 | tf_op jit(solution)/shard_map/ppermute | solution.py:655
  54.5 17.8 %collective-permute-start.7 = (f32[512,128]{1,0:T(8,128)S(1)}, f32[512,128]{1,0:T(8,128)S(1)}, u32[]{:S(2)}, u32[]{:S(2)}) collective-permute-start(f32[512,128]{1,0:T(8,128)S(1)} %get-tuple-element.74.m), channel_id=1, source_target_pairs={{0,1},{1,0},{2,3},{3,2},{4,5},{5,4},{6,7},{7,6},{8,9},{9,8},{10,11... | collective-permute-start | bytes 786440 | tf_op jit(solution)/shard_map/ppermute | solution.py:655
  55.6 7.9 %collective-permute-start.4 = (f32[16,128]{1,0:T(8,128)S(1)}, f32[16,128]{1,0:T(8,128)S(1)}, u32[]{:S(2)}, u32[]{:S(2)}) collective-permute-start(f32[16,128]{1,0:T(8,128)S(1)} %get-tuple-element.72), channel_id=1, source_target_pairs={{0,2},{2,0},{4,6},{6,4},{8,10},{10,8},{12,14},{14,12},{16,18},{18,... | collective-permute-start | bytes 24584 | tf_op jit(solution)/shard_map/ppermute | solution.py:665
  55.6 9.5 %collective-permute-start.5 = (f32[16,128]{1,0:T(8,128)S(1)}, f32[16,128]{1,0:T(8,128)S(1)}, u32[]{:S(2)}, u32[]{:S(2)}) collective-permute-start(f32[16,128]{1,0:T(8,128)S(1)} %get-tuple-element.73), channel_id=1, source_target_pairs={{2,4},{4,2},{6,8},{8,6},{10,12},{12,10},{14,16},{16,14},{18,20},{2... | collective-permute-start | bytes 24584 | tf_op jit(solution)/shard_map/ppermute | solution.py:665
  62.3 4.3 %collective-permute-start.8 = (bf16[32,1024]{1,0:T(8,128)(2,1)S(1)}, bf16[32,1024]{1,0:T(8,128)(2,1)S(1)}, u32[]{:S(2)}, u32[]{:S(2)}) collective-permute-start(bf16[32,1024]{1,0:T(8,128)(2,1)S(1)} %pad_maximum_fusion), channel_id=1, source_target_pairs={{0,1},{1,0},{2,3},{3,2},{4,5},{5,4},{6,7},{7,6},{8,9},{9,8},{10,11... | collective-permute-start | bytes 196616 | tf_op jit(solution)/shard_map/ppermute | solution.py:655
  65.0 12.8 %collective-permute-start.6 = (f32[32,128]{1,0:T(8,128)S(1)}, f32[32,128]{1,0:T(8,128)S(1)}, u32[]{:S(2)}, u32[]{:S(2)}) collective-permute-start(f32[32,128]{1,0:T(8,128)S(1)} %pad_maximum_fusion.1), channel_id=1, source_target_pairs={{0,1},{1,0},{2,3},{3,2},{4,5},{5,4},{6,7},{7,6},{8,9},{9,8},{10,11... | collective-permute-start | bytes 49160 | tf_op jit(solution)/shard_map/ppermute | solution.py:655
